TPU v7x, 512 devices: a whole 4x4x16 slice. The times are simulated.
512 devices in a mesh: ctx: 64 (over z, x_lo, core), tp: 8 (over x_hi, y).
Axes of the slice: x: 4 (x_hi: 2, x_lo: 2; x = x_hi * 2 + x_lo), y: 4, z: 16, core: 2. Of those that a mesh axis runs over, the one named last changes fastest.
Arguments:
- query: bfloat16 [8192, 4096], P(('ctx', 'tp')), may hold values from -200 to 200
- keys: bfloat16 [8192, 1024], P(('ctx', 'tp')), may hold values from -20 to 20
- values: bfloat16 [8192, 1024], P(('ctx', 'tp')), may hold values from -6 to 6
- output_gradient: bfloat16 [8192, 4096], P(('ctx', 'tp')), may hold values from -6 to 6
Outputs:
- attn_out: bfloat16 [8192, 4096], P(('ctx', 'tp'))
- grad_query: bfloat16 [8192, 4096], P(('ctx', 'tp'))
- key_gradient: bfloat16 [8192, 1024], P(('ctx', 'tp'))
- value_gradient: bfloat16 [8192, 1024], P(('ctx', 'tp'))
All inputs are finite; a program needn't handle non-finite values.
Results may differ from a plain program's by a relative error of at most 0.025.
Values may be sent and summed in bfloat16 or wider, within the bound.
No kernel may reach another device: no remote copies, remote signals or barrier semaphores. Data moves between devices by JAX's collectives and lax.ppermute only.
A program may use at most 64 MiB of HBM per device.

v0:
```python
import jax
import jax.numpy as jnp
from jax import lax
from jax.sharding import PartitionSpec as P

HEAD_WIDTH = 128
QUERY_GROUP = 4


steps_per_turn = 4


def sent_together(arrays, axis, dim, along):
    both = jnp.concatenate(arrays, axis=along)
    out, at, outs = (lax.all_gather(both, axis, axis=dim, tiled=True), 0, [])
    for a in arrays:
        outs.append(lax.slice_in_dim(out, at, at + a.shape[along], axis=along))
        at += a.shape[along]
    return tuple(outs)


def shifted(block, axis, distance):
    devices = range(lax.axis_size(axis))
    route = [((i - distance) % len(devices), i) for i in devices]
    return lax.ppermute(block, axis, route)


def shards(query, keys, values, output_gradient):
    ctx_count = lax.axis_size("ctx")
    ctx_index = lax.axis_index("ctx")
    queries_in, keys_in, values_in, grads_in = (
        lax.all_to_all(query, "tp", split_axis=1, concat_axis=0, tiled=True),
        lax.all_to_all(keys, "tp", split_axis=1, concat_axis=0, tiled=True),
        lax.all_to_all(values, "tp", split_axis=1, concat_axis=0, tiled=True),
        lax.all_to_all(output_gradient, "tp", split_axis=1, concat_axis=0, tiled=True),
    )
    tok_rows = queries_in.shape[0]
    kv_heads = keys_in.shape[1] // HEAD_WIDTH
    query_row_block = QUERY_GROUP * tok_rows
    score_scale = HEAD_WIDTH ** (-0.5)

    def to_rows(tensor):
        return (
            tensor.reshape(tok_rows, kv_heads, QUERY_GROUP, HEAD_WIDTH)
            .transpose(1, 2, 0, 3)
            .reshape(kv_heads, query_row_block, HEAD_WIDTH)
        )

    def from_rows(tensor):
        return (
            tensor.reshape(kv_heads, QUERY_GROUP, tok_rows, HEAD_WIDTH)
            .transpose(2, 0, 1, 3)
            .reshape(tok_rows, kv_heads * QUERY_GROUP * HEAD_WIDTH)
        )

    def from_keys(tensor):
        return tensor.transpose(1, 0, 2).reshape(tok_rows, kv_heads * HEAD_WIDTH)

    query_local = to_rows(queries_in)
    grad_local = to_rows(grads_in)
    whole_keys, whole_values = sent_together((keys_in, values_in), "ctx", 0, 1)
    key_major = whole_keys.reshape(-1, kv_heads, HEAD_WIDTH).transpose(1, 0, 2)
    value_major = whole_values.reshape(-1, kv_heads, HEAD_WIDTH).transpose(1, 0, 2)
    row_pos = ctx_index * tok_rows + jnp.arange(query_row_block) % tok_rows
    last_query = ctx_index * tok_rows + tok_rows - 1

    def masked_logits(first_key, key_count):
        key_block = lax.dynamic_slice_in_dim(key_major, first_key, key_count, 1)
        logits = score_scale * jnp.einsum(
            "hrd,hcd->hrc", query_local, key_block, preferred_element_type=jnp.float32
        )
        allowed = row_pos[:, None] >= first_key + jnp.arange(key_count, dtype=jnp.int32)[None, :]
        return (jnp.where(allowed[None], logits, -1e30), allowed)

    block_keys = steps_per_turn * tok_rows
    turn_count = ctx_count // steps_per_turn

    def stat_step(block_index, loop_state):
        first_key = block_index * block_keys

        def stat_update(old_state):
            running_max, running_sum = old_state
            logits, allowed = masked_logits(first_key, block_keys)
            new_max = jnp.maximum(running_max, jnp.max(logits, axis=2))
            terms = jnp.where(allowed[None], jnp.exp(logits - new_max[..., None]), 0.0)
            return (new_max, running_sum * jnp.exp(running_max - new_max) + jnp.sum(terms, axis=2))

        return lax.cond(
            first_key <= last_query, stat_update, lambda old_state: old_state, loop_state
        )

    start_max = jnp.full((kv_heads, query_row_block), -1e30, jnp.float32)
    start_sum = jnp.zeros((kv_heads, query_row_block), jnp.float32)
    running_max, running_sum = lax.fori_loop(0, turn_count, stat_step, (start_max, start_sum))
    lse = running_max + jnp.log(running_sum)

    def out_step(block_index, output_sum):
        first_key = block_index * block_keys

        def out_update(old_sum):
            logits, allowed = masked_logits(first_key, block_keys)
            weights = jnp.where(allowed[None], jnp.exp(logits - lse[..., None]), 0.0).astype(
                jnp.bfloat16
            )
            value_block = lax.dynamic_slice_in_dim(value_major, first_key, block_keys, 1)
            return old_sum + jnp.einsum(
                "hrc,hcd->hrd", weights, value_block, preferred_element_type=jnp.float32
            )

        return lax.cond(first_key <= last_query, out_update, lambda old_sum: old_sum, output_sum)

    output_sum = lax.fori_loop(
        0, turn_count, out_step, jnp.zeros((kv_heads, query_row_block, HEAD_WIDTH), jnp.float32)
    )
    attention = output_sum.astype(jnp.bfloat16)
    row_delta = jnp.sum(grad_local.astype(jnp.float32) * attention.astype(jnp.float32), axis=2)

    def gradients(first_key, key_count):
        logits, allowed = masked_logits(first_key, key_count)
        probs = jnp.where(allowed[None], jnp.exp(logits - lse[..., None]), 0.0)
        weights = probs.astype(jnp.bfloat16)
        key_block = lax.dynamic_slice_in_dim(key_major, first_key, key_count, 1)
        value_block = lax.dynamic_slice_in_dim(value_major, first_key, key_count, 1)
        value_part = jnp.einsum(
            "hrc,hrd->hcd", weights, grad_local, preferred_element_type=jnp.float32
        )
        prob_grad = jnp.einsum(
            "hrd,hcd->hrc", grad_local, value_block, preferred_element_type=jnp.float32
        )
        score_grad = (probs * (prob_grad - row_delta[..., None])).astype(jnp.bfloat16)
        query_part = jnp.einsum(
            "hrc,hcd->hrd", score_grad, key_block, preferred_element_type=jnp.float32
        )
        key_part = jnp.einsum(
            "hrc,hrd->hcd", score_grad, query_local, preferred_element_type=jnp.float32
        )
        return (query_part, jnp.stack([key_part, value_part]))

    def guarded(is_live, first_key, key_count):

        def nothing():
            return (
                jnp.zeros((kv_heads, query_row_block, HEAD_WIDTH), jnp.float32),
                jnp.zeros((2, kv_heads, key_count, HEAD_WIDTH), jnp.float32),
            )

        return lax.cond(is_live, lambda: gradients(first_key, key_count), nothing)

    start_query = jnp.zeros((kv_heads, query_row_block, HEAD_WIDTH), jnp.float32)

    def turn(turn_index, loop_state):
        query_sum, key_grads = loop_state
        for inner_step in range(steps_per_turn):
            cycle_step = turn_index * steps_per_turn + inner_step
            block_index = (ctx_index - cycle_step) % ctx_count
            query_part, pair_part = guarded(
                cycle_step <= ctx_index, block_index * tok_rows, tok_rows
            )
            query_sum = query_sum + query_part
            key_grads = shifted(key_grads + pair_part, "ctx", 1)
        return (query_sum, key_grads)

    start_pair = jnp.zeros((2, kv_heads, tok_rows, HEAD_WIDTH), jnp.float32)
    query_sum, key_grads = lax.fori_loop(0, turn_count, turn, (start_query, start_pair))
    grad_query = (score_scale * query_sum).astype(jnp.bfloat16)
    key_gradient = (score_scale * key_grads[0]).astype(jnp.bfloat16)
    value_gradient = key_grads[1].astype(jnp.bfloat16)
    return (
        lax.all_to_all(from_rows(attention), "tp", split_axis=0, concat_axis=1, tiled=True),
        lax.all_to_all(from_rows(grad_query), "tp", split_axis=0, concat_axis=1, tiled=True),
        lax.all_to_all(from_keys(key_gradient), "tp", split_axis=0, concat_axis=1, tiled=True),
        lax.all_to_all(from_keys(value_gradient), "tp", split_axis=0, concat_axis=1, tiled=True),
    )


def solution(mesh):
    placed = (
        P(("ctx", "tp"), None),
        P(("ctx", "tp"), None),
        P(("ctx", "tp"), None),
        P(("ctx", "tp"), None),
    )
    return jax.shard_map(
        shards,
        mesh=mesh,
        in_specs=placed,
        out_specs=(
            P(("ctx", "tp"), None),
            P(("ctx", "tp"), None),
            P(("ctx", "tp"), None),
            P(("ctx", "tp"), None),
        ),
        check_vma=False,
    )
```

profile of v0, /device:TPU:384, one launch (start us, length us, event | category | flops | bytes accessed | tf_op | source)
XLA Modules:
  0.0 839.1 jit_solution(5740200702789504746)
XLA Ops:
  8.5 6.9 all-to-all-start
  16.3 7.0 all-to-all-done
  23.2 10.1 %all_to_all.140 = bf16[16,8,128]{2,0,1:T(8,128)(2,1)S(1)} all-to-all(bf16[16,8,128]{2,0,1:T(8,128)(2,1)S(1)} %copy_bitcast_fusion.6), channel_id=1, replica_groups=mesh['ctx'=64,'tp'=8] {'tp'}, dimensions={1} | all-to-all | bytes 65536 | tf_op jit(solution)/shard_map/all_to_all | solution.py:34
  35.6 3.4 all-to-all-start.2
  40.5 6.5 all-to-all-done.2
  47.0 3.4 all-to-all-start.4
  50.5 7.9 all-to-all-done.4
  58.5 92.4 %all-gather.2.cloned.1.call-done = bf16[8192,256]{1,0:T(8,128)(2,1)} async-done(((bf16[128,256]{1,0:T(8,128)(2,1)}), bf16[8192,256]{1,0:T(8,128)(2,1)}) %all-gather.2.cloned.1.call-update) | async-done | bytes 4194320 | tf_op jit(solution)/shard_map/all_gather | solution.py:15
  150.9 4.5 slice_bitcast_fusion
  155.4 21.0 %while.51 = (s32[]{:T(128)}, f32[1,512]{1,0:T(1,128)S(1)}, f32[1,512]{1,0:T(1,128)S(1)}, s32[]{:T(128)}, bf16[1,8192,128]{2,1,0:T(8,128)(2,1)}, /*index=5*/bf16[...) while((s32[]{:T(128)}, f32[1,512]{1,0:T(1,128)S(1)}, ...), condition=%wide.region_5.6_spmd.clone, body=%wide.region_0.5_spmd.clone.sunk | while | flops 69211136 | bytes 2412849 | solution.py:94
  176.5 23.9 %while.52 = (s32[]{:T(128)}, f32[1,512,128]{2,1,0:T(8,128)S(1)}, s32[]{:T(128)}, bf16[1,8192,128]{2,1,0:T(8,128)(2,1)}, bf16[1,512,128]{2,1,0:T(8,128)(2,1)S(1)}...) while((s32[]{:T(128)}, f32[1,512,128]{2,1,0:T(8,128)S(1)}, ...), condition=%wide.region_9.10_spmd.clone, body=%wide.region_6.9_spmd.clone.sunk | while | flops 135860224 | bytes 943389 | solution.py:112
  200.6 582.1 %while.53 = (s32[]{:T(128)}, f32[1,512,128]{2,1,0:T(8,128)S(1)}, f32[2,1,128,128]{3,2,1,0:T(8,128)S(1)}, s32[]{:T(128)}, bf16[1,8192,128]{2,1,0:T(8,128)(2,1)}, ...) while((s32[]{:T(128)}, f32[1,512,128]{2,1,0:T(8,128)S(1)}, ...), condition=%wide.region_20.21_spmd.clone, body=%wide.region_11.20_spmd.clone.sunk | while | flops 338497600 | bytes 15105511 | solution.py:164
  200.6 3.4 conditional.23
  206.2 3.4 conditional.22
  214.4 3.4 conditional.21
  222.8 3.4 conditional.20
  231.4 6.2 collective-permute-done.3
  242.9 3.4 conditional.22
  251.4 3.4 conditional.21
  259.8 3.4 conditional.20
  268.4 6.2 collective-permute-done.3
  279.9 3.4 conditional.22
  305.4 6.2 collective-permute-done.3
  316.9 3.4 conditional.22
  342.4 6.2 collective-permute-done.3
  353.9 3.4 conditional.22
  379.4 6.2 collective-permute-done.3
  390.9 3.4 conditional.22
  416.4 6.2 collective-permute-done.3
  427.9 3.4 conditional.22
  453.4 6.2 collective-permute-done.3
  464.8 3.4 conditional.22
  490.3 6.2 collective-permute-done.3
  501.8 3.4 conditional.22
  527.3 6.2 collective-permute-done.3
  538.8 3.4 conditional.22
  564.3 6.2 collective-permute-done.3
  575.8 3.4 conditional.22
  601.3 6.2 collective-permute-done.3
  612.8 3.4 conditional.22
  638.3 6.2 collective-permute-done.3
  649.8 6.4 collective-permute-done
  658.3 6.4 collective-permute-done.1
  666.7 6.4 collective-permute-done.2
  675.3 6.2 collective-permute-done.3
  683.6 6.4 collective-permute-done
  692.0 6.4 collective-permute-done.1
  700.4 6.4 collective-permute-done.2
  709.0 6.2 collective-permute-done.3
  717.3 6.4 collective-permute-done
  725.7 6.4 collective-permute-done.1
  734.1 6.4 collective-permute-done.2
  742.7 6.2 collective-permute-done.3
  751.0 6.4 collective-permute-done
  759.4 6.4 collective-permute-done.1
  767.8 6.4 collective-permute-done.2
  776.4 6.2 collective-permute-done.3
  783.3 6.6 all-to-all-start.7
  790.5 7.1 all-to-all-done.7
  802.7 6.1 all-to-all-done.6
  808.8 3.4 all-to-all-start.5
  812.8 7.4 all-to-all-done.5
  820.2 3.4 all-to-all-start.3
  824.9 6.7 all-to-all-done.3
  (848 shorter events, 608.5 us)
Async XLA Ops:
  8.5 14.7 %all-to-all-start = ((bf16[16,8,128]{2,0,1:T(8,128)(2,1)}), bf16[16,8,128]{2,0,1:T(8,128)(2,1)S(1)}, u32[]{:S(2)}, u32[]{:S(2)}) async-start(bf16[16,8,128]{2,0,1:T(8,128)(2,1)} %copy_bitcast_fusion.7), calls=%async_computation | async-start | bytes 65536 | tf_op jit(solution)/shard_map/all_to_all | solution.py:33
  15.5 135.4 %all-gather.2.cloned.1.call-start = ((), (), s32[]{:S(2)}) async-start(), calls=%async_computation.8 | async-start | bytes 4259840 | tf_op jit(solution)/shard_map/all_gather | solution.py:15
  35.6 11.4 %all-to-all-start.2 = ((bf16[16,8,512]{2,0,1:T(8,128)(2,1)}), bf16[16,8,512]{2,0,1:T(8,128)(2,1)S(1)}, u32[]{:S(2)}, u32[]{:S(2)}) async-start(bf16[16,8,512]{2,0,1:T(8,128)(2,1)} %bitcast.304), calls=%async_computation.2 | async-start | bytes 262144 | tf_op jit(solution)/shard_map/all_to_all | solution.py:32
  47.0 11.4 %all-to-all-start.4 = ((bf16[16,8,512]{2,0,1:T(8,128)(2,1)}), bf16[16,8,512]{2,0,1:T(8,128)(2,1)S(1)}, u32[]{:S(2)}, u32[]{:S(2)}) async-start(bf16[16,8,512]{2,0,1:T(8,128)(2,1)} %bitcast.303), calls=%async_computation.4 | async-start | bytes 262144 | tf_op jit(solution)/shard_map/all_to_all | solution.py:35
  204.0 8.4 %collective-permute-start = (f32[2,1,128,128]{3,2,1,0:T(8,128)S(1)}, f32[2,1,128,128]{3,2,1,0:T(8,128)S(1)}, u32[]{:S(2)}, u32[]{:S(2)}) collective-permute-start(f32[2,1,128,128]{3,2,1,0:T(8,128)S(1)} %add.491), channel_id=1, source_target_pairs={{504,0},{0,8},{8,16},{16,24},{24,32},{32,40},{40,48},{48,56},{56,6... | collective-permute-start | bytes 393224 | tf_op jit(solution)/shard_map/while/body/eval_jaxpr/ppermute | solution.py:25
  212.4 8.4 %collective-permute-start.1 = (f32[2,1,128,128]{3,2,1,0:T(8,128)S(1)}, f32[2,1,128,128]{3,2,1,0:T(8,128)S(1)}, u32[]{:S(2)}, u32[]{:S(2)}) collective-permute-start(f32[2,1,128,128]{3,2,1,0:T(8,128)S(1)} %add.492), channel_id=1, source_target_pairs={{504,0},{0,8},{8,16},{16,24},{24,32},{32,40},{40,48},{48,56},{56,6... | collective-permute-start | bytes 393224 | tf_op jit(solution)/shard_map/while/body/eval_jaxpr/ppermute | solution.py:25
  220.8 8.4 %collective-permute-start.2 = (f32[2,1,128,128]{3,2,1,0:T(8,128)S(1)}, f32[2,1,128,128]{3,2,1,0:T(8,128)S(1)}, u32[]{:S(2)}, u32[]{:S(2)}) collective-permute-start(f32[2,1,128,128]{3,2,1,0:T(8,128)S(1)} %add.493), channel_id=1, source_target_pairs={{504,0},{0,8},{8,16},{16,24},{24,32},{32,40},{40,48},{48,56},{56,6... | collective-permute-start | bytes 393224 | tf_op jit(solution)/shard_map/while/body/eval_jaxpr/ppermute | solution.py:25
  229.3 8.4 %collective-permute-start.3 = (f32[2,1,128,128]{3,2,1,0:T(8,128)S(1)}, f32[2,1,128,128]{3,2,1,0:T(8,128)S(1)}, u32[]{:S(2)}, u32[]{:S(2)}) collective-permute-start(f32[2,1,128,128]{3,2,1,0:T(8,128)S(1)} %add.494), channel_id=1, source_target_pairs={{504,0},{0,8},{8,16},{16,24},{24,32},{32,40},{40,48},{48,56},{56,6... | collective-permute-start | bytes 393224 | tf_op jit(solution)/shard_map/while/body/eval_jaxpr/ppermute | solution.py:25
  241.0 8.4 %collective-permute-start = (f32[2,1,128,128]{3,2,1,0:T(8,128)S(1)}, f32[2,1,128,128]{3,2,1,0:T(8,128)S(1)}, u32[]{:S(2)}, u32[]{:S(2)}) collective-permute-start(f32[2,1,128,128]{3,2,1,0:T(8,128)S(1)} %add.491), channel_id=1, source_target_pairs={{504,0},{0,8},{8,16},{16,24},{24,32},{32,40},{40,48},{48,56},{56,6... | collective-permute-start | bytes 393224 | tf_op jit(solution)/shard_map/while/body/eval_jaxpr/ppermute | solution.py:25
  249.4 8.4 %collective-permute-start.1 = (f32[2,1,128,128]{3,2,1,0:T(8,128)S(1)}, f32[2,1,128,128]{3,2,1,0:T(8,128)S(1)}, u32[]{:S(2)}, u32[]{:S(2)}) collective-permute-start(f32[2,1,128,128]{3,2,1,0:T(8,128)S(1)} %add.492), channel_id=1, source_target_pairs={{504,0},{0,8},{8,16},{16,24},{24,32},{32,40},{40,48},{48,56},{56,6... | collective-permute-start | bytes 393224 | tf_op jit(solution)/shard_map/while/body/eval_jaxpr/ppermute | solution.py:25
  257.8 8.4 %collective-permute-start.2 = (f32[2,1,128,128]{3,2,1,0:T(8,128)S(1)}, f32[2,1,128,128]{3,2,1,0:T(8,128)S(1)}, u32[]{:S(2)}, u32[]{:S(2)}) collective-permute-start(f32[2,1,128,128]{3,2,1,0:T(8,128)S(1)} %add.493), channel_id=1, source_target_pairs={{504,0},{0,8},{8,16},{16,24},{24,32},{32,40},{40,48},{48,56},{56,6... | collective-permute-start | bytes 393224 | tf_op jit(solution)/shard_map/while/body/eval_jaxpr/ppermute | solution.py:25
  266.2 8.4 %collective-permute-start.3 = (f32[2,1,128,128]{3,2,1,0:T(8,128)S(1)}, f32[2,1,128,128]{3,2,1,0:T(8,128)S(1)}, u32[]{:S(2)}, u32[]{:S(2)}) collective-permute-start(f32[2,1,128,128]{3,2,1,0:T(8,128)S(1)} %add.494), channel_id=1, source_target_pairs={{504,0},{0,8},{8,16},{16,24},{24,32},{32,40},{40,48},{48,56},{56,6... | collective-permute-start | bytes 393224 | tf_op jit(solution)/shard_map/while/body/eval_jaxpr/ppermute | solution.py:25
  278.0 8.4 %collective-permute-start = (f32[2,1,128,128]{3,2,1,0:T(8,128)S(1)}, f32[2,1,128,128]{3,2,1,0:T(8,128)S(1)}, u32[]{:S(2)}, u32[]{:S(2)}) collective-permute-start(f32[2,1,128,128]{3,2,1,0:T(8,128)S(1)} %add.491), channel_id=1, source_target_pairs={{504,0},{0,8},{8,16},{16,24},{24,32},{32,40},{40,48},{48,56},{56,6... | collective-permute-start | bytes 393224 | tf_op jit(solution)/shard_map/while/body/eval_jaxpr/ppermute | solution.py:25
  286.4 8.4 %collective-permute-start.1 = (f32[2,1,128,128]{3,2,1,0:T(8,128)S(1)}, f32[2,1,128,128]{3,2,1,0:T(8,128)S(1)}, u32[]{:S(2)}, u32[]{:S(2)}) collective-permute-start(f32[2,1,128,128]{3,2,1,0:T(8,128)S(1)} %add.492), channel_id=1, source_target_pairs={{504,0},{0,8},{8,16},{16,24},{24,32},{32,40},{40,48},{48,56},{56,6... | collective-permute-start | bytes 393224 | tf_op jit(solution)/shard_map/while/body/eval_jaxpr/ppermute | solution.py:25
  294.8 8.4 %collective-permute-start.2 = (f32[2,1,128,128]{3,2,1,0:T(8,128)S(1)}, f32[2,1,128,128]{3,2,1,0:T(8,128)S(1)}, u32[]{:S(2)}, u32[]{:S(2)}) collective-permute-start(f32[2,1,128,128]{3,2,1,0:T(8,128)S(1)} %add.493), channel_id=1, source_target_pairs={{504,0},{0,8},{8,16},{16,24},{24,32},{32,40},{40,48},{48,56},{56,6... | collective-permute-start | bytes 393224 | tf_op jit(solution)/shard_map/while/body/eval_jaxpr/ppermute | solution.py:25
  303.2 8.4 %collective-permute-start.3 = (f32[2,1,128,128]{3,2,1,0:T(8,128)S(1)}, f32[2,1,128,128]{3,2,1,0:T(8,128)S(1)}, u32[]{:S(2)}, u32[]{:S(2)}) collective-permute-start(f32[2,1,128,128]{3,2,1,0:T(8,128)S(1)} %add.494), channel_id=1, source_target_pairs={{504,0},{0,8},{8,16},{16,24},{24,32},{32,40},{40,48},{48,56},{56,6... | collective-permute-start | bytes 393224 | tf_op jit(solution)/shard_map/while/body/eval_jaxpr/ppermute | solution.py:25
  315.0 8.4 %collective-permute-start = (f32[2,1,128,128]{3,2,1,0:T(8,128)S(1)}, f32[2,1,128,128]{3,2,1,0:T(8,128)S(1)}, u32[]{:S(2)}, u32[]{:S(2)}) collective-permute-start(f32[2,1,128,128]{3,2,1,0:T(8,128)S(1)} %add.491), channel_id=1, source_target_pairs={{504,0},{0,8},{8,16},{16,24},{24,32},{32,40},{40,48},{48,56},{56,6... | collective-permute-start | bytes 393224 | tf_op jit(solution)/shard_map/while/body/eval_jaxpr/ppermute | solution.py:25
  323.4 8.4 %collective-permute-start.1 = (f32[2,1,128,128]{3,2,1,0:T(8,128)S(1)}, f32[2,1,128,128]{3,2,1,0:T(8,128)S(1)}, u32[]{:S(2)}, u32[]{:S(2)}) collective-permute-start(f32[2,1,128,128]{3,2,1,0:T(8,128)S(1)} %add.492), channel_id=1, source_target_pairs={{504,0},{0,8},{8,16},{16,24},{24,32},{32,40},{40,48},{48,56},{56,6... | collective-permute-start | bytes 393224 | tf_op jit(solution)/shard_map/while/body/eval_jaxpr/ppermute | solution.py:25
  331.8 8.4 %collective-permute-start.2 = (f32[2,1,128,128]{3,2,1,0:T(8,128)S(1)}, f32[2,1,128,128]{3,2,1,0:T(8,128)S(1)}, u32[]{:S(2)}, u32[]{:S(2)}) collective-permute-start(f32[2,1,128,128]{3,2,1,0:T(8,128)S(1)} %add.493), channel_id=1, source_target_pairs={{504,0},{0,8},{8,16},{16,24},{24,32},{32,40},{40,48},{48,56},{56,6... | collective-permute-start | bytes 393224 | tf_op jit(solution)/shard_map/while/body/eval_jaxpr/ppermute | solution.py:25
  340.2 8.4 %collective-permute-start.3 = (f32[2,1,128,128]{3,2,1,0:T(8,128)S(1)}, f32[2,1,128,128]{3,2,1,0:T(8,128)S(1)}, u32[]{:S(2)}, u32[]{:S(2)}) collective-permute-start(f32[2,1,128,128]{3,2,1,0:T(8,128)S(1)} %add.494), channel_id=1, source_target_pairs={{504,0},{0,8},{8,16},{16,24},{24,32},{32,40},{40,48},{48,56},{56,6... | collective-permute-start | bytes 393224 | tf_op jit(solution)/shard_map/while/body/eval_jaxpr/ppermute | solution.py:25
  352.0 8.4 %collective-permute-start = (f32[2,1,128,128]{3,2,1,0:T(8,128)S(1)}, f32[2,1,128,128]{3,2,1,0:T(8,128)S(1)}, u32[]{:S(2)}, u32[]{:S(2)}) collective-permute-start(f32[2,1,128,128]{3,2,1,0:T(8,128)S(1)} %add.491), channel_id=1, source_target_pairs={{504,0},{0,8},{8,16},{16,24},{24,32},{32,40},{40,48},{48,56},{56,6... | collective-permute-start | bytes 393224 | tf_op jit(solution)/shard_map/while/body/eval_jaxpr/ppermute | solution.py:25
  360.4 8.4 %collective-permute-start.1 = (f32[2,1,128,128]{3,2,1,0:T(8,128)S(1)}, f32[2,1,128,128]{3,2,1,0:T(8,128)S(1)}, u32[]{:S(2)}, u32[]{:S(2)}) collective-permute-start(f32[2,1,128,128]{3,2,1,0:T(8,128)S(1)} %add.492), channel_id=1, source_target_pairs={{504,0},{0,8},{8,16},{16,24},{24,32},{32,40},{40,48},{48,56},{56,6... | collective-permute-start | bytes 393224 | tf_op jit(solution)/shard_map/while/body/eval_jaxpr/ppermute | solution.py:25
  368.8 8.4 %collective-permute-start.2 = (f32[2,1,128,128]{3,2,1,0:T(8,128)S(1)}, f32[2,1,128,128]{3,2,1,0:T(8,128)S(1)}, u32[]{:S(2)}, u32[]{:S(2)}) collective-permute-start(f32[2,1,128,128]{3,2,1,0:T(8,128)S(1)} %add.493), channel_id=1, source_target_pairs={{504,0},{0,8},{8,16},{16,24},{24,32},{32,40},{40,48},{48,56},{56,6... | collective-permute-start | bytes 393224 | tf_op jit(solution)/shard_map/while/body/eval_jaxpr/ppermute | solution.py:25
  377.2 8.4 %collective-permute-start.3 = (f32[2,1,128,128]{3,2,1,0:T(8,128)S(1)}, f32[2,1,128,128]{3,2,1,0:T(8,128)S(1)}, u32[]{:S(2)}, u32[]{:S(2)}) collective-permute-start(f32[2,1,128,128]{3,2,1,0:T(8,128)S(1)} %add.494), channel_id=1, source_target_pairs={{504,0},{0,8},{8,16},{16,24},{24,32},{32,40},{40,48},{48,56},{56,6... | collective-permute-start | bytes 393224 | tf_op jit(solution)/shard_map/while/body/eval_jaxpr/ppermute | solution.py:25
  388.9 8.4 %collective-permute-start = (f32[2,1,128,128]{3,2,1,0:T(8,128)S(1)}, f32[2,1,128,128]{3,2,1,0:T(8,128)S(1)}, u32[]{:S(2)}, u32[]{:S(2)}) collective-permute-start(f32[2,1,128,128]{3,2,1,0:T(8,128)S(1)} %add.491), channel_id=1, source_target_pairs={{504,0},{0,8},{8,16},{16,24},{24,32},{32,40},{40,48},{48,56},{56,6... | collective-permute-start | bytes 393224 | tf_op jit(solution)/shard_map/while/body/eval_jaxpr/ppermute | solution.py:25
  397.4 8.4 %collective-permute-start.1 = (f32[2,1,128,128]{3,2,1,0:T(8,128)S(1)}, f32[2,1,128,128]{3,2,1,0:T(8,128)S(1)}, u32[]{:S(2)}, u32[]{:S(2)}) collective-permute-start(f32[2,1,128,128]{3,2,1,0:T(8,128)S(1)} %add.492), channel_id=1, source_target_pairs={{504,0},{0,8},{8,16},{16,24},{24,32},{32,40},{40,48},{48,56},{56,6... | collective-permute-start | bytes 393224 | tf_op jit(solution)/shard_map/while/body/eval_jaxpr/ppermute | solution.py:25
  405.8 8.4 %collective-permute-start.2 = (f32[2,1,128,128]{3,2,1,0:T(8,128)S(1)}, f32[2,1,128,128]{3,2,1,0:T(8,128)S(1)}, u32[]{:S(2)}, u32[]{:S(2)}) collective-permute-start(f32[2,1,128,128]{3,2,1,0:T(8,128)S(1)} %add.493), channel_id=1, source_target_pairs={{504,0},{0,8},{8,16},{16,24},{24,32},{32,40},{40,48},{48,56},{56,6... | collective-permute-start | bytes 393224 | tf_op jit(solution)/shard_map/while/body/eval_jaxpr/ppermute | solution.py:25
  414.2 8.4 %collective-permute-start.3 = (f32[2,1,128,128]{3,2,1,0:T(8,128)S(1)}, f32[2,1,128,128]{3,2,1,0:T(8,128)S(1)}, u32[]{:S(2)}, u32[]{:S(2)}) collective-permute-start(f32[2,1,128,128]{3,2,1,0:T(8,128)S(1)} %add.494), channel_id=1, source_target_pairs={{504,0},{0,8},{8,16},{16,24},{24,32},{32,40},{40,48},{48,56},{56,6... | collective-permute-start | bytes 393224 | tf_op jit(solution)/shard_map/while/body/eval_jaxpr/ppermute | solution.py:25
  425.9 8.4 %collective-permute-start = (f32[2,1,128,128]{3,2,1,0:T(8,128)S(1)}, f32[2,1,128,128]{3,2,1,0:T(8,128)S(1)}, u32[]{:S(2)}, u32[]{:S(2)}) collective-permute-start(f32[2,1,128,128]{3,2,1,0:T(8,128)S(1)} %add.491), channel_id=1, source_target_pairs={{504,0},{0,8},{8,16},{16,24},{24,32},{32,40},{40,48},{48,56},{56,6... | collective-permute-start | bytes 393224 | tf_op jit(solution)/shard_map/while/body/eval_jaxpr/ppermute | solution.py:25
  442.8 8.4 %collective-permute-start.2 = (f32[2,1,128,128]{3,2,1,0:T(8,128)S(1)}, f32[2,1,128,128]{3,2,1,0:T(8,128)S(1)}, u32[]{:S(2)}, u32[]{:S(2)}) collective-permute-start(f32[2,1,128,128]{3,2,1,0:T(8,128)S(1)} %add.493), channel_id=1, source_target_pairs={{504,0},{0,8},{8,16},{16,24},{24,32},{32,40},{40,48},{48,56},{56,6... | collective-permute-start | bytes 393224 | tf_op jit(solution)/shard_map/while/body/eval_jaxpr/ppermute | solution.py:25
  462.9 8.4 %collective-permute-start = (f32[2,1,128,128]{3,2,1,0:T(8,128)S(1)}, f32[2,1,128,128]{3,2,1,0:T(8,128)S(1)}, u32[]{:S(2)}, u32[]{:S(2)}) collective-permute-start(f32[2,1,128,128]{3,2,1,0:T(8,128)S(1)} %add.491), channel_id=1, source_target_pairs={{504,0},{0,8},{8,16},{16,24},{24,32},{32,40},{40,48},{48,56},{56,6... | collective-permute-start | bytes 393224 | tf_op jit(solution)/shard_map/while/body/eval_jaxpr/ppermute | solution.py:25
  471.3 8.4 %collective-permute-start.1 = (f32[2,1,128,128]{3,2,1,0:T(8,128)S(1)}, f32[2,1,128,128]{3,2,1,0:T(8,128)S(1)}, u32[]{:S(2)}, u32[]{:S(2)}) collective-permute-start(f32[2,1,128,128]{3,2,1,0:T(8,128)S(1)} %add.492), channel_id=1, source_target_pairs={{504,0},{0,8},{8,16},{16,24},{24,32},{32,40},{40,48},{48,56},{56,6... | collective-permute-start | bytes 393224 | tf_op jit(solution)/shard_map/while/body/eval_jaxpr/ppermute | solution.py:25
  479.7 8.4 %collective-permute-start.2 = (f32[2,1,128,128]{3,2,1,0:T(8,128)S(1)}, f32[2,1,128,128]{3,2,1,0:T(8,128)S(1)}, u32[]{:S(2)}, u32[]{:S(2)}) collective-permute-start(f32[2,1,128,128]{3,2,1,0:T(8,128)S(1)} %add.493), channel_id=1, source_target_pairs={{504,0},{0,8},{8,16},{16,24},{24,32},{32,40},{40,48},{48,56},{56,6... | collective-permute-start | bytes 393224 | tf_op jit(solution)/shard_map/while/body/eval_jaxpr/ppermute | solution.py:25
  488.2 8.4 %collective-permute-start.3 = (f32[2,1,128,128]{3,2,1,0:T(8,128)S(1)}, f32[2,1,128,128]{3,2,1,0:T(8,128)S(1)}, u32[]{:S(2)}, u32[]{:S(2)}) collective-permute-start(f32[2,1,128,128]{3,2,1,0:T(8,128)S(1)} %add.494), channel_id=1, source_target_pairs={{504,0},{0,8},{8,16},{16,24},{24,32},{32,40},{40,48},{48,56},{56,6... | collective-permute-start | bytes 393224 | tf_op jit(solution)/shard_map/while/body/eval_jaxpr/ppermute | solution.py:25
  508.3 8.4 %collective-permute-start.1 = (f32[2,1,128,128]{3,2,1,0:T(8,128)S(1)}, f32[2,1,128,128]{3,2,1,0:T(8,128)S(1)}, u32[]{:S(2)}, u32[]{:S(2)}) collective-permute-start(f32[2,1,128,128]{3,2,1,0:T(8,128)S(1)} %add.492), channel_id=1, source_target_pairs={{504,0},{0,8},{8,16},{16,24},{24,32},{32,40},{40,48},{48,56},{56,6... | collective-permute-start | bytes 393224 | tf_op jit(solution)/shard_map/while/body/eval_jaxpr/ppermute | solution.py:25
  516.7 8.4 %collective-permute-start.2 = (f32[2,1,128,128]{3,2,1,0:T(8,128)S(1)}, f32[2,1,128,128]{3,2,1,0:T(8,128)S(1)}, u32[]{:S(2)}, u32[]{:S(2)}) collective-permute-start(f32[2,1,128,128]{3,2,1,0:T(8,128)S(1)} %add.493), channel_id=1, source_target_pairs={{504,0},{0,8},{8,16},{16,24},{24,32},{32,40},{40,48},{48,56},{56,6... | collective-permute-start | bytes 393224 | tf_op jit(solution)/shard_map/while/body/eval_jaxpr/ppermute | solution.py:25
  525.1 8.4 %collective-permute-start.3 = (f32[2,1,128,128]{3,2,1,0:T(8,128)S(1)}, f32[2,1,128,128]{3,2,1,0:T(8,128)S(1)}, u32[]{:S(2)}, u32[]{:S(2)}) collective-permute-start(f32[2,1,128,128]{3,2,1,0:T(8,128)S(1)} %add.494), channel_id=1, source_target_pairs={{504,0},{0,8},{8,16},{16,24},{24,32},{32,40},{40,48},{48,56},{56,6... | collective-permute-start | bytes 393224 | tf_op jit(solution)/shard_map/while/body/eval_jaxpr/ppermute | solution.py:25
  545.3 8.4 %collective-permute-start.1 = (f32[2,1,128,128]{3,2,1,0:T(8,128)S(1)}, f32[2,1,128,128]{3,2,1,0:T(8,128)S(1)}, u32[]{:S(2)}, u32[]{:S(2)}) collective-permute-start(f32[2,1,128,128]{3,2,1,0:T(8,128)S(1)} %add.492), channel_id=1, source_target_pairs={{504,0},{0,8},{8,16},{16,24},{24,32},{32,40},{40,48},{48,56},{56,6... | collective-permute-start | bytes 393224 | tf_op jit(solution)/shard_map/while/body/eval_jaxpr/ppermute | solution.py:25
  562.1 8.4 %collective-permute-start.3 = (f32[2,1,128,128]{3,2,1,0:T(8,128)S(1)}, f32[2,1,128,128]{3,2,1,0:T(8,128)S(1)}, u32[]{:S(2)}, u32[]{:S(2)}) collective-permute-start(f32[2,1,128,128]{3,2,1,0:T(8,128)S(1)} %add.494), channel_id=1, source_target_pairs={{504,0},{0,8},{8,16},{16,24},{24,32},{32,40},{40,48},{48,56},{56,6... | collective-permute-start | bytes 393224 | tf_op jit(solution)/shard_map/while/body/eval_jaxpr/ppermute | solution.py:25
  573.9 8.4 %collective-permute-start = (f32[2,1,128,128]{3,2,1,0:T(8,128)S(1)}, f32[2,1,128,128]{3,2,1,0:T(8,128)S(1)}, u32[]{:S(2)}, u32[]{:S(2)}) collective-permute-start(f32[2,1,128,128]{3,2,1,0:T(8,128)S(1)} %add.491), channel_id=1, source_target_pairs={{504,0},{0,8},{8,16},{16,24},{24,32},{32,40},{40,48},{48,56},{56,6... | collective-permute-start | bytes 393224 | tf_op jit(solution)/shard_map/while/body/eval_jaxpr/ppermute | solution.py:25
  582.3 8.4 %collective-permute-start.1 = (f32[2,1,128,128]{3,2,1,0:T(8,128)S(1)}, f32[2,1,128,128]{3,2,1,0:T(8,128)S(1)}, u32[]{:S(2)}, u32[]{:S(2)}) collective-permute-start(f32[2,1,128,128]{3,2,1,0:T(8,128)S(1)} %add.492), channel_id=1, source_target_pairs={{504,0},{0,8},{8,16},{16,24},{24,32},{32,40},{40,48},{48,56},{56,6... | collective-permute-start | bytes 393224 | tf_op jit(solution)/shard_map/while/body/eval_jaxpr/ppermute | solution.py:25
  590.7 8.4 %collective-permute-start.2 = (f32[2,1,128,128]{3,2,1,0:T(8,128)S(1)}, f32[2,1,128,128]{3,2,1,0:T(8,128)S(1)}, u32[]{:S(2)}, u32[]{:S(2)}) collective-permute-start(f32[2,1,128,128]{3,2,1,0:T(8,128)S(1)} %add.493), channel_id=1, source_target_pairs={{504,0},{0,8},{8,16},{16,24},{24,32},{32,40},{40,48},{48,56},{56,6... | collective-permute-start | bytes 393224 | tf_op jit(solution)/shard_map/while/body/eval_jaxpr/ppermute | solution.py:25
  599.1 8.4 %collective-permute-start.3 = (f32[2,1,128,128]{3,2,1,0:T(8,128)S(1)}, f32[2,1,128,128]{3,2,1,0:T(8,128)S(1)}, u32[]{:S(2)}, u32[]{:S(2)}) collective-permute-start(f32[2,1,128,128]{3,2,1,0:T(8,128)S(1)} %add.494), channel_id=1, source_target_pairs={{504,0},{0,8},{8,16},{16,24},{24,32},{32,40},{40,48},{48,56},{56,6... | collective-permute-start | bytes 393224 | tf_op jit(solution)/shard_map/while/body/eval_jaxpr/ppermute | solution.py:25
  610.9 8.4 %collective-permute-start = (f32[2,1,128,128]{3,2,1,0:T(8,128)S(1)}, f32[2,1,128,128]{3,2,1,0:T(8,128)S(1)}, u32[]{:S(2)}, u32[]{:S(2)}) collective-permute-start(f32[2,1,128,128]{3,2,1,0:T(8,128)S(1)} %add.491), channel_id=1, source_target_pairs={{504,0},{0,8},{8,16},{16,24},{24,32},{32,40},{40,48},{48,56},{56,6... | collective-permute-start | bytes 393224 | tf_op jit(solution)/shard_map/while/body/eval_jaxpr/ppermute | solution.py:25
  619.3 8.4 %collective-permute-start.1 = (f32[2,1,128,128]{3,2,1,0:T(8,128)S(1)}, f32[2,1,128,128]{3,2,1,0:T(8,128)S(1)}, u32[]{:S(2)}, u32[]{:S(2)}) collective-permute-start(f32[2,1,128,128]{3,2,1,0:T(8,128)S(1)} %add.492), channel_id=1, source_target_pairs={{504,0},{0,8},{8,16},{16,24},{24,32},{32,40},{40,48},{48,56},{56,6... | collective-permute-start | bytes 393224 | tf_op jit(solution)/shard_map/while/body/eval_jaxpr/ppermute | solution.py:25
  627.7 8.4 %collective-permute-start.2 = (f32[2,1,128,128]{3,2,1,0:T(8,128)S(1)}, f32[2,1,128,128]{3,2,1,0:T(8,128)S(1)}, u32[]{:S(2)}, u32[]{:S(2)}) collective-permute-start(f32[2,1,128,128]{3,2,1,0:T(8,128)S(1)} %add.493), channel_id=1, source_target_pairs={{504,0},{0,8},{8,16},{16,24},{24,32},{32,40},{40,48},{48,56},{56,6... | collective-permute-start | bytes 393224 | tf_op jit(solution)/shard_map/while/body/eval_jaxpr/ppermute | solution.py:25
  636.1 8.4 %collective-permute-start.3 = (f32[2,1,128,128]{3,2,1,0:T(8,128)S(1)}, f32[2,1,128,128]{3,2,1,0:T(8,128)S(1)}, u32[]{:S(2)}, u32[]{:S(2)}) collective-permute-start(f32[2,1,128,128]{3,2,1,0:T(8,128)S(1)} %add.494), channel_id=1, source_target_pairs={{504,0},{0,8},{8,16},{16,24},{24,32},{32,40},{40,48},{48,56},{56,6... | collective-permute-start | bytes 393224 | tf_op jit(solution)/shard_map/while/body/eval_jaxpr/ppermute | solution.py:25
  647.8 8.4 %collective-permute-start = (f32[2,1,128,128]{3,2,1,0:T(8,128)S(1)}, f32[2,1,128,128]{3,2,1,0:T(8,128)S(1)}, u32[]{:S(2)}, u32[]{:S(2)}) collective-permute-start(f32[2,1,128,128]{3,2,1,0:T(8,128)S(1)} %add.491), channel_id=1, source_target_pairs={{504,0},{0,8},{8,16},{16,24},{24,32},{32,40},{40,48},{48,56},{56,6... | collective-permute-start | bytes 393224 | tf_op jit(solution)/shard_map/while/body/eval_jaxpr/ppermute | solution.py:25
  664.7 8.4 %collective-permute-start.2 = (f32[2,1,128,128]{3,2,1,0:T(8,128)S(1)}, f32[2,1,128,128]{3,2,1,0:T(8,128)S(1)}, u32[]{:S(2)}, u32[]{:S(2)}) collective-permute-start(f32[2,1,128,128]{3,2,1,0:T(8,128)S(1)} %add.493), channel_id=1, source_target_pairs={{504,0},{0,8},{8,16},{16,24},{24,32},{32,40},{40,48},{48,56},{56,6... | collective-permute-start | bytes 393224 | tf_op jit(solution)/shard_map/while/body/eval_jaxpr/ppermute | solution.py:25
  681.6 8.4 %collective-permute-start = (f32[2,1,128,128]{3,2,1,0:T(8,128)S(1)}, f32[2,1,128,128]{3,2,1,0:T(8,128)S(1)}, u32[]{:S(2)}, u32[]{:S(2)}) collective-permute-start(f32[2,1,128,128]{3,2,1,0:T(8,128)S(1)} %add.491), channel_id=1, source_target_pairs={{504,0},{0,8},{8,16},{16,24},{24,32},{32,40},{40,48},{48,56},{56,6... | collective-permute-start | bytes 393224 | tf_op jit(solution)/shard_map/while/body/eval_jaxpr/ppermute | solution.py:25
  690.0 8.4 %collective-permute-start.1 = (f32[2,1,128,128]{3,2,1,0:T(8,128)S(1)}, f32[2,1,128,128]{3,2,1,0:T(8,128)S(1)}, u32[]{:S(2)}, u32[]{:S(2)}) collective-permute-start(f32[2,1,128,128]{3,2,1,0:T(8,128)S(1)} %add.492), channel_id=1, source_target_pairs={{504,0},{0,8},{8,16},{16,24},{24,32},{32,40},{40,48},{48,56},{56,6... | collective-permute-start | bytes 393224 | tf_op jit(solution)/shard_map/while/body/eval_jaxpr/ppermute | solution.py:25
  706.8 8.4 %collective-permute-start.3 = (f32[2,1,128,128]{3,2,1,0:T(8,128)S(1)}, f32[2,1,128,128]{3,2,1,0:T(8,128)S(1)}, u32[]{:S(2)}, u32[]{:S(2)}) collective-permute-start(f32[2,1,128,128]{3,2,1,0:T(8,128)S(1)} %add.494), channel_id=1, source_target_pairs={{504,0},{0,8},{8,16},{16,24},{24,32},{32,40},{40,48},{48,56},{56,6... | collective-permute-start | bytes 393224 | tf_op jit(solution)/shard_map/while/body/eval_jaxpr/ppermute | solution.py:25
  715.3 8.4 %collective-permute-start = (f32[2,1,128,128]{3,2,1,0:T(8,128)S(1)}, f32[2,1,128,128]{3,2,1,0:T(8,128)S(1)}, u32[]{:S(2)}, u32[]{:S(2)}) collective-permute-start(f32[2,1,128,128]{3,2,1,0:T(8,128)S(1)} %add.491), channel_id=1, source_target_pairs={{504,0},{0,8},{8,16},{16,24},{24,32},{32,40},{40,48},{48,56},{56,6... | collective-permute-start | bytes 393224 | tf_op jit(solution)/shard_map/while/body/eval_jaxpr/ppermute | solution.py:25
  723.7 8.4 %collective-permute-start.1 = (f32[2,1,128,128]{3,2,1,0:T(8,128)S(1)}, f32[2,1,128,128]{3,2,1,0:T(8,128)S(1)}, u32[]{:S(2)}, u32[]{:S(2)}) collective-permute-start(f32[2,1,128,128]{3,2,1,0:T(8,128)S(1)} %add.492), channel_id=1, source_target_pairs={{504,0},{0,8},{8,16},{16,24},{24,32},{32,40},{40,48},{48,56},{56,6... | collective-permute-start | bytes 393224 | tf_op jit(solution)/shard_map/while/body/eval_jaxpr/ppermute | solution.py:25
  732.1 8.4 %collective-permute-start.2 = (f32[2,1,128,128]{3,2,1,0:T(8,128)S(1)}, f32[2,1,128,128]{3,2,1,0:T(8,128)S(1)}, u32[]{:S(2)}, u32[]{:S(2)}) collective-permute-start(f32[2,1,128,128]{3,2,1,0:T(8,128)S(1)} %add.493), channel_id=1, source_target_pairs={{504,0},{0,8},{8,16},{16,24},{24,32},{32,40},{40,48},{48,56},{56,6... | collective-permute-start | bytes 393224 | tf_op jit(solution)/shard_map/while/body/eval_jaxpr/ppermute | solution.py:25
  740.5 8.4 %collective-permute-start.3 = (f32[2,1,128,128]{3,2,1,0:T(8,128)S(1)}, f32[2,1,128,128]{3,2,1,0:T(8,128)S(1)}, u32[]{:S(2)}, u32[]{:S(2)}) collective-permute-start(f32[2,1,128,128]{3,2,1,0:T(8,128)S(1)} %add.494), channel_id=1, source_target_pairs={{504,0},{0,8},{8,16},{16,24},{24,32},{32,40},{40,48},{48,56},{56,6... | collective-permute-start | bytes 393224 | tf_op jit(solution)/shard_map/while/body/eval_jaxpr/ppermute | solution.py:25
  749.0 8.4 %collective-permute-start = (f32[2,1,128,128]{3,2,1,0:T(8,128)S(1)}, f32[2,1,128,128]{3,2,1,0:T(8,128)S(1)}, u32[]{:S(2)}, u32[]{:S(2)}) collective-permute-start(f32[2,1,128,128]{3,2,1,0:T(8,128)S(1)} %add.491), channel_id=1, source_target_pairs={{504,0},{0,8},{8,16},{16,24},{24,32},{32,40},{40,48},{48,56},{56,6... | collective-permute-start | bytes 393224 | tf_op jit(solution)/shard_map/while/body/eval_jaxpr/ppermute | solution.py:25
  757.4 8.4 %collective-permute-start.1 = (f32[2,1,128,128]{3,2,1,0:T(8,128)S(1)}, f32[2,1,128,128]{3,2,1,0:T(8,128)S(1)}, u32[]{:S(2)}, u32[]{:S(2)}) collective-permute-start(f32[2,1,128,128]{3,2,1,0:T(8,128)S(1)} %add.492), channel_id=1, source_target_pairs={{504,0},{0,8},{8,16},{16,24},{24,32},{32,40},{40,48},{48,56},{56,6... | collective-permute-start | bytes 393224 | tf_op jit(solution)/shard_map/while/body/eval_jaxpr/ppermute | solution.py:25
  765.8 8.4 %collective-permute-start.2 = (f32[2,1,128,128]{3,2,1,0:T(8,128)S(1)}, f32[2,1,128,128]{3,2,1,0:T(8,128)S(1)}, u32[]{:S(2)}, u32[]{:S(2)}) collective-permute-start(f32[2,1,128,128]{3,2,1,0:T(8,128)S(1)} %add.493), channel_id=1, source_target_pairs={{504,0},{0,8},{8,16},{16,24},{24,32},{32,40},{40,48},{48,56},{56,6... | collective-permute-start | bytes 393224 | tf_op jit(solution)/shard_map/while/body/eval_jaxpr/ppermute | solution.py:25
  774.3 8.4 %collective-permute-start.3 = (f32[2,1,128,128]{3,2,1,0:T(8,128)S(1)}, f32[2,1,128,128]{3,2,1,0:T(8,128)S(1)}, u32[]{:S(2)}, u32[]{:S(2)}) collective-permute-start(f32[2,1,128,128]{3,2,1,0:T(8,128)S(1)} %add.494), channel_id=1, source_target_pairs={{504,0},{0,8},{8,16},{16,24},{24,32},{32,40},{40,48},{48,56},{56,6... | collective-permute-start | bytes 393224 | tf_op jit(solution)/shard_map/while/body/eval_jaxpr/ppermute | solution.py:25
  783.3 14.4 %all-to-all-start.7 = ((bf16[8,16,128]{2,1,0:T(8,128)(2,1)}), bf16[8,16,128]{2,1,0:T(8,128)(2,1)S(1)}, u32[]{:S(2)}, u32[]{:S(2)}) async-start(bf16[8,16,128]{2,1,0:T(8,128)(2,1)} %bitcast.77), calls=%async_computation.7 | async-start | bytes 65536 | tf_op jit(solution)/shard_map/all_to_all | solution.py:172
  797.6 11.1 %all-to-all-start.6 = ((bf16[8,16,128]{2,1,0:T(8,128)(2,1)}), bf16[8,16,128]{2,1,0:T(8,128)(2,1)S(1)}, u32[]{:S(2)}, u32[]{:S(2)}) async-start(bf16[8,16,128]{2,1,0:T(8,128)(2,1)} %bitcast.75), calls=%async_computation.6 | async-start | bytes 65536 | tf_op jit(solution)/shard_map/all_to_all | solution.py:171
  808.8 11.4 %all-to-all-start.5 = ((bf16[8,16,512]{2,1,0:T(8,128)(2,1)}), bf16[8,16,512]{2,1,0:T(8,128)(2,1)S(1)}, u32[]{:S(2)}, u32[]{:S(2)}) async-start(bf16[8,16,512]{2,1,0:T(8,128)(2,1)} %all_to_all.122), calls=%async_computation.5 | async-start | bytes 262144 | tf_op jit(solution)/shard_map/all_to_all | solution.py:170
  820.2 11.4 %all-to-all-start.3 = ((bf16[8,16,512]{2,1,0:T(8,128)(2,1)}), bf16[8,16,512]{2,1,0:T(8,128)(2,1)S(1)}, u32[]{:S(2)}, u32[]{:S(2)}) async-start(bf16[8,16,512]{2,1,0:T(8,128)(2,1)} %all_to_all.115), calls=%async_computation.3 | async-start | bytes 262144 | tf_op jit(solution)/shard_map/all_to_all | solution.py:169
  (9 other events, 67.9 us)
Sparse Core Ops, SparseCore 0:
  34.1 116.6 all-gather.1
where the time goes:
time: 855 us; the launch traced here: 839 us
  waiting for transfers between devices  428 us (50%)
  matrix products  198 us (23%)
  starting transfers between devices  154 us (18%)
  local copies, waits for them, and re-layouts  15.3 us (2%)
  between operations  14.2 us (2%)
  other arithmetic  11.1 us (1%)
  blocking collectives  10.1 us (1%)
    ppermute x64, waiting for transfers between devices, shifted(): return lax.ppermute(block, axis, route)  287 us
    ppermute x64, starting transfers between devices, shifted(): return lax.ppermute(block, axis, route)  123 us
    all_gather x1, waiting for transfers between devices, sent_together(): out, at, outs = (lax.all_gather(both, axis, axis=dim, tiled=True), 0, [])  92.4 us
    dot_general x62, matrix products, masked_logits(): jnp.einsum('hrd,hcd->hrc', query_local, key_block, preferred_element_type...  64.2 us
    dot_general x49, matrix products, gradients(): jnp.einsum('hrc,hcd->hrd', score_grad, key_block, preferred_element_type=...  47.4 us
    dot_general x49, matrix products, gradients(): jnp.einsum('hrd,hcd->hrc', grad_local, value_block, preferred_element_typ...  46.8 us
    dot_general x13, matrix products, out_update(): jnp.einsum('hrc,hcd->hrd', weights, value_block, preferred_element_type=j...  22.6 us
  transfers between devices with their start and end apart: 72, of which 72 were waited for; matrix products, arithmetic and copies ran while one was open for 15% of the time, Pallas kernels for 0%

commit v1 on v0

v1 whole, which is shorter than its diff:
```python
import functools

import jax
import jax.numpy as jnp
from jax import lax
from jax.experimental import pallas as pl
from jax.experimental.pallas import tpu as pltpu
from jax.sharding import Mesh, PartitionSpec as P

D = 128
G = 4
SCALE = D ** (-0.5)
LOG2E = 1.4426950408889634
C2 = SCALE * LOG2E
NEG = -1e30
PLANE = ("xl", "core", "tp")
COLS = ("xl", "core")
NT = (((1,), (1,)), ((), ()))
NN = (((1,), (0,)), ((), ()))
BF = jnp.bfloat16
F32 = jnp.float32


def dot(a, b, dims):
    return lax.dot_general(a, b, dims, preferred_element_type=F32)


def place_keys(z, own, lo1, hi1, lo2, hi2, kv_s, nz):
    for ref, offs in (
        (own, (0, -4, -8, -12)),
        (lo1, (-1, -5, -9, -13)),
        (hi1, (1, -3, -7, -11)),
        (lo2, (-6, -10)),
        (hi2, (2, -2)),
    ):
        for j, off in enumerate(offs):
            kv_s[(z + (off + nz)) % nz] = ref[j]


def chunk_mask(z, c, g, keys, rows, per):
    ki = lax.broadcasted_iota(jnp.int32, (keys, rows), 0)
    ri = lax.broadcasted_iota(jnp.int32, (keys, rows), 1)
    key_pos = (g * (keys // per) + ki // per) * rows + c * per + ki % per
    return key_pos <= z * rows + ri


def fwd_kernel(idx, qd, own, lo1, hi1, lo2, hi2, o_out, st_out, kv_s, vt_s, acc, m_s, l_s):
    z, c = idx[0], idx[1]
    rows = qd.shape[0]
    nz, per, _ = kv_s.shape
    keys = 4 * per
    place_keys(z, own, lo1, hi1, lo2, hi2, kv_s, nz)
    live = z // 4

    def flip(g, _):
        v = kv_s[pl.ds(4 * g, 4)][:, :, D:].reshape(keys, D)
        vt_s[g] = v.T
        return 0

    lax.fori_loop(0, live + 1, flip, 0)
    st_out[...] = jnp.zeros(st_out.shape, F32)
    for h in range(G):
        q = qd[:, h * D : (h + 1) * D]
        m_s[...] = jnp.full(m_s.shape, NEG, F32)
        l_s[...] = jnp.zeros(l_s.shape, F32)
        acc[...] = jnp.zeros(acc.shape, F32)

        def step(g, masked):
            k = kv_s[pl.ds(4 * g, 4)][:, :, :D].reshape(keys, D)
            s = dot(k, q, NT)
            if masked:
                s = jnp.where(chunk_mask(z, c, g, keys, rows, per), s, NEG)
            m_old = m_s[...]
            m_new = jnp.maximum(m_old, jnp.max(s, axis=0, keepdims=True))
            p = jnp.exp2((s - m_new) * C2)
            alpha = jnp.exp2((m_old - m_new) * C2)
            m_s[...] = m_new
            l_s[...] = l_s[...] * alpha + jnp.sum(p, axis=0, keepdims=True)
            acc[...] = acc[...] * alpha + dot(vt_s[g], p.astype(BF), NN)

        def full(g, _):
            step(g, False)
            return 0

        lax.fori_loop(0, live, full, 0)
        step(live, True)
        l = l_s[...]
        o_t = acc[...]
        do_t = qd[:, (G + h) * D : (G + h + 1) * D].T.astype(F32)
        st_out[pl.ds(h, 1), :] = m_s[...]
        st_out[pl.ds(G + h, 1), :] = l
        st_out[pl.ds(2 * G + h, 1), :] = jnp.sum(do_t * o_t, axis=0, keepdims=True)
        o_out[h] = o_t * (1.0 / l)


def bwd_kernel(
    idx, qd, own, lo1, hi1, lo2, hi2, o_in, st_own, st_all,
    od_out, g_own, g_lo1, g_hi1, g_lo2, g_hi2,
    kv_s, kt_s, dk_s, dv_s, dq_s,
):
    z, c = idx[0], idx[1]
    rows = qd.shape[0]
    nz, per, _ = kv_s.shape
    keys = 4 * per
    place_keys(z, own, lo1, hi1, lo2, hi2, kv_s, nz)
    live = z // 4
    dk_s[...] = jnp.zeros(dk_s.shape, F32)
    dv_s[...] = jnp.zeros(dv_s.shape, F32)

    def flip(g, _):
        kt_s[g] = kv_s[pl.ds(4 * g, 4)][:, :, :D].reshape(keys, D).T
        return 0

    lax.fori_loop(0, live + 1, flip, 0)
    for h in range(G):
        ms = [st_all[i, pl.ds(h, 1), :] for i in range(4)]
        ls = [st_all[i, pl.ds(G + h, 1), :] for i in range(4)]
        ds = [st_all[i, pl.ds(2 * G + h, 1), :] for i in range(4)]
        top = functools.reduce(jnp.maximum, ms)
        w = [jnp.exp2((m - top) * C2) for m in ms]
        total = functools.reduce(jnp.add, [a * b for a, b in zip(w, ls)])
        inv = 1.0 / total
        delta = functools.reduce(jnp.add, [a * b for a, b in zip(w, ds)]) * inv
        lse2 = top * C2 + jnp.log2(total)
        m_own = st_own[pl.ds(h, 1), :]
        l_own = st_own[pl.ds(G + h, 1), :]
        share = jnp.exp2((m_own - top) * C2) * l_own * inv
        od_out[:, h * D : (h + 1) * D] = (o_in[h] * share).T.astype(BF)
        q = qd[:, h * D : (h + 1) * D]
        do = qd[:, (G + h) * D : (G + h + 1) * D]
        dq_s[...] = jnp.zeros(dq_s.shape, F32)

        def step(g, masked):
            kv = kv_s[pl.ds(4 * g, 4)]
            k = kv[:, :, :D].reshape(keys, D)
            v = kv[:, :, D:].reshape(keys, D)
            s = dot(k, q, NT)
            p = jnp.exp2(s * C2 - lse2)
            if masked:
                p = jnp.where(chunk_mask(z, c, g, keys, rows, per), p, 0.0)
            dv_s[g] += dot(p.astype(BF), do, NN)
            dp = dot(v, do, NT)
            dsc = (p * (dp - delta)).astype(BF)
            dk_s[g] += dot(dsc, q, NN)
            dq_s[...] += dot(kt_s[g], dsc, NN)

        def full(g, _):
            step(g, False)
            return 0

        lax.fori_loop(0, live, full, 0)
        step(live, True)
        od_out[:, (G + h) * D : (G + h + 1) * D] = (dq_s[...] * SCALE).T.astype(BF)

    for ref, offs in (
        (g_own, (0, -4, -8, -12)),
        (g_lo1, (-1, -5, -9, -13)),
        (g_hi1, (1, -3, -7, -11)),
        (g_lo2, (-6, -10)),
        (g_hi2, (2, -2)),
    ):
        for j, off in enumerate(offs):
            t = (z + (off + nz)) % nz
            g, i = t // 4, t % 4
            dk = dk_s[g, pl.ds(pl.multiple_of(i * per, per), per), :] * SCALE
            dv = dv_s[g, pl.ds(pl.multiple_of(i * per, per), per), :]
            ref[j] = jnp.concatenate([dk, dv], axis=1).astype(ref.dtype)


def attention_forward(idx, qd, parts):
    rows = qd.shape[0]
    nz, per = 16, parts[0].shape[1]
    vm = pl.BlockSpec(memory_space=pltpu.VMEM)
    return pl.pallas_call(
        fwd_kernel,
        out_shape=(
            jax.ShapeDtypeStruct((G, D, rows), F32),
            jax.ShapeDtypeStruct((16, rows), F32),
        ),
        in_specs=[pl.BlockSpec(memory_space=pltpu.SMEM)] + [vm] * 6,
        out_specs=(vm, vm),
        scratch_shapes=[
            pltpu.VMEM((nz, per, 2 * D), BF),
            pltpu.VMEM((nz // 4, D, 4 * per), BF),
            pltpu.VMEM((D, rows), F32),
            pltpu.VMEM((1, rows), F32),
            pltpu.VMEM((1, rows), F32),
        ],
        compiler_params=pltpu.CompilerParams(vmem_limit_bytes=40 << 20),
        name="attn_fwd",
    )(idx, qd, *parts)


def attention_backward(idx, qd, parts, o, st, st_all):
    rows = qd.shape[0]
    nz, per = 16, parts[0].shape[1]
    vm = pl.BlockSpec(memory_space=pltpu.VMEM)
    own, lo1, hi1, lo2, hi2 = parts
    return pl.pallas_call(
        bwd_kernel,
        out_shape=(
            jax.ShapeDtypeStruct((rows, 2 * G * D), BF),
            jax.ShapeDtypeStruct(own.shape, F32),
            jax.ShapeDtypeStruct(lo1.shape, BF),
            jax.ShapeDtypeStruct(hi1.shape, BF),
            jax.ShapeDtypeStruct(lo2.shape, BF),
            jax.ShapeDtypeStruct(hi2.shape, BF),
        ),
        in_specs=[pl.BlockSpec(memory_space=pltpu.SMEM)] + [vm] * 9,
        out_specs=(vm,) * 6,
        scratch_shapes=[
            pltpu.VMEM((nz, per, 2 * D), BF),
            pltpu.VMEM((nz // 4, D, 4 * per), BF),
            pltpu.VMEM((nz // 4, 4 * per, D), F32),
            pltpu.VMEM((nz // 4, 4 * per, D), F32),
            pltpu.VMEM((D, rows), F32),
        ],
        compiler_params=pltpu.CompilerParams(vmem_limit_bytes=48 << 20),
        name="attn_bwd",
    )(idx, qd, own, lo1, hi1, lo2, hi2, o, st, st_all)


def shift(x, by):
    n = lax.axis_size("z")
    return lax.ppermute(x, "z", [(i, (i + by) % n) for i in range(n)])


def shards(query, keys, values, grad):
    tok = query.shape[0]
    tp = lax.axis_size("tp")
    cols = lax.axis_size("xl") * lax.axis_size("core")
    z = lax.axis_index("z")
    c = lax.axis_index("xl") * lax.axis_size("core") + lax.axis_index("core")
    idx = jnp.stack([z, c]).astype(jnp.int32)
    hw = G * D

    kv = jnp.concatenate([keys.reshape(tok, tp, D), values.reshape(tok, tp, D)], axis=2)
    kv = lax.all_to_all(kv.transpose(1, 0, 2), "tp", split_axis=0, concat_axis=0, tiled=True)
    kv = kv.reshape(tp * tok, 2 * D)
    qd = jnp.concatenate([query.reshape(tok, tp, hw), grad.reshape(tok, tp, hw)], axis=2)
    qd = jnp.broadcast_to(qd.transpose(1, 0, 2)[None], (cols, tp, tok, 2 * hw))
    qd = qd.reshape(cols * tp, tok, 2 * hw)
    qd = lax.all_to_all(qd, PLANE, split_axis=0, concat_axis=0, tiled=True)
    qd = qd.reshape(cols * tp * tok, 2 * hw)

    own = jnp.stack([kv, shift(kv, 4), shift(kv, 8), shift(kv, -4)])
    parts = (own, shift(own, 1), shift(own, -1), shift(own[1:3], 2), shift(own[:2], -2))

    o, st = attention_forward(idx, qd, parts)
    st_all = lax.all_gather(st, COLS, axis=0, tiled=False)
    od, g_own, g_lo1, g_hi1, g_lo2, g_hi2 = attention_backward(idx, qd, parts, o, st, st_all)

    od = lax.all_to_all(
        od.reshape(cols * tp, tok, 2 * hw), PLANE, split_axis=0, concat_axis=0, tiled=True
    )
    od = jnp.sum(od.reshape(cols, tp, tok, 2 * hw).astype(F32), axis=0).astype(BF)

    up1, down1 = shift(g_hi1, 1).astype(F32), shift(g_lo1, -1).astype(F32)
    up2, down2 = shift(g_hi2, 2).astype(F32), shift(g_lo2, -2).astype(F32)
    four = g_own + up1 + down1
    four = four + jnp.concatenate([up2, jnp.zeros_like(up2)])
    four = four + jnp.pad(down2, ((1, 1), (0, 0), (0, 0)))
    send = four[1:].astype(BF)
    gkv = four[0] + shift(send[0], -4).astype(F32)
    gkv = gkv + shift(send[1], 8).astype(F32) + shift(send[2], 4).astype(F32)
    gkv = gkv.astype(BF).reshape(tp, tok, 2 * D)
    gkv = lax.all_to_all(gkv, "tp", split_axis=0, concat_axis=0, tiled=True)

    def to_tokens(x):
        return x.transpose(1, 0, 2).reshape(tok, -1)

    return (
        to_tokens(od[:, :, :hw]),
        to_tokens(od[:, :, hw:]),
        to_tokens(gkv[:, :, :D]),
        to_tokens(gkv[:, :, D:]),
    )


def solution(mesh):
    tp = mesh.shape["tp"]
    inner = Mesh(mesh.devices.reshape(16, 2, 2, tp), ("z", "xl", "core", "tp"))
    spec = P(("z", "xl", "core", "tp"), None)
    return jax.shard_map(
        shards, mesh=inner, in_specs=(spec,) * 4, out_specs=(spec,) * 4, check_vma=False
    )
```

time: 855 us -> 194 us (0.23)
  the two profiles are of different devices: /device:TPU:384 before, /device:TPU:1 now
where the time goes in v1:
time: 194 us; the launch traced here: 193 us
  starting transfers between devices  117 us (60%)
  waiting for transfers between devices  37.1 us (19%)
  blocking collectives  20.7 us (11%)
  Pallas kernels  9.87 us (5%)
  local copies, waits for them, and re-layouts  6.38 us (3%)
    ppermute x14, starting transfers between devices, shift(): return lax.ppermute(x, 'z', [(i, (i + by) % n) for i in range(n)])  93.8 us
    ppermute x14, waiting for transfers between devices, shift(): return lax.ppermute(x, 'z', [(i, (i + by) % n) for i in range(n)])  16.7 us
    all_to_all x1, waiting for transfers between devices, shards(): lax.all_to_all(od.reshape(cols * tp, tok, 2 * hw), PLANE, split_axis=0, c...  14.8 us
    all_to_all x1, blocking collectives, shards(): gkv = lax.all_to_all(gkv, 'tp', split_axis=0, concat_axis=0, tiled=True)  13.2 us
    all_to_all x1, starting transfers between devices, shards(): lax.all_to_all(od.reshape(cols * tp, tok, 2 * hw), PLANE, split_axis=0, c...  8.01 us
    all_gather x1, blocking collectives, shards(): st_all = lax.all_gather(st, COLS, axis=0, tiled=False)  7.53 us
    all_to_all x1, starting transfers between devices, shards(): lax.all_to_all(kv.transpose(1, 0, 2), 'tp', split_axis=0, concat_axis=0,...  7.47 us
    all_to_all x1, starting transfers between devices, shards(): qd = lax.all_to_all(qd, PLANE, split_axis=0, concat_axis=0, tiled=True)  7.44 us
  transfers between devices with their start and end apart: 17, of which 8 were waited for; matrix products, arithmetic and copies ran while one was open for 1% of the time, Pallas kernels for 0%

profile of v1, /device:TPU:1, one launch (start us, length us, event | category | flops | bytes accessed | tf_op | source)
XLA Modules:
  0.0 192.8 jit_solution(7285183392543629323)
XLA Ops:
  0.6 0.0 copy-start
  0.6 0.7 copy-done
  1.4 0.8 copy_bitcast_fusion.2
  2.2 0.0 copy-start.1
  2.2 0.6 maximum_bitcast_fusion.1
  2.8 7.5 %all-to-all-start.1 = ((bf16[8,16,256]{2,1,0:T(8,128)(2,1)}), bf16[8,16,256]{2,1,0:T(8,128)(2,1)S(1)}, u32[]{:S(2)}, u32[]{:S(2)}) async-start(bf16[8,16,256]{2,1,0:T(8,128)(2,1)} %maximum_bitcast_fusion.1), calls=%async_computation.1 | async-start | bytes 131072 | tf_op jit(solution)/shard_map/all_to_all | solution.py:238
  10.3 0.0 copy-done.1
  10.3 0.0 copy-start.2
  10.4 0.8 copy-done.2
  11.3 0.2 copy.18
  11.4 5.6 %all-to-all-done.1 = bf16[8,16,256]{2,1,0:T(8,128)(2,1)S(1)} async-done(((bf16[8,16,256]{2,1,0:T(8,128)(2,1)}), bf16[8,16,256]{2,1,0:T(8,128)(2,1)S(1)}, u32[]{:S(2)}, u32[]{:S(2)}) %all-to-all-start.1) | async-done | bytes 65568 | tf_op jit(solution)/shard_map/all_to_all | solution.py:238
  17.0 1.1 broadcast_in_dim.2
  18.1 7.4 %all-to-all-start = ((bf16[32,16,1024]{2,1,0:T(8,128)(2,1)}), bf16[32,16,1024]{2,1,0:T(8,128)(2,1)S(1)}, u32[]{:S(2)}, u32[]{:S(2)}) async-start(bf16[32,16,1024]{2,1,0:T(8,128)(2,1)} %bitcast.3), calls=%async_computation | async-start | bytes 2097152 | tf_op jit(solution)/shard_map/all_to_all | solution.py:243
  25.6 10.8 %collective-permute-start.2 = (bf16[128,256]{1,0:T(8,128)(2,1)S(1)}, bf16[128,256]{1,0:T(8,128)(2,1)S(1)}, u32[]{:S(2)}, u32[]{:S(2)}) collective-permute-start(bf16[128,256]{1,0:T(8,128)(2,1)S(1)} %bitcast.71), channel_id=1, source_target_pairs={{0,384},{32,416},{64,448},{96,480},{128,0},{160,32},{192,64},{224,... | collective-permute-start | bytes 196616 | tf_op jit(solution)/shard_map/ppermute | solution.py:225
  36.3 4.9 %collective-permute-start.1 = (bf16[128,256]{1,0:T(8,128)(2,1)S(1)}, bf16[128,256]{1,0:T(8,128)(2,1)S(1)}, u32[]{:S(2)}, u32[]{:S(2)}) collective-permute-start(bf16[128,256]{1,0:T(8,128)(2,1)S(1)} %bitcast.72), channel_id=1, source_target_pairs={{0,256},{32,288},{64,320},{96,352},{128,384},{160,416},{192,448},{... | collective-permute-start | bytes 196616 | tf_op jit(solution)/shard_map/ppermute | solution.py:225
  41.3 7.3 %collective-permute-start = (bf16[128,256]{1,0:T(8,128)(2,1)S(1)}, bf16[128,256]{1,0:T(8,128)(2,1)S(1)}, u32[]{:S(2)}, u32[]{:S(2)}) collective-permute-start(bf16[128,256]{1,0:T(8,128)(2,1)S(1)} %bitcast.73), channel_id=1, source_target_pairs={{0,128},{32,160},{64,192},{96,224},{128,256},{160,288},{192,320},{... | collective-permute-start | bytes 196616 | tf_op jit(solution)/shard_map/ppermute | solution.py:225
  48.5 0.0 collective-permute-done.2
  48.5 1.8 collective-permute-done.1
  50.4 3.7 %collective-permute-done = bf16[128,256]{1,0:T(8,128)(2,1)S(1)} collective-permute-done((bf16[128,256]{1,0:T(8,128)(2,1)S(1)}, bf16[128,256]{1,0:T(8,128)(2,1)S(1)}, u32[]{:S(2)}, u32[]{:S(2)}) %collective-permute-start) | collective-permute-done | bytes 65568 | tf_op jit(solution)/shard_map/ppermute | solution.py:225
  54.1 8.2 %collective-permute-start.4 = (bf16[4,128,256]{2,1,0:T(8,128)(2,1)S(1)}, bf16[4,128,256]{2,1,0:T(8,128)(2,1)S(1)}, u32[]{:S(2)}, u32[]{:S(2)}) collective-permute-start(bf16[4,128,256]{2,1,0:T(8,128)(2,1)S(1)} %pad_maximum_fusion.own), channel_id=1, source_target_pairs={{0,480},{32,0},{64,32},{96,64},{128,96},{160,128},{192,160},{224,1... | collective-permute-start | bytes 786440 | tf_op jit(solution)/shard_map/ppermute | solution.py:225
  62.3 1.9 collective-permute-start.3
  64.3 3.1 %collective-permute-start.6 = (bf16[2,128,256]{2,1,0:T(8,128)(2,1)S(1)}, bf16[2,128,256]{2,1,0:T(8,128)(2,1)S(1)}, u32[]{:S(2)}, u32[]{:S(2)}) collective-permute-start(bf16[2,128,256]{2,1,0:T(8,128)(2,1)S(1)} %get-tuple-element.29), channel_id=1, source_target_pairs={{0,448},{32,480},{64,0},{96,32},{128,64},{160,96},{192,128},{224,1... | collective-permute-start | bytes 393224 | tf_op jit(solution)/shard_map/ppermute | solution.py:225
  67.4 3.1 %collective-permute-start.5 = (bf16[2,128,256]{2,1,0:T(8,128)(2,1)S(1)}, bf16[2,128,256]{2,1,0:T(8,128)(2,1)S(1)}, u32[]{:S(2)}, u32[]{:S(2)}) collective-permute-start(bf16[2,128,256]{2,1,0:T(8,128)(2,1)S(1)} %get-tuple-element.30), channel_id=1, source_target_pairs={{0,64},{32,96},{64,128},{96,160},{128,192},{160,224},{192,256},{22... | collective-permute-start | bytes 393224 | tf_op jit(solution)/shard_map/ppermute | solution.py:225
  70.5 0.1 pad_add_fusion.idx
  70.6 3.5 %collective-permute-done.6.hi2 = bf16[2,128,256]{2,1,0:T(8,128)(2,1)S(1)} collective-permute-done((bf16[2,128,256]{2,1,0:T(8,128)(2,1)S(1)}, bf16[2,128,256]{2,1,0:T(8,128)(2,1)S(1)}, u32[]{:S(2)}, u32[]{:S(2)}) %collective-permute-start.6) | collective-permute-done | bytes 131104 | tf_op jit(solution)/shard_map/ppermute | solution.py:225
  74.1 1.1 collective-permute-done.5.lo2
  75.2 0.0 collective-permute-done.4.hi1
  75.2 0.0 collective-permute-done.3.lo1
  75.2 0.0 all-to-all-done
  75.2 3.8 %attn_fwd.1 = (f32[4,128,512]{2,1,0:T(8,128)S(1)}, f32[16,512]{1,0:T(8,128)S(1)}) custom-call(s32[2]{0:T(128)S(1)} %pad_add_fusion.idx, bf16[512,1024]{1,0:T(8,128)(2,1)S(1)} %bitcast.67, bf16[4,128,256]{2,1,0:T(8,128)(2,1)S(1)} %pad_maximum_fusion.own, bf16[4,128,256]{2,1,0:T(8,128)(2,1)S(1)} %collective-permute-done.3.lo1, ...), custom_call_target="tpu_custom_call" | custom-call | tf_op jit(solution)/shard_map/attn_fwd/pallas_call | solution.py:174
  79.0 7.5 %all-gather = f32[64,512]{1,0:T(8,128)S(1)} all-gather(f32[16,512]{1,0:T(8,128)S(1)} %get-tuple-element.13.st_own), channel_id=2, replica_groups=mesh['z'=16,'xl'=2,'core'=2,'tp'=8] {'xl','core'}, dimensions={0}, use_global_device_ids=true | all-gather | bytes 163840 | tf_op jit(solution)/shard_map/all_gather | solution.py:250
  86.6 6.1 %attn_bwd.1 = (bf16[512,1024]{1,0:T(8,128)(2,1)}, f32[4,128,256]{2,1,0:T(8,128)S(1)}, bf16[4,128,256]{2,1,0:T(8,128)(2,1)S(1)}, bf16[4,128,256]{2,1,0:T(8,128)(2...) custom-call(s32[2]{0:T(128)S(1)} %pad_add_fusion.idx, bf16[512,1024]{1,0:T(8,128)(2,1)S(1)} %bitcast.68, ...), custom_call_target="tpu_custom_call" | custom-call | tf_op jit(solution)/shard_map/attn_bwd/pallas_call | solution.py:199
  92.7 5.8 %collective-permute-start.7 = (bf16[4,128,256]{2,1,0:T(8,128)(2,1)S(1)}, bf16[4,128,256]{2,1,0:T(8,128)(2,1)S(1)}, u32[]{:S(2)}, u32[]{:S(2)}) collective-permute-start(bf16[4,128,256]{2,1,0:T(8,128)(2,1)S(1)} %get-tuple-element.16), channel_id=1, source_target_pairs={{0,32},{32,64},{64,96},{96,128},{128,160},{160,192},{192,224},{224... | collective-permute-start | bytes 786440 | tf_op jit(solution)/shard_map/ppermute | solution.py:225
  98.4 19.7 %collective-permute-start.8 = (bf16[4,128,256]{2,1,0:T(8,128)(2,1)S(1)}, bf16[4,128,256]{2,1,0:T(8,128)(2,1)S(1)}, u32[]{:S(2)}, u32[]{:S(2)}) collective-permute-start(bf16[4,128,256]{2,1,0:T(8,128)(2,1)S(1)} %get-tuple-element.17), channel_id=1, source_target_pairs={{0,480},{32,0},{64,32},{96,64},{128,96},{160,128},{192,160},{224,1... | collective-permute-start | bytes 786440 | tf_op jit(solution)/shard_map/ppermute | solution.py:225
  118.1 1.9 collective-permute-start.9
  120.1 5.5 %collective-permute-start.10 = (bf16[2,128,256]{2,1,0:T(8,128)(2,1)S(1)}, bf16[2,128,256]{2,1,0:T(8,128)(2,1)S(1)}, u32[]{:S(2)}, u32[]{:S(2)}) collective-permute-start(bf16[2,128,256]{2,1,0:T(8,128)(2,1)S(1)} %get-tuple-element.19), channel_id=1, source_target_pairs={{0,448},{32,480},{64,0},{96,32},{128,64},{160,96},{192,128},{224,1... | collective-permute-start | bytes 393224 | tf_op jit(solution)/shard_map/ppermute | solution.py:225
  125.5 2.8 %collective-permute-done.9 = bf16[2,128,256]{2,1,0:T(8,128)(2,1)S(1)} collective-permute-done((bf16[2,128,256]{2,1,0:T(8,128)(2,1)S(1)}, bf16[2,128,256]{2,1,0:T(8,128)(2,1)S(1)}, u32[]{:S(2)}, u32[]{:S(2)}) %collective-permute-start.9) | collective-permute-done | bytes 131104 | tf_op jit(solution)/shard_map/ppermute | solution.py:225
  128.3 0.0 collective-permute-done.10
  128.3 0.0 collective-permute-done.7
  128.3 0.0 collective-permute-done.8
  128.3 0.1 fusion.4
  128.5 9.6 %collective-permute-start.11 = (bf16[128,256]{1,0:T(8,128)(2,1)S(1)}, bf16[128,256]{1,0:T(8,128)(2,1)S(1)}, u32[]{:S(2)}, u32[]{:S(2)}) collective-permute-start(bf16[128,256]{1,0:T(8,128)(2,1)S(1)} %get-tuple-element.22), channel_id=1, source_target_pairs={{0,384},{32,416},{64,448},{96,480},{128,0},{160,32},{192,64},{224,... | collective-permute-start | bytes 196616 | tf_op jit(solution)/shard_map/ppermute | solution.py:225
  138.1 1.9 collective-permute-start.13
  140.0 10.2 %collective-permute-start.12 = (bf16[128,256]{1,0:T(8,128)(2,1)S(1)}, bf16[128,256]{1,0:T(8,128)(2,1)S(1)}, u32[]{:S(2)}, u32[]{:S(2)}) collective-permute-start(bf16[128,256]{1,0:T(8,128)(2,1)S(1)} %get-tuple-element.24), channel_id=1, source_target_pairs={{0,256},{32,288},{64,320},{96,352},{128,384},{160,416},{192,448},{... | collective-permute-start | bytes 196616 | tf_op jit(solution)/shard_map/ppermute | solution.py:225
  150.2 0.0 collective-permute-done.11
  150.2 0.0 collective-permute-done.13
  150.2 3.8 %collective-permute-done.12 = bf16[128,256]{1,0:T(8,128)(2,1)S(1)} collective-permute-done((bf16[128,256]{1,0:T(8,128)(2,1)S(1)}, bf16[128,256]{1,0:T(8,128)(2,1)S(1)}, u32[]{:S(2)}, u32[]{:S(2)}) %collective-permute-start.12) | collective-permute-done | bytes 65568 | tf_op jit(solution)/shard_map/ppermute | solution.py:225
  154.0 13.2 %all_to_all.20 = bf16[8,16,256]{2,1,0:T(8,128)(2,1)S(1)} all-to-all(bf16[8,16,256]{2,1,0:T(8,128)(2,1)S(1)} %bitcast.78), channel_id=1, replica_groups=mesh['z'=16,'xl'=2,'core'=2,'tp'=8] {'tp'}, dimensions={0} | all-to-all | bytes 131072 | tf_op jit(solution)/shard_map/all_to_all | solution.py:267
  167.2 8.0 %all-to-all-start.2 = ((bf16[32,16,1024]{2,1,0:T(8,128)(2,1)}), bf16[32,16,1024]{2,1,0:T(8,128)(2,1)S(1)}, u32[]{:S(2)}, u32[]{:S(2)}) async-start(bf16[32,16,1024]{2,1,0:T(8,128)(2,1)} %bitcast.12), calls=%async_computation.2 | async-start | bytes 2097152 | tf_op jit(solution)/shard_map/all_to_all | solution.py:253
  175.2 0.6 copy.37
  175.9 0.6 copy.38
  176.5 14.8 %all-to-all-done.2 = bf16[32,16,1024]{2,1,0:T(8,128)(2,1)S(1)} async-done(((bf16[32,16,1024]{2,1,0:T(8,128)(2,1)}), bf16[32,16,1024]{2,1,0:T(8,128)(2,1)S(1)}, u32[]{:S(2)}, u32[]{:S(2)}) %all-to-all-start.2) | async-done | bytes 1048608 | tf_op jit(solution)/shard_map/all_to_all | solution.py:253
  191.3 0.2 reduce_sum.12
  191.5 0.7 copy.28
  192.2 0.7 copy.27
  (9 shorter events, 0.3 us)
Async XLA Ops:
  0.6 0.8 copy-start
  2.2 8.1 %copy-start.1 = (bf16[16,4096]{1,0:T(8,128)(2,1)S(1)}, bf16[16,4096]{1,0:T(8,128)(2,1)}, u32[]{:S(2)}) copy-start(bf16[16,4096]{1,0:T(8,128)(2,1)} %param.4) | copy-start | bytes 393220
  2.8 14.2 %all-to-all-start.1 = ((bf16[8,16,256]{2,1,0:T(8,128)(2,1)}), bf16[8,16,256]{2,1,0:T(8,128)(2,1)S(1)}, u32[]{:S(2)}, u32[]{:S(2)}) async-start(bf16[8,16,256]{2,1,0:T(8,128)(2,1)} %maximum_bitcast_fusion.1), calls=%async_computation.1 | async-start | bytes 131072 | tf_op jit(solution)/shard_map/all_to_all | solution.py:238
  10.3 0.9 copy-start.2
  18.1 57.1 %all-to-all-start = ((bf16[32,16,1024]{2,1,0:T(8,128)(2,1)}), bf16[32,16,1024]{2,1,0:T(8,128)(2,1)S(1)}, u32[]{:S(2)}, u32[]{:S(2)}) async-start(bf16[32,16,1024]{2,1,0:T(8,128)(2,1)} %bitcast.3), calls=%async_computation | async-start | bytes 2097152 | tf_op jit(solution)/shard_map/all_to_all | solution.py:243
  25.6 23.0 %collective-permute-start.2 = (bf16[128,256]{1,0:T(8,128)(2,1)S(1)}, bf16[128,256]{1,0:T(8,128)(2,1)S(1)}, u32[]{:S(2)}, u32[]{:S(2)}) collective-permute-start(bf16[128,256]{1,0:T(8,128)(2,1)S(1)} %bitcast.71), channel_id=1, source_target_pairs={{0,384},{32,416},{64,448},{96,480},{128,0},{160,32},{192,64},{224,... | collective-permute-start | bytes 196616 | tf_op jit(solution)/shard_map/ppermute | solution.py:225
  36.3 14.0 %collective-permute-start.1 = (bf16[128,256]{1,0:T(8,128)(2,1)S(1)}, bf16[128,256]{1,0:T(8,128)(2,1)S(1)}, u32[]{:S(2)}, u32[]{:S(2)}) collective-permute-start(bf16[128,256]{1,0:T(8,128)(2,1)S(1)} %bitcast.72), channel_id=1, source_target_pairs={{0,256},{32,288},{64,320},{96,352},{128,384},{160,416},{192,448},{... | collective-permute-start | bytes 196616 | tf_op jit(solution)/shard_map/ppermute | solution.py:225
  41.3 12.8 %collective-permute-start = (bf16[128,256]{1,0:T(8,128)(2,1)S(1)}, bf16[128,256]{1,0:T(8,128)(2,1)S(1)}, u32[]{:S(2)}, u32[]{:S(2)}) collective-permute-start(bf16[128,256]{1,0:T(8,128)(2,1)S(1)} %bitcast.73), channel_id=1, source_target_pairs={{0,128},{32,160},{64,192},{96,224},{128,256},{160,288},{192,320},{... | collective-permute-start | bytes 196616 | tf_op jit(solution)/shard_map/ppermute | solution.py:225
  54.1 21.2 %collective-permute-start.4 = (bf16[4,128,256]{2,1,0:T(8,128)(2,1)S(1)}, bf16[4,128,256]{2,1,0:T(8,128)(2,1)S(1)}, u32[]{:S(2)}, u32[]{:S(2)}) collective-permute-start(bf16[4,128,256]{2,1,0:T(8,128)(2,1)S(1)} %pad_maximum_fusion.own), channel_id=1, source_target_pairs={{0,480},{32,0},{64,32},{96,64},{128,96},{160,128},{192,160},{224,1... | collective-permute-start | bytes 786440 | tf_op jit(solution)/shard_map/ppermute | solution.py:225
  62.3 12.9 %collective-permute-start.3 = (bf16[4,128,256]{2,1,0:T(8,128)(2,1)S(1)}, bf16[4,128,256]{2,1,0:T(8,128)(2,1)S(1)}, u32[]{:S(2)}, u32[]{:S(2)}) collective-permute-start(bf16[4,128,256]{2,1,0:T(8,128)(2,1)S(1)} %pad_maximum_fusion.own), channel_id=1, source_target_pairs={{0,32},{32,64},{64,96},{96,128},{128,160},{160,192},{192,224},{224... | collective-permute-start | bytes 786440 | tf_op jit(solution)/shard_map/ppermute | solution.py:225
  64.3 9.8 %collective-permute-start.6 = (bf16[2,128,256]{2,1,0:T(8,128)(2,1)S(1)}, bf16[2,128,256]{2,1,0:T(8,128)(2,1)S(1)}, u32[]{:S(2)}, u32[]{:S(2)}) collective-permute-start(bf16[2,128,256]{2,1,0:T(8,128)(2,1)S(1)} %get-tuple-element.29), channel_id=1, source_target_pairs={{0,448},{32,480},{64,0},{96,32},{128,64},{160,96},{192,128},{224,1... | collective-permute-start | bytes 393224 | tf_op jit(solution)/shard_map/ppermute | solution.py:225
  67.4 7.8 %collective-permute-start.5 = (bf16[2,128,256]{2,1,0:T(8,128)(2,1)S(1)}, bf16[2,128,256]{2,1,0:T(8,128)(2,1)S(1)}, u32[]{:S(2)}, u32[]{:S(2)}) collective-permute-start(bf16[2,128,256]{2,1,0:T(8,128)(2,1)S(1)} %get-tuple-element.30), channel_id=1, source_target_pairs={{0,64},{32,96},{64,128},{96,160},{128,192},{160,224},{192,256},{22... | collective-permute-start | bytes 393224 | tf_op jit(solution)/shard_map/ppermute | solution.py:225
  92.7 35.6 %collective-permute-start.7 = (bf16[4,128,256]{2,1,0:T(8,128)(2,1)S(1)}, bf16[4,128,256]{2,1,0:T(8,128)(2,1)S(1)}, u32[]{:S(2)}, u32[]{:S(2)}) collective-permute-start(bf16[4,128,256]{2,1,0:T(8,128)(2,1)S(1)} %get-tuple-element.16), channel_id=1, source_target_pairs={{0,32},{32,64},{64,96},{96,128},{128,160},{160,192},{192,224},{224... | collective-permute-start | bytes 786440 | tf_op jit(solution)/shard_map/ppermute | solution.py:225
  98.4 29.9 %collective-permute-start.8 = (bf16[4,128,256]{2,1,0:T(8,128)(2,1)S(1)}, bf16[4,128,256]{2,1,0:T(8,128)(2,1)S(1)}, u32[]{:S(2)}, u32[]{:S(2)}) collective-permute-start(bf16[4,128,256]{2,1,0:T(8,128)(2,1)S(1)} %get-tuple-element.17), channel_id=1, source_target_pairs={{0,480},{32,0},{64,32},{96,64},{128,96},{160,128},{192,160},{224,1... | collective-permute-start | bytes 786440 | tf_op jit(solution)/shard_map/ppermute | solution.py:225
  118.1 10.2 %collective-permute-start.9 = (bf16[2,128,256]{2,1,0:T(8,128)(2,1)S(1)}, bf16[2,128,256]{2,1,0:T(8,128)(2,1)S(1)}, u32[]{:S(2)}, u32[]{:S(2)}) collective-permute-start(bf16[2,128,256]{2,1,0:T(8,128)(2,1)S(1)} %get-tuple-element.18), channel_id=1, source_target_pairs={{0,64},{32,96},{64,128},{96,160},{128,192},{160,224},{192,256},{22... | collective-permute-start | bytes 393224 | tf_op jit(solution)/shard_map/ppermute | solution.py:225
  120.1 8.2 %collective-permute-start.10 = (bf16[2,128,256]{2,1,0:T(8,128)(2,1)S(1)}, bf16[2,128,256]{2,1,0:T(8,128)(2,1)S(1)}, u32[]{:S(2)}, u32[]{:S(2)}) collective-permute-start(bf16[2,128,256]{2,1,0:T(8,128)(2,1)S(1)} %get-tuple-element.19), channel_id=1, source_target_pairs={{0,448},{32,480},{64,0},{96,32},{128,64},{160,96},{192,128},{224,1... | collective-permute-start | bytes 393224 | tf_op jit(solution)/shard_map/ppermute | solution.py:225
  128.5 21.7 %collective-permute-start.11 = (bf16[128,256]{1,0:T(8,128)(2,1)S(1)}, bf16[128,256]{1,0:T(8,128)(2,1)S(1)}, u32[]{:S(2)}, u32[]{:S(2)}) collective-permute-start(bf16[128,256]{1,0:T(8,128)(2,1)S(1)} %get-tuple-element.22), channel_id=1, source_target_pairs={{0,384},{32,416},{64,448},{96,480},{128,0},{160,32},{192,64},{224,... | collective-permute-start | bytes 196616 | tf_op jit(solution)/shard_map/ppermute | solution.py:225
  138.1 12.1 %collective-permute-start.13 = (bf16[128,256]{1,0:T(8,128)(2,1)S(1)}, bf16[128,256]{1,0:T(8,128)(2,1)S(1)}, u32[]{:S(2)}, u32[]{:S(2)}) collective-permute-start(bf16[128,256]{1,0:T(8,128)(2,1)S(1)} %get-tuple-element.23), channel_id=1, source_target_pairs={{0,128},{32,160},{64,192},{96,224},{128,256},{160,288},{192,320},{... | collective-permute-start | bytes 196616 | tf_op jit(solution)/shard_map/ppermute | solution.py:225
  140.0 14.0 %collective-permute-start.12 = (bf16[128,256]{1,0:T(8,128)(2,1)S(1)}, bf16[128,256]{1,0:T(8,128)(2,1)S(1)}, u32[]{:S(2)}, u32[]{:S(2)}) collective-permute-start(bf16[128,256]{1,0:T(8,128)(2,1)S(1)} %get-tuple-element.24), channel_id=1, source_target_pairs={{0,256},{32,288},{64,320},{96,352},{128,384},{160,416},{192,448},{... | collective-permute-start | bytes 196616 | tf_op jit(solution)/shard_map/ppermute | solution.py:225
  167.2 24.1 %all-to-all-start.2 = ((bf16[32,16,1024]{2,1,0:T(8,128)(2,1)}), bf16[32,16,1024]{2,1,0:T(8,128)(2,1)S(1)}, u32[]{:S(2)}, u32[]{:S(2)}) async-start(bf16[32,16,1024]{2,1,0:T(8,128)(2,1)} %bitcast.12), calls=%async_computation.2 | async-start | bytes 2097152 | tf_op jit(solution)/shard_map/all_to_all | solution.py:253

commit v2 on v1

v2 whole, which is shorter than its diff:
```python
import functools

import jax
import jax.numpy as jnp
from jax import lax
from jax.experimental import pallas as pl
from jax.experimental.pallas import tpu as pltpu
from jax.sharding import Mesh, PartitionSpec as P

D = 128
G = 4
SCALE = D ** (-0.5)
LOG2E = 1.4426950408889634
C2 = SCALE * LOG2E
NEG = -1e30
SIDE = ("xl", "tp")
COLS = ("xl", "core")
NT = (((1,), (1,)), ((), ()))
NN = (((1,), (0,)), ((), ()))
BF = jnp.bfloat16
F32 = jnp.float32


def dot(a, b, dims):
    return lax.dot_general(a, b, dims, preferred_element_type=F32)


def place_keys(z, own, lo1, hi1, lo2, hi2, kv_s, nz):
    for ref, offs in (
        (own, (0, -4, -8, -12)),
        (lo1, (-1, -5, -9, -13)),
        (hi1, (1, -3, -7, -11)),
        (lo2, (-6, -10)),
        (hi2, (2, -2)),
    ):
        for j, off in enumerate(offs):
            kv_s[(z + (off + nz)) % nz] = ref[j]


def chunk_mask(idx, g, keys, rows, per, tok):
    z, xl, core = idx[0], idx[1], idx[2]
    share = tok // 2
    k = lax.broadcasted_iota(jnp.int32, (keys, 1), 0)
    i = k % per
    src = i // share
    tp = per // tok
    key_tok = ((src // tp) * 2 + core) * per + (src % tp) * tok + xl * share + i % share
    key_pos = (g * 4 + k // per) * rows + key_tok
    r = lax.broadcasted_iota(jnp.int32, (1, rows), 1)
    half = rows // 2
    row_core = jnp.where(r < half, core, 1 - core)
    row_tok = (((r % half) // per) * 2 + row_core) * per + r % per
    return key_pos <= z * rows + row_tok


def both(a, b, lo):
    return jnp.concatenate([a[:, lo : lo + D], b[:, lo : lo + D]], axis=0)


def put_row(ref, row, x, core):
    half = x.shape[1] // 2
    ref[row : row + 1, pl.ds(pl.multiple_of(core * half, half), half)] = x[:, :half]
    ref[row : row + 1, pl.ds(pl.multiple_of((1 - core) * half, half), half)] = x[:, half:]


def get_row(ref, row, core):
    half = ref.shape[-1] // 2
    lo = ref[row : row + 1, pl.ds(pl.multiple_of(core * half, half), half)]
    hi = ref[row : row + 1, pl.ds(pl.multiple_of((1 - core) * half, half), half)]
    return jnp.concatenate([lo, hi], axis=1)


def fwd_kernel(
    tok, idx, qa, qb, own, lo1, hi1, lo2, hi2, o_out, st_out, kv_s, vt_s, acc, m_s, l_s
):
    z, core = idx[0], idx[2]
    rows = 2 * qa.shape[0]
    nz, per, _ = kv_s.shape
    keys = 4 * per
    place_keys(z, own, lo1, hi1, lo2, hi2, kv_s, nz)
    live = z // 4

    def flip(g, _):
        v = kv_s[pl.ds(4 * g, 4)][:, :, D:].reshape(keys, D)
        vt_s[g] = v.T
        return 0

    lax.fori_loop(0, live + 1, flip, 0)
    st_out[...] = jnp.zeros(st_out.shape, F32)
    for h in range(G):
        q = both(qa, qb, h * D)
        m_s[...] = jnp.full(m_s.shape, NEG, F32)
        l_s[...] = jnp.zeros(l_s.shape, F32)
        acc[...] = jnp.zeros(acc.shape, F32)

        def step(g, masked):
            k = kv_s[pl.ds(4 * g, 4)][:, :, :D].reshape(keys, D)
            s = dot(k, q, NT)
            if masked:
                s = jnp.where(chunk_mask(idx, g, keys, rows, per, tok), s, NEG)
            m_old = m_s[...]
            m_new = jnp.maximum(m_old, jnp.max(s, axis=0, keepdims=True))
            p = jnp.exp2((s - m_new) * C2)
            alpha = jnp.exp2((m_old - m_new) * C2)
            m_s[...] = m_new
            l_s[...] = l_s[...] * alpha + jnp.sum(p, axis=0, keepdims=True)
            acc[...] = acc[...] * alpha + dot(vt_s[g], p.astype(BF), NN)

        def full(g, _):
            step(g, False)
            return 0

        lax.fori_loop(0, live, full, 0)
        step(live, True)
        l = l_s[...]
        o_t = acc[...]
        do_t = both(qa, qb, (G + h) * D).T.astype(F32)
        put_row(st_out, h, m_s[...], core)
        put_row(st_out, G + h, l, core)
        put_row(st_out, 2 * G + h, jnp.sum(do_t * o_t, axis=0, keepdims=True), core)
        o_out[h] = o_t * (1.0 / l)


def bwd_kernel(
    tok, idx, qa, qb, own, lo1, hi1, lo2, hi2, o_in, st_own, st_all,
    od_a, od_b, g_own, g_lo1, g_hi1, g_lo2, g_hi2,
    kv_s, kt_s, dk_s, dv_s, dq_s,
):
    z, core = idx[0], idx[2]
    half = qa.shape[0]
    rows = 2 * half
    nz, per, _ = kv_s.shape
    keys = 4 * per
    place_keys(z, own, lo1, hi1, lo2, hi2, kv_s, nz)
    live = z // 4
    dk_s[...] = jnp.zeros(dk_s.shape, F32)
    dv_s[...] = jnp.zeros(dv_s.shape, F32)

    def flip(g, _):
        kt_s[g] = kv_s[pl.ds(4 * g, 4)][:, :, :D].reshape(keys, D).T
        return 0

    lax.fori_loop(0, live + 1, flip, 0)
    for h in range(G):
        ms = [get_row(st_all.at[i], h, core) for i in range(4)]
        ls = [get_row(st_all.at[i], G + h, core) for i in range(4)]
        ds = [get_row(st_all.at[i], 2 * G + h, core) for i in range(4)]
        top = functools.reduce(jnp.maximum, ms)
        w = [jnp.exp2((m - top) * C2) for m in ms]
        total = functools.reduce(jnp.add, [a * b for a, b in zip(w, ls)])
        inv = 1.0 / total
        delta = functools.reduce(jnp.add, [a * b for a, b in zip(w, ds)]) * inv
        lse2 = top * C2 + jnp.log2(total)
        m_own = get_row(st_own, h, core)
        l_own = get_row(st_own, G + h, core)
        share = jnp.exp2((m_own - top) * C2) * l_own * inv
        o_rows = (o_in[h] * share).T.astype(BF)
        od_a[:, h * D : (h + 1) * D] = o_rows[:half]
        od_b[:, h * D : (h + 1) * D] = o_rows[half:]
        q = both(qa, qb, h * D)
        do = both(qa, qb, (G + h) * D)
        dq_s[...] = jnp.zeros(dq_s.shape, F32)

        def step(g, masked):
            kv = kv_s[pl.ds(4 * g, 4)]
            k = kv[:, :, :D].reshape(keys, D)
            v = kv[:, :, D:].reshape(keys, D)
            s = dot(k, q, NT)
            p = jnp.exp2(s * C2 - lse2)
            if masked:
                p = jnp.where(chunk_mask(idx, g, keys, rows, per, tok), p, 0.0)
            dv_s[g] += dot(p.astype(BF), do, NN)
            dp = dot(v, do, NT)
            dsc = (p * (dp - delta)).astype(BF)
            dk_s[g] += dot(dsc, q, NN)
            dq_s[...] += dot(kt_s[g], dsc, NN)

        def full(g, _):
            step(g, False)
            return 0

        lax.fori_loop(0, live, full, 0)
        step(live, True)
        dq = (dq_s[...] * SCALE).T.astype(BF)
        od_a[:, (G + h) * D : (G + h + 1) * D] = dq[:half]
        od_b[:, (G + h) * D : (G + h + 1) * D] = dq[half:]

    for ref, offs in (
        (g_own, (0, -4, -8, -12)),
        (g_lo1, (-1, -5, -9, -13)),
        (g_hi1, (1, -3, -7, -11)),
        (g_lo2, (-6, -10)),
        (g_hi2, (2, -2)),
    ):
        for j, off in enumerate(offs):
            t = (z + (off + nz)) % nz
            g, i = t // 4, t % 4
            dk = dk_s[g, pl.ds(pl.multiple_of(i * per, per), per), :] * SCALE
            dv = dv_s[g, pl.ds(pl.multiple_of(i * per, per), per), :]
            ref[j] = jnp.concatenate([dk, dv], axis=1).astype(ref.dtype)


def attention_forward(tok, idx, qa, qb, parts):
    rows = 2 * qa.shape[0]
    nz, per = 16, parts[0].shape[1]
    vm = pl.BlockSpec(memory_space=pltpu.VMEM)
    return pl.pallas_call(
        functools.partial(fwd_kernel, tok),
        out_shape=(
            jax.ShapeDtypeStruct((G, D, rows), F32),
            jax.ShapeDtypeStruct((16, rows), F32),
        ),
        in_specs=[pl.BlockSpec(memory_space=pltpu.SMEM)] + [vm] * 7,
        out_specs=(vm, vm),
        scratch_shapes=[
            pltpu.VMEM((nz, per, 2 * D), BF),
            pltpu.VMEM((nz // 4, D, 4 * per), BF),
            pltpu.VMEM((D, rows), F32),
            pltpu.VMEM((1, rows), F32),
            pltpu.VMEM((1, rows), F32),
        ],
        compiler_params=pltpu.CompilerParams(vmem_limit_bytes=40 << 20),
        name="attn_fwd",
    )(idx, qa, qb, *parts)


def attention_backward(tok, idx, qa, qb, parts, o, st, st_all):
    nz, per = 16, parts[0].shape[1]
    vm = pl.BlockSpec(memory_space=pltpu.VMEM)
    own, lo1, hi1, lo2, hi2 = parts
    return pl.pallas_call(
        functools.partial(bwd_kernel, tok),
        out_shape=(
            jax.ShapeDtypeStruct(qa.shape, BF),
            jax.ShapeDtypeStruct(qa.shape, BF),
            jax.ShapeDtypeStruct(own.shape, F32),
            jax.ShapeDtypeStruct(lo1.shape, BF),
            jax.ShapeDtypeStruct(hi1.shape, BF),
            jax.ShapeDtypeStruct(lo2.shape, BF),
            jax.ShapeDtypeStruct(hi2.shape, BF),
        ),
        in_specs=[pl.BlockSpec(memory_space=pltpu.SMEM)] + [vm] * 10,
        out_specs=(vm,) * 7,
        scratch_shapes=[
            pltpu.VMEM((nz, per, 2 * D), BF),
            pltpu.VMEM((nz // 4, D, 4 * per), BF),
            pltpu.VMEM((nz // 4, 4 * per, D), F32),
            pltpu.VMEM((nz // 4, 4 * per, D), F32),
            pltpu.VMEM((D, 2 * qa.shape[0]), F32),
        ],
        compiler_params=pltpu.CompilerParams(vmem_limit_bytes=48 << 20),
        name="attn_bwd",
    )(idx, qa, qb, own, lo1, hi1, lo2, hi2, o, st, st_all)


def shift(x, by):
    n = lax.axis_size("z")
    return lax.ppermute(x, "z", [(i, (i + by) % n) for i in range(n)])


def other_core(x):
    return lax.ppermute(x, "core", [(0, 1), (1, 0)])


def shards(query, keys, values, grad):
    tok = query.shape[0]
    tp = lax.axis_size("tp")
    nx = lax.axis_size("xl")
    share = tok // nx
    idx = jnp.stack([lax.axis_index(a) for a in ("z", "xl", "core")]).astype(jnp.int32)
    hw = G * D

    def kv_rows(x):
        return x.reshape(nx, share, tp, D).transpose(0, 2, 1, 3)

    kv = jnp.concatenate([kv_rows(keys), kv_rows(values)], axis=2)
    qd = jnp.concatenate([query.reshape(tok, tp, hw), grad.reshape(tok, tp, hw)], axis=2)
    qd = jnp.broadcast_to(qd.transpose(1, 0, 2)[None], (nx, tp, tok, 2 * hw))
    sent = jnp.concatenate([qd, kv], axis=3).reshape(nx * tp, tok, 2 * hw + D)
    got = lax.all_to_all(sent, SIDE, split_axis=0, concat_axis=0, tiled=True)
    qa = got[:, :, : 2 * hw].reshape(nx * tp * tok, 2 * hw)
    kv = got[:, :, 2 * hw :]
    kv = jnp.concatenate([kv[:, :share], kv[:, share:]], axis=2).reshape(nx * tp * share, 2 * D)

    own = jnp.stack([kv, shift(kv, 4), shift(kv, 8), shift(kv, -4)])
    qb = other_core(qa)
    parts = (own, shift(own, 1), shift(own, -1), shift(own[1:3], 2), shift(own[:2], -2))

    o, st = attention_forward(tok, idx, qa, qb, parts)
    st_all = lax.all_gather(st, COLS, axis=0, tiled=False)
    od_a, od_b, g_own, g_lo1, g_hi1, g_lo2, g_hi2 = attention_backward(
        tok, idx, qa, qb, parts, o, st, st_all
    )

    od = od_a.astype(F32) + other_core(od_b).astype(F32)
    od = od.astype(BF).reshape(nx * tp, tok, 2 * hw)

    up1, down1 = shift(g_hi1, 1).astype(F32), shift(g_lo1, -1).astype(F32)
    up2, down2 = shift(g_hi2, 2).astype(F32), shift(g_lo2, -2).astype(F32)
    four = g_own + up1 + down1
    four = four + jnp.concatenate([up2, jnp.zeros_like(up2)])
    four = four + jnp.pad(down2, ((1, 1), (0, 0), (0, 0)))
    send = four[1:].astype(BF)
    gkv = four[0] + shift(send[0], -4).astype(F32)
    gkv = gkv + shift(send[1], 8).astype(F32) + shift(send[2], 4).astype(F32)
    gkv = gkv.astype(BF).reshape(nx * tp, share, 2 * D)
    gkv = jnp.concatenate([gkv[:, :, :D], gkv[:, :, D:]], axis=1)

    back = jnp.concatenate([od, gkv], axis=2)
    back = lax.all_to_all(back, SIDE, split_axis=0, concat_axis=0, tiled=True)
    back = back.reshape(nx, tp, tok, 2 * hw + D)
    od = jnp.sum(back[:, :, :, : 2 * hw].astype(F32), axis=0).astype(BF)

    def to_tokens(x):
        return x.transpose(1, 0, 2).reshape(tok, -1)

    def kv_tokens(x):
        return x.transpose(0, 2, 1, 3).reshape(tok, tp * D)

    return (
        to_tokens(od[:, :, :hw]),
        to_tokens(od[:, :, hw:]),
        kv_tokens(back[:, :, :share, 2 * hw :]),
        kv_tokens(back[:, :, share:, 2 * hw :]),
    )


def solution(mesh):
    tp = mesh.shape["tp"]
    inner = Mesh(mesh.devices.reshape(16, 2, 2, tp), ("z", "xl", "core", "tp"))
    spec = P(("z", "xl", "core", "tp"), None)
    return jax.shard_map(
        shards, mesh=inner, in_specs=(spec,) * 4, out_specs=(spec,) * 4, check_vma=False
    )
```

time: 194 us -> 174 us (0.90)
  waiting for transfers between devices: 37.1 us -> 14.3 us
  blocking collectives: 20.7 us -> 37.8 us
  starting transfers between devices: 117 us -> 104 us
  local copies, waits for them, and re-layouts: 6.38 us -> 4.18 us
    all_to_all x3 -> x0, starting transfers between devices: 22.9 us -> none  [the longest x1 8.01 us: shards(): lax.all_to_all(od.reshape(cols * tp, tok, 2 * hw), PLANE, split_axis=0, c...]
    all_to_all x3 -> x0, waiting for transfers between devices: 20.4 us -> none  [the longest x1 14.8 us: shards(): lax.all_to_all(od.reshape(cols * tp, tok, 2 * hw), PLANE, split_axis=0, c...]
    all_to_all x1 -> x2, blocking collectives: 13.2 us -> 30.3 us  [the longest x1 17.5 us: shards(): got = lax.all_to_all(sent, SIDE, split_axis=0, concat_axis=0, tiled=True)]
    ppermute x0 -> x2, starting transfers between devices: none -> 8.34 us  [other_core(): return lax.ppermute(x, 'core', [(0, 1), (1, 0)])]
    ppermute x14, waiting for transfers between devices: 16.7 us -> 13.4 us  [shift(): return lax.ppermute(x, 'z', [(i, (i + by) % n) for i in range(n)])]
  transfers between devices with their start and end apart: 17 -> 16, of which waited for: 8 -> 7; matrix products, arithmetic and copies ran while one was open for 1% -> 0% of each run, Pallas kernels for 0% -> 0%
where the time goes in v2:
time: 174 us; the launch traced here: 171 us
  starting transfers between devices  104 us (60%)
  blocking collectives  37.8 us (22%)
  waiting for transfers between devices  14.3 us (8%)
  Pallas kernels  9.2 us (5%)
  local copies, waits for them, and re-layouts  4.18 us (2%)
    ppermute x14, starting transfers between devices, shift(): return lax.ppermute(x, 'z', [(i, (i + by) % n) for i in range(n)])  95.5 us
    all_to_all x1, blocking collectives, shards(): got = lax.all_to_all(sent, SIDE, split_axis=0, concat_axis=0, tiled=True)  17.5 us
    ppermute x14, waiting for transfers between devices, shift(): return lax.ppermute(x, 'z', [(i, (i + by) % n) for i in range(n)])  13.4 us
    all_to_all x1, blocking collectives, shards(): back = lax.all_to_all(back, SIDE, split_axis=0, concat_axis=0, tiled=True)  12.8 us
    ppermute x2, starting transfers between devices, other_core(): return lax.ppermute(x, 'core', [(0, 1), (1, 0)])  8.34 us
    all_gather x1, blocking collectives, shards(): st_all = lax.all_gather(st, COLS, axis=0, tiled=False)  7.5 us
    pallas_call x1, Pallas kernels, attention_backward(): pl.pallas_call(functools.partial(bwd_kernel, tok), out_shape=(jax.ShapeDt...  5.3 us
    pallas_call x1, Pallas kernels, attention_forward(): pl.pallas_call(functools.partial(fwd_kernel, tok), out_shape=(jax.ShapeDt...  3.9 us
  transfers between devices with their start and end apart: 16, of which 7 were waited for; matrix products, arithmetic and copies ran while one was open for 0% of the time, Pallas kernels for 0%

profile of v2, /device:TPU:1, one launch (start us, length us, event | category | flops | bytes accessed | tf_op | source)
XLA Modules:
  0.0 171.1 jit_solution(13350964153063144519)
XLA Ops:
  0.6 0.9 copy.15
  1.6 0.0 copy-start
  1.6 0.0 copy-start.1
  1.6 1.0 copy.16
  2.6 0.2 copy.10
  2.7 0.1 broadcast_in_dim.2
  2.8 0.0 copy-done
  2.8 0.0 copy-done.1
  2.9 17.5 %all_to_all.10 = bf16[16,16,1152]{2,1,0:T(8,128)(2,1)S(1)} all-to-all(bf16[16,16,1152]{2,1,0:T(8,128)(2,1)S(1)} %bitcast.69), channel_id=1, replica_groups=mesh['z'=16,'xl'=2,'core'=2,'tp'=8] {'xl','tp'}, dimensions={0} | all-to-all | bytes 1179648 | tf_op jit(solution)/shard_map/all_to_all | solution.py:280
  20.4 0.1 slice.68
  20.4 5.0 %collective-permute-start = (bf16[256,1024]{1,0:T(8,128)(2,1)S(1)}, bf16[256,1024]{1,0:T(8,128)(2,1)S(1)}, u32[]{:S(2)}, u32[]{:S(2)}) collective-permute-start(bf16[256,1024]{1,0:T(8,128)(2,1)S(1)} %bitcast.63), channel_id=1, source_target_pairs={{0,8},{8,0},{1,9},{9,1},{2,10},{10,2},{3,11},{11,3},{4,12},{12,4},... | collective-permute-start | bytes 1572872 | tf_op jit(solution)/shard_map/ppermute | solution.py:262
  25.5 12.5 %collective-permute-start.3 = (bf16[128,256]{1,0:T(8,128)(2,1)S(1)}, bf16[128,256]{1,0:T(8,128)(2,1)S(1)}, u32[]{:S(2)}, u32[]{:S(2)}) collective-permute-start(bf16[128,256]{1,0:T(8,128)(2,1)S(1)} %get-tuple-element.38), channel_id=1, source_target_pairs={{0,384},{32,416},{64,448},{96,480},{128,0},{160,32},{192,64},{224,... | collective-permute-start | bytes 196616 | tf_op jit(solution)/shard_map/ppermute | solution.py:258
  38.0 4.9 %collective-permute-start.2 = (bf16[128,256]{1,0:T(8,128)(2,1)S(1)}, bf16[128,256]{1,0:T(8,128)(2,1)S(1)}, u32[]{:S(2)}, u32[]{:S(2)}) collective-permute-start(bf16[128,256]{1,0:T(8,128)(2,1)S(1)} %get-tuple-element.38), channel_id=1, source_target_pairs={{0,256},{32,288},{64,320},{96,352},{128,384},{160,416},{192,448},{... | collective-permute-start | bytes 196616 | tf_op jit(solution)/shard_map/ppermute | solution.py:258
  42.9 7.3 %collective-permute-start.1 = (bf16[128,256]{1,0:T(8,128)(2,1)S(1)}, bf16[128,256]{1,0:T(8,128)(2,1)S(1)}, u32[]{:S(2)}, u32[]{:S(2)}) collective-permute-start(bf16[128,256]{1,0:T(8,128)(2,1)S(1)} %get-tuple-element.38), channel_id=1, source_target_pairs={{0,128},{32,160},{64,192},{96,224},{128,256},{160,288},{192,320},{... | collective-permute-start | bytes 196616 | tf_op jit(solution)/shard_map/ppermute | solution.py:258
  50.2 0.0 collective-permute-done.3
  50.2 1.9 %collective-permute-done.2 = bf16[128,256]{1,0:T(8,128)(2,1)S(1)} collective-permute-done((bf16[128,256]{1,0:T(8,128)(2,1)S(1)}, bf16[128,256]{1,0:T(8,128)(2,1)S(1)}, u32[]{:S(2)}, u32[]{:S(2)}) %collective-permute-start.2) | collective-permute-done | bytes 65568 | tf_op jit(solution)/shard_map/ppermute | solution.py:258
  52.1 3.6 %collective-permute-done.1 = bf16[128,256]{1,0:T(8,128)(2,1)S(1)} collective-permute-done((bf16[128,256]{1,0:T(8,128)(2,1)S(1)}, bf16[128,256]{1,0:T(8,128)(2,1)S(1)}, u32[]{:S(2)}, u32[]{:S(2)}) %collective-permute-start.1) | collective-permute-done | bytes 65568 | tf_op jit(solution)/shard_map/ppermute | solution.py:258
  55.7 8.1 %collective-permute-start.5 = (bf16[4,128,256]{2,1,0:T(8,128)(2,1)S(1)}, bf16[4,128,256]{2,1,0:T(8,128)(2,1)S(1)}, u32[]{:S(2)}, u32[]{:S(2)}) collective-permute-start(bf16[4,128,256]{2,1,0:T(8,128)(2,1)S(1)} %pad_maximum_fusion.own), channel_id=1, source_target_pairs={{0,480},{32,0},{64,32},{96,64},{128,96},{160,128},{192,160},{224,1... | collective-permute-start | bytes 786440 | tf_op jit(solution)/shard_map/ppermute | solution.py:258
  63.9 1.9 %collective-permute-start.4 = (bf16[4,128,256]{2,1,0:T(8,128)(2,1)S(1)}, bf16[4,128,256]{2,1,0:T(8,128)(2,1)S(1)}, u32[]{:S(2)}, u32[]{:S(2)}) collective-permute-start(bf16[4,128,256]{2,1,0:T(8,128)(2,1)S(1)} %pad_maximum_fusion.own), channel_id=1, source_target_pairs={{0,32},{32,64},{64,96},{96,128},{128,160},{160,192},{192,224},{224... | collective-permute-start | bytes 786440 | tf_op jit(solution)/shard_map/ppermute | solution.py:258
  65.8 3.1 %collective-permute-start.7 = (bf16[2,128,256]{2,1,0:T(8,128)(2,1)S(1)}, bf16[2,128,256]{2,1,0:T(8,128)(2,1)S(1)}, u32[]{:S(2)}, u32[]{:S(2)}) collective-permute-start(bf16[2,128,256]{2,1,0:T(8,128)(2,1)S(1)} %get-tuple-element.35), channel_id=1, source_target_pairs={{0,448},{32,480},{64,0},{96,32},{128,64},{160,96},{192,128},{224,1... | collective-permute-start | bytes 393224 | tf_op jit(solution)/shard_map/ppermute | solution.py:258
  68.9 3.1 %collective-permute-start.6 = (bf16[2,128,256]{2,1,0:T(8,128)(2,1)S(1)}, bf16[2,128,256]{2,1,0:T(8,128)(2,1)S(1)}, u32[]{:S(2)}, u32[]{:S(2)}) collective-permute-start(bf16[2,128,256]{2,1,0:T(8,128)(2,1)S(1)} %get-tuple-element.36), channel_id=1, source_target_pairs={{0,64},{32,96},{64,128},{96,160},{128,192},{160,224},{192,256},{22... | collective-permute-start | bytes 393224 | tf_op jit(solution)/shard_map/ppermute | solution.py:258
  72.0 0.1 pad_add_fusion.idx
  72.1 3.5 %collective-permute-done.7.hi2 = bf16[2,128,256]{2,1,0:T(8,128)(2,1)S(1)} collective-permute-done((bf16[2,128,256]{2,1,0:T(8,128)(2,1)S(1)}, bf16[2,128,256]{2,1,0:T(8,128)(2,1)S(1)}, u32[]{:S(2)}, u32[]{:S(2)}) %collective-permute-start.7) | collective-permute-done | bytes 131104 | tf_op jit(solution)/shard_map/ppermute | solution.py:258
  75.6 1.2 collective-permute-done.6.lo2
  76.8 0.0 collective-permute-done.5.hi1
  76.8 0.0 collective-permute-done.4.lo1
  76.8 0.0 collective-permute-done.qb
  76.8 3.9 %attn_fwd.1 = (f32[4,128,512]{2,1,0:T(8,128)S(1)}, f32[16,512]{1,0:T(8,128)S(1)}) custom-call(s32[3]{0:T(128)S(1)} %pad_add_fusion.idx, bf16[256,1024]{1,0:T(8,128)(2,1)S(1)} %bitcast.64, bf16[256,1024]{1,0:T(8,128)(2,1)S(1)} %collective-permute-done.qb, bf16[4,128,256]{2,1,0:T(8,128)(2,1)S(1)} %pad_maximum_fusion.own, ...), custom_call_target="tpu_custom_call" | custom-call | tf_op jit(solution)/shard_map/attn_fwd/pallas_call | solution.py:207
  80.7 7.5 %all-gather = f32[64,512]{1,0:T(8,128)S(1)} all-gather(f32[16,512]{1,0:T(8,128)S(1)} %get-tuple-element.14.st_own), channel_id=2, replica_groups=mesh['z'=16,'xl'=2,'core'=2,'tp'=8] {'xl','core'}, dimensions={0}, use_global_device_ids=true | all-gather | bytes 163840 | tf_op jit(solution)/shard_map/all_gather | solution.py:290
  88.2 5.3 %attn_bwd.1 = (bf16[256,1024]{1,0:T(8,128)(2,1)S(1)}, bf16[256,1024]{1,0:T(8,128)(2,1)S(1)}, f32[4,128,256]{2,1,0:T(8,128)S(1)}, bf16[4,128,256]{2,1,0:T(8,128)(...) custom-call(s32[3]{0:T(128)S(1)} %pad_add_fusion.idx, ...), custom_call_target="tpu_custom_call" | custom-call | tf_op jit(solution)/shard_map/attn_bwd/pallas_call | solution.py:231
  93.5 5.8 %collective-permute-start.9 = (bf16[4,128,256]{2,1,0:T(8,128)(2,1)S(1)}, bf16[4,128,256]{2,1,0:T(8,128)(2,1)S(1)}, u32[]{:S(2)}, u32[]{:S(2)}) collective-permute-start(bf16[4,128,256]{2,1,0:T(8,128)(2,1)S(1)} %get-tuple-element.18), channel_id=1, source_target_pairs={{0,32},{32,64},{64,96},{96,128},{128,160},{160,192},{192,224},{224... | collective-permute-start | bytes 786440 | tf_op jit(solution)/shard_map/ppermute | solution.py:258
  99.3 19.7 %collective-permute-start.10 = (bf16[4,128,256]{2,1,0:T(8,128)(2,1)S(1)}, bf16[4,128,256]{2,1,0:T(8,128)(2,1)S(1)}, u32[]{:S(2)}, u32[]{:S(2)}) collective-permute-start(bf16[4,128,256]{2,1,0:T(8,128)(2,1)S(1)} %get-tuple-element.19), channel_id=1, source_target_pairs={{0,480},{32,0},{64,32},{96,64},{128,96},{160,128},{192,160},{224,1... | collective-permute-start | bytes 786440 | tf_op jit(solution)/shard_map/ppermute | solution.py:258
  119.0 1.9 %collective-permute-start.11 = (bf16[2,128,256]{2,1,0:T(8,128)(2,1)S(1)}, bf16[2,128,256]{2,1,0:T(8,128)(2,1)S(1)}, u32[]{:S(2)}, u32[]{:S(2)}) collective-permute-start(bf16[2,128,256]{2,1,0:T(8,128)(2,1)S(1)} %get-tuple-element.20), channel_id=1, source_target_pairs={{0,64},{32,96},{64,128},{96,160},{128,192},{160,224},{192,256},{22... | collective-permute-start | bytes 393224 | tf_op jit(solution)/shard_map/ppermute | solution.py:258
  121.0 5.5 %collective-permute-start.12 = (bf16[2,128,256]{2,1,0:T(8,128)(2,1)S(1)}, bf16[2,128,256]{2,1,0:T(8,128)(2,1)S(1)}, u32[]{:S(2)}, u32[]{:S(2)}) collective-permute-start(bf16[2,128,256]{2,1,0:T(8,128)(2,1)S(1)} %get-tuple-element.21), channel_id=1, source_target_pairs={{0,448},{32,480},{64,0},{96,32},{128,64},{160,96},{192,128},{224,1... | collective-permute-start | bytes 393224 | tf_op jit(solution)/shard_map/ppermute | solution.py:258
  126.5 2.7 %collective-permute-done.11 = bf16[2,128,256]{2,1,0:T(8,128)(2,1)S(1)} collective-permute-done((bf16[2,128,256]{2,1,0:T(8,128)(2,1)S(1)}, bf16[2,128,256]{2,1,0:T(8,128)(2,1)S(1)}, u32[]{:S(2)}, u32[]{:S(2)}) %collective-permute-start.11) | collective-permute-done | bytes 131104 | tf_op jit(solution)/shard_map/ppermute | solution.py:258
  129.2 0.0 collective-permute-done.12
  129.2 0.0 collective-permute-done.9
  129.2 0.0 collective-permute-done.10
  129.2 0.1 fusion.7
  129.3 9.7 %collective-permute-start.13 = (bf16[128,256]{1,0:T(8,128)(2,1)S(1)}, bf16[128,256]{1,0:T(8,128)(2,1)S(1)}, u32[]{:S(2)}, u32[]{:S(2)}) collective-permute-start(bf16[128,256]{1,0:T(8,128)(2,1)S(1)} %get-tuple-element.30), channel_id=1, source_target_pairs={{0,384},{32,416},{64,448},{96,480},{128,0},{160,32},{192,64},{224,... | collective-permute-start | bytes 196616 | tf_op jit(solution)/shard_map/ppermute | solution.py:258
  139.1 1.9 %collective-permute-start.15 = (bf16[128,256]{1,0:T(8,128)(2,1)S(1)}, bf16[128,256]{1,0:T(8,128)(2,1)S(1)}, u32[]{:S(2)}, u32[]{:S(2)}) collective-permute-start(bf16[128,256]{1,0:T(8,128)(2,1)S(1)} %get-tuple-element.31), channel_id=1, source_target_pairs={{0,128},{32,160},{64,192},{96,224},{128,256},{160,288},{192,320},{... | collective-permute-start | bytes 196616 | tf_op jit(solution)/shard_map/ppermute | solution.py:258
  141.0 10.0 %collective-permute-start.14 = (bf16[128,256]{1,0:T(8,128)(2,1)S(1)}, bf16[128,256]{1,0:T(8,128)(2,1)S(1)}, u32[]{:S(2)}, u32[]{:S(2)}) collective-permute-start(bf16[128,256]{1,0:T(8,128)(2,1)S(1)} %get-tuple-element.32), channel_id=1, source_target_pairs={{0,256},{32,288},{64,320},{96,352},{128,384},{160,416},{192,448},{... | collective-permute-start | bytes 196616 | tf_op jit(solution)/shard_map/ppermute | solution.py:258
  151.1 3.3 %collective-permute-start.8 = (bf16[256,1024]{1,0:T(8,128)(2,1)S(1)}, bf16[256,1024]{1,0:T(8,128)(2,1)S(1)}, u32[]{:S(2)}, u32[]{:S(2)}) collective-permute-start(bf16[256,1024]{1,0:T(8,128)(2,1)S(1)} %get-tuple-element.16), channel_id=1, source_target_pairs={{0,8},{8,0},{1,9},{9,1},{2,10},{10,2},{3,11},{11,3},{4,12},{12,4},... | collective-permute-start | bytes 1572872 | tf_op jit(solution)/shard_map/ppermute | solution.py:262
  154.4 0.0 collective-permute-done.13
  154.4 0.0 collective-permute-done.15
  154.4 0.5 collective-permute-done.14
  155.0 0.9 collective-permute-done.8
  155.9 0.2 add_convert_fusion
  156.2 12.8 %all_to_all.11 = bf16[16,16,1152]{2,1,0:T(8,128)(2,1)S(1)} all-to-all(bf16[16,16,1152]{2,1,0:T(8,128)(2,1)S(1)} %maximum_maximum_fusion.1), channel_id=1, replica_groups=mesh['z'=16,'xl'=2,'core'=2,'tp'=8] {'xl','tp'}, dimensions={0} | all-to-all | bytes 1179648 | tf_op jit(solution)/shard_map/all_to_all | solution.py:310
  169.0 0.6 slice_bitcast_fusion.6
  169.6 0.1 slice_reduce_fusion
  169.7 0.7 copy.14
  170.4 0.7 copy.13
  (11 shorter events, 0.3 us)
Async XLA Ops:
  1.6 1.2 copy-start
  1.6 1.2 copy-start.1
  20.4 56.4 %collective-permute-start = (bf16[256,1024]{1,0:T(8,128)(2,1)S(1)}, bf16[256,1024]{1,0:T(8,128)(2,1)S(1)}, u32[]{:S(2)}, u32[]{:S(2)}) collective-permute-start(bf16[256,1024]{1,0:T(8,128)(2,1)S(1)} %bitcast.63), channel_id=1, source_target_pairs={{0,8},{8,0},{1,9},{9,1},{2,10},{10,2},{3,11},{11,3},{4,12},{12,4},... | collective-permute-start | bytes 1572872 | tf_op jit(solution)/shard_map/ppermute | solution.py:262
  25.5 24.7 %collective-permute-start.3 = (bf16[128,256]{1,0:T(8,128)(2,1)S(1)}, bf16[128,256]{1,0:T(8,128)(2,1)S(1)}, u32[]{:S(2)}, u32[]{:S(2)}) collective-permute-start(bf16[128,256]{1,0:T(8,128)(2,1)S(1)} %get-tuple-element.38), channel_id=1, source_target_pairs={{0,384},{32,416},{64,448},{96,480},{128,0},{160,32},{192,64},{224,... | collective-permute-start | bytes 196616 | tf_op jit(solution)/shard_map/ppermute | solution.py:258
  38.0 14.1 %collective-permute-start.2 = (bf16[128,256]{1,0:T(8,128)(2,1)S(1)}, bf16[128,256]{1,0:T(8,128)(2,1)S(1)}, u32[]{:S(2)}, u32[]{:S(2)}) collective-permute-start(bf16[128,256]{1,0:T(8,128)(2,1)S(1)} %get-tuple-element.38), channel_id=1, source_target_pairs={{0,256},{32,288},{64,320},{96,352},{128,384},{160,416},{192,448},{... | collective-permute-start | bytes 196616 | tf_op jit(solution)/shard_map/ppermute | solution.py:258
  42.9 12.8 %collective-permute-start.1 = (bf16[128,256]{1,0:T(8,128)(2,1)S(1)}, bf16[128,256]{1,0:T(8,128)(2,1)S(1)}, u32[]{:S(2)}, u32[]{:S(2)}) collective-permute-start(bf16[128,256]{1,0:T(8,128)(2,1)S(1)} %get-tuple-element.38), channel_id=1, source_target_pairs={{0,128},{32,160},{64,192},{96,224},{128,256},{160,288},{192,320},{... | collective-permute-start | bytes 196616 | tf_op jit(solution)/shard_map/ppermute | solution.py:258
  55.7 21.1 %collective-permute-start.5 = (bf16[4,128,256]{2,1,0:T(8,128)(2,1)S(1)}, bf16[4,128,256]{2,1,0:T(8,128)(2,1)S(1)}, u32[]{:S(2)}, u32[]{:S(2)}) collective-permute-start(bf16[4,128,256]{2,1,0:T(8,128)(2,1)S(1)} %pad_maximum_fusion.own), channel_id=1, source_target_pairs={{0,480},{32,0},{64,32},{96,64},{128,96},{160,128},{192,160},{224,1... | collective-permute-start | bytes 786440 | tf_op jit(solution)/shard_map/ppermute | solution.py:258
  63.9 12.9 %collective-permute-start.4 = (bf16[4,128,256]{2,1,0:T(8,128)(2,1)S(1)}, bf16[4,128,256]{2,1,0:T(8,128)(2,1)S(1)}, u32[]{:S(2)}, u32[]{:S(2)}) collective-permute-start(bf16[4,128,256]{2,1,0:T(8,128)(2,1)S(1)} %pad_maximum_fusion.own), channel_id=1, source_target_pairs={{0,32},{32,64},{64,96},{96,128},{128,160},{160,192},{192,224},{224... | collective-permute-start | bytes 786440 | tf_op jit(solution)/shard_map/ppermute | solution.py:258
  65.8 9.8 %collective-permute-start.7 = (bf16[2,128,256]{2,1,0:T(8,128)(2,1)S(1)}, bf16[2,128,256]{2,1,0:T(8,128)(2,1)S(1)}, u32[]{:S(2)}, u32[]{:S(2)}) collective-permute-start(bf16[2,128,256]{2,1,0:T(8,128)(2,1)S(1)} %get-tuple-element.35), channel_id=1, source_target_pairs={{0,448},{32,480},{64,0},{96,32},{128,64},{160,96},{192,128},{224,1... | collective-permute-start | bytes 393224 | tf_op jit(solution)/shard_map/ppermute | solution.py:258
  68.9 7.8 %collective-permute-start.6 = (bf16[2,128,256]{2,1,0:T(8,128)(2,1)S(1)}, bf16[2,128,256]{2,1,0:T(8,128)(2,1)S(1)}, u32[]{:S(2)}, u32[]{:S(2)}) collective-permute-start(bf16[2,128,256]{2,1,0:T(8,128)(2,1)S(1)} %get-tuple-element.36), channel_id=1, source_target_pairs={{0,64},{32,96},{64,128},{96,160},{128,192},{160,224},{192,256},{22... | collective-permute-start | bytes 393224 | tf_op jit(solution)/shard_map/ppermute | solution.py:258
  93.5 35.7 %collective-permute-start.9 = (bf16[4,128,256]{2,1,0:T(8,128)(2,1)S(1)}, bf16[4,128,256]{2,1,0:T(8,128)(2,1)S(1)}, u32[]{:S(2)}, u32[]{:S(2)}) collective-permute-start(bf16[4,128,256]{2,1,0:T(8,128)(2,1)S(1)} %get-tuple-element.18), channel_id=1, source_target_pairs={{0,32},{32,64},{64,96},{96,128},{128,160},{160,192},{192,224},{224... | collective-permute-start | bytes 786440 | tf_op jit(solution)/shard_map/ppermute | solution.py:258
  99.3 29.9 %collective-permute-start.10 = (bf16[4,128,256]{2,1,0:T(8,128)(2,1)S(1)}, bf16[4,128,256]{2,1,0:T(8,128)(2,1)S(1)}, u32[]{:S(2)}, u32[]{:S(2)}) collective-permute-start(bf16[4,128,256]{2,1,0:T(8,128)(2,1)S(1)} %get-tuple-element.19), channel_id=1, source_target_pairs={{0,480},{32,0},{64,32},{96,64},{128,96},{160,128},{192,160},{224,1... | collective-permute-start | bytes 786440 | tf_op jit(solution)/shard_map/ppermute | solution.py:258
  119.0 10.1 %collective-permute-start.11 = (bf16[2,128,256]{2,1,0:T(8,128)(2,1)S(1)}, bf16[2,128,256]{2,1,0:T(8,128)(2,1)S(1)}, u32[]{:S(2)}, u32[]{:S(2)}) collective-permute-start(bf16[2,128,256]{2,1,0:T(8,128)(2,1)S(1)} %get-tuple-element.20), channel_id=1, source_target_pairs={{0,64},{32,96},{64,128},{96,160},{128,192},{160,224},{192,256},{22... | collective-permute-start | bytes 393224 | tf_op jit(solution)/shard_map/ppermute | solution.py:258
  121.0 8.2 %collective-permute-start.12 = (bf16[2,128,256]{2,1,0:T(8,128)(2,1)S(1)}, bf16[2,128,256]{2,1,0:T(8,128)(2,1)S(1)}, u32[]{:S(2)}, u32[]{:S(2)}) collective-permute-start(bf16[2,128,256]{2,1,0:T(8,128)(2,1)S(1)} %get-tuple-element.21), channel_id=1, source_target_pairs={{0,448},{32,480},{64,0},{96,32},{128,64},{160,96},{192,128},{224,1... | collective-permute-start | bytes 393224 | tf_op jit(solution)/shard_map/ppermute | solution.py:258
  129.3 25.1 %collective-permute-start.13 = (bf16[128,256]{1,0:T(8,128)(2,1)S(1)}, bf16[128,256]{1,0:T(8,128)(2,1)S(1)}, u32[]{:S(2)}, u32[]{:S(2)}) collective-permute-start(bf16[128,256]{1,0:T(8,128)(2,1)S(1)} %get-tuple-element.30), channel_id=1, source_target_pairs={{0,384},{32,416},{64,448},{96,480},{128,0},{160,32},{192,64},{224,... | collective-permute-start | bytes 196616 | tf_op jit(solution)/shard_map/ppermute | solution.py:258
  139.1 15.3 %collective-permute-start.15 = (bf16[128,256]{1,0:T(8,128)(2,1)S(1)}, bf16[128,256]{1,0:T(8,128)(2,1)S(1)}, u32[]{:S(2)}, u32[]{:S(2)}) collective-permute-start(bf16[128,256]{1,0:T(8,128)(2,1)S(1)} %get-tuple-element.31), channel_id=1, source_target_pairs={{0,128},{32,160},{64,192},{96,224},{128,256},{160,288},{192,320},{... | collective-permute-start | bytes 196616 | tf_op jit(solution)/shard_map/ppermute | solution.py:258
  141.0 14.0 %collective-permute-start.14 = (bf16[128,256]{1,0:T(8,128)(2,1)S(1)}, bf16[128,256]{1,0:T(8,128)(2,1)S(1)}, u32[]{:S(2)}, u32[]{:S(2)}) collective-permute-start(bf16[128,256]{1,0:T(8,128)(2,1)S(1)} %get-tuple-element.32), channel_id=1, source_target_pairs={{0,256},{32,288},{64,320},{96,352},{128,384},{160,416},{192,448},{... | collective-permute-start | bytes 196616 | tf_op jit(solution)/shard_map/ppermute | solution.py:258
  151.1 4.9 %collective-permute-start.8 = (bf16[256,1024]{1,0:T(8,128)(2,1)S(1)}, bf16[256,1024]{1,0:T(8,128)(2,1)S(1)}, u32[]{:S(2)}, u32[]{:S(2)}) collective-permute-start(bf16[256,1024]{1,0:T(8,128)(2,1)S(1)} %get-tuple-element.16), channel_id=1, source_target_pairs={{0,8},{8,0},{1,9},{9,1},{2,10},{10,2},{3,11},{11,3},{4,12},{12,4},... | collective-permute-start | bytes 1572872 | tf_op jit(solution)/shard_map/ppermute | solution.py:262

commit v3 on v2

--- a/solution.py
+++ b/solution.py
@@ -25,16 +25,15 @@
     return lax.dot_general(a, b, dims, preferred_element_type=F32)
 
 
-def place_keys(z, own, lo1, hi1, lo2, hi2, kv_s, nz):
-    for ref, offs in (
-        (own, (0, -4, -8, -12)),
-        (lo1, (-1, -5, -9, -13)),
-        (hi1, (1, -3, -7, -11)),
-        (lo2, (-6, -10)),
-        (hi2, (2, -2)),
-    ):
+PARTS = ((0, -5, 5), (-1, -6, 4), (1, -4, 6), (-2, -7, 3), (2, -3, 7), (8,))
+
+
+def place_keys(z, core, parts, kv_s):
+    nz = kv_s.shape[0]
+    sign = 1 - 2 * core
+    for ref, offs in zip(parts, PARTS):
         for j, off in enumerate(offs):
-            kv_s[(z + (off + nz)) % nz] = ref[j]
+            kv_s[(z + sign * off + nz) % nz] = ref[j]
 
 
 def chunk_mask(idx, g, keys, rows, per, tok):
@@ -71,13 +70,13 @@
 
 
 def fwd_kernel(
-    tok, idx, qa, qb, own, lo1, hi1, lo2, hi2, o_out, st_out, kv_s, vt_s, acc, m_s, l_s
+    tok, idx, qa, qb, p0, p1, p2, p3, p4, p5, o_out, st_out, kv_s, vt_s, acc, m_s, l_s
 ):
     z, core = idx[0], idx[2]
     rows = 2 * qa.shape[0]
     nz, per, _ = kv_s.shape
     keys = 4 * per
-    place_keys(z, own, lo1, hi1, lo2, hi2, kv_s, nz)
+    place_keys(z, core, (p0, p1, p2, p3, p4, p5), kv_s)
     live = z // 4
 
     def flip(g, _):
@@ -122,8 +121,8 @@
 
 
 def bwd_kernel(
-    tok, idx, qa, qb, own, lo1, hi1, lo2, hi2, o_in, st_own, st_all,
-    od_a, od_b, g_own, g_lo1, g_hi1, g_lo2, g_hi2,
+    tok, idx, qa, qb, p0, p1, p2, p3, p4, p5, o_in, st_own, st_all,
+    od_a, od_b, g0, g1, g2, g3, g4, g5,
     kv_s, kt_s, dk_s, dv_s, dq_s,
 ):
     z, core = idx[0], idx[2]
@@ -131,7 +130,7 @@
     rows = 2 * half
     nz, per, _ = kv_s.shape
     keys = 4 * per
-    place_keys(z, own, lo1, hi1, lo2, hi2, kv_s, nz)
+    place_keys(z, core, (p0, p1, p2, p3, p4, p5), kv_s)
     live = z // 4
     dk_s[...] = jnp.zeros(dk_s.shape, F32)
     dv_s[...] = jnp.zeros(dv_s.shape, F32)
@@ -185,15 +184,9 @@
         od_a[:, (G + h) * D : (G + h + 1) * D] = dq[:half]
         od_b[:, (G + h) * D : (G + h + 1) * D] = dq[half:]
 
-    for ref, offs in (
-        (g_own, (0, -4, -8, -12)),
-        (g_lo1, (-1, -5, -9, -13)),
-        (g_hi1, (1, -3, -7, -11)),
-        (g_lo2, (-6, -10)),
-        (g_hi2, (2, -2)),
-    ):
+    for ref, offs in zip((g0, g1, g2, g3, g4, g5), PARTS):
         for j, off in enumerate(offs):
-            t = (z + (off + nz)) % nz
+            t = (z + (1 - 2 * core) * off + nz) % nz
             g, i = t // 4, t % 4
             dk = dk_s[g, pl.ds(pl.multiple_of(i * per, per), per), :] * SCALE
             dv = dv_s[g, pl.ds(pl.multiple_of(i * per, per), per), :]
@@ -210,7 +203,7 @@
             jax.ShapeDtypeStruct((G, D, rows), F32),
             jax.ShapeDtypeStruct((16, rows), F32),
         ),
-        in_specs=[pl.BlockSpec(memory_space=pltpu.SMEM)] + [vm] * 7,
+        in_specs=[pl.BlockSpec(memory_space=pltpu.SMEM)] + [vm] * 8,
         out_specs=(vm, vm),
         scratch_shapes=[
             pltpu.VMEM((nz, per, 2 * D), BF),
@@ -227,20 +220,16 @@
 def attention_backward(tok, idx, qa, qb, parts, o, st, st_all):
     nz, per = 16, parts[0].shape[1]
     vm = pl.BlockSpec(memory_space=pltpu.VMEM)
-    own, lo1, hi1, lo2, hi2 = parts
     return pl.pallas_call(
         functools.partial(bwd_kernel, tok),
         out_shape=(
             jax.ShapeDtypeStruct(qa.shape, BF),
             jax.ShapeDtypeStruct(qa.shape, BF),
-            jax.ShapeDtypeStruct(own.shape, F32),
-            jax.ShapeDtypeStruct(lo1.shape, BF),
-            jax.ShapeDtypeStruct(hi1.shape, BF),
-            jax.ShapeDtypeStruct(lo2.shape, BF),
-            jax.ShapeDtypeStruct(hi2.shape, BF),
+            jax.ShapeDtypeStruct(parts[0].shape, F32),
+            *(jax.ShapeDtypeStruct(p.shape, BF) for p in parts[1:]),
         ),
-        in_specs=[pl.BlockSpec(memory_space=pltpu.SMEM)] + [vm] * 10,
-        out_specs=(vm,) * 7,
+        in_specs=[pl.BlockSpec(memory_space=pltpu.SMEM)] + [vm] * 11,
+        out_specs=(vm,) * 8,
         scratch_shapes=[
             pltpu.VMEM((nz, per, 2 * D), BF),
             pltpu.VMEM((nz // 4, D, 4 * per), BF),
@@ -250,12 +239,13 @@
         ],
         compiler_params=pltpu.CompilerParams(vmem_limit_bytes=48 << 20),
         name="attn_bwd",
-    )(idx, qa, qb, own, lo1, hi1, lo2, hi2, o, st, st_all)
+    )(idx, qa, qb, *parts, o, st, st_all)
 
 
 def shift(x, by):
     n = lax.axis_size("z")
-    return lax.ppermute(x, "z", [(i, (i + by) % n) for i in range(n)])
+    route = [(2 * i + c, 2 * ((i + by * (1 - 2 * c)) % n) + c) for i in range(n) for c in range(2)]
+    return lax.ppermute(x, ("z", "core"), route)
 
 
 def other_core(x):
@@ -282,27 +272,25 @@
     kv = got[:, :, 2 * hw :]
     kv = jnp.concatenate([kv[:, :share], kv[:, share:]], axis=2).reshape(nx * tp * share, 2 * D)
 
-    own = jnp.stack([kv, shift(kv, 4), shift(kv, 8), shift(kv, -4)])
+    own = jnp.stack([kv, shift(kv, 5), shift(kv, -5)])
     qb = other_core(qa)
-    parts = (own, shift(own, 1), shift(own, -1), shift(own[1:3], 2), shift(own[:2], -2))
+    parts = (own, *(shift(own, by) for by in (1, -1, 2, -2)), shift(own[2:], -3))
 
     o, st = attention_forward(tok, idx, qa, qb, parts)
     st_all = lax.all_gather(st, COLS, axis=0, tiled=False)
-    od_a, od_b, g_own, g_lo1, g_hi1, g_lo2, g_hi2 = attention_backward(
+    od_a, od_b, g_own, *g_far = attention_backward(
         tok, idx, qa, qb, parts, o, st, st_all
     )
 
     od = od_a.astype(F32) + other_core(od_b).astype(F32)
     od = od.astype(BF).reshape(nx * tp, tok, 2 * hw)
 
-    up1, down1 = shift(g_hi1, 1).astype(F32), shift(g_lo1, -1).astype(F32)
-    up2, down2 = shift(g_hi2, 2).astype(F32), shift(g_lo2, -2).astype(F32)
-    four = g_own + up1 + down1
-    four = four + jnp.concatenate([up2, jnp.zeros_like(up2)])
-    four = four + jnp.pad(down2, ((1, 1), (0, 0), (0, 0)))
-    send = four[1:].astype(BF)
-    gkv = four[0] + shift(send[0], -4).astype(F32)
-    gkv = gkv + shift(send[1], 8).astype(F32) + shift(send[2], 4).astype(F32)
+    three = g_own
+    for g, by in zip(g_far[:4], (-1, 1, -2, 2)):
+        three = three + shift(g, by).astype(F32)
+    last = three[2] + shift(g_far[4], 3)[0].astype(F32)
+    gkv = three[0] + shift(three[1].astype(BF), -5).astype(F32)
+    gkv = gkv + shift(last.astype(BF), 5).astype(F32)
     gkv = gkv.astype(BF).reshape(nx * tp, share, 2 * D)
     gkv = jnp.concatenate([gkv[:, :, :D], gkv[:, :, D:]], axis=1)
 

time: 174 us -> 162 us (0.931)
  the two profiles are of different devices: /device:TPU:1 before, /device:TPU:2 now
where the time goes in v3:
time: 162 us
  starting transfers between devices  80.9 us (50%)
  blocking collectives  37.3 us (23%)
  waiting for transfers between devices  28.7 us (18%)
  Pallas kernels  9.12 us (6%)
  local copies, waits for them, and re-layouts  4.18 us (3%)
    ppermute x14, starting transfers between devices, shift(): return lax.ppermute(x, ('z', 'core'), route)  77.1 us
    ppermute x14, waiting for transfers between devices, shift(): return lax.ppermute(x, ('z', 'core'), route)  28.7 us
    all_to_all x1, blocking collectives, shards(): got = lax.all_to_all(sent, SIDE, split_axis=0, concat_axis=0, tiled=True)  18.2 us
    all_to_all x1, blocking collectives, shards(): back = lax.all_to_all(back, SIDE, split_axis=0, concat_axis=0, tiled=True)  13.7 us
    all_gather x1, blocking collectives, shards(): st_all = lax.all_gather(st, COLS, axis=0, tiled=False)  5.42 us
    pallas_call x1, Pallas kernels, attention_backward(): pl.pallas_call(functools.partial(bwd_kernel, tok), out_shape=(jax.ShapeDt...  5.27 us
    pallas_call x1, Pallas kernels, attention_forward(): pl.pallas_call(functools.partial(fwd_kernel, tok), out_shape=(jax.ShapeDt...  3.85 us
    ppermute x2, starting transfers between devices, other_core(): return lax.ppermute(x, 'core', [(0, 1), (1, 0)])  3.84 us
  transfers between devices with their start and end apart: 16, of which 8 were waited for; matrix products, arithmetic and copies ran while one was open for 0% of the time, Pallas kernels for 0%

profile of v3, /device:TPU:2, one launch (start us, length us, event | category | flops | bytes accessed | tf_op | source)
XLA Modules:
  0.0 161.7 jit_solution(8259105790423819441)
XLA Ops:
  0.6 0.9 copy.15
  1.6 0.0 copy-start
  1.6 0.0 copy-start.1
  1.6 1.0 copy.16
  2.6 0.2 copy.10
  2.7 0.1 broadcast_in_dim.2
  2.8 0.0 copy-done
  2.8 0.0 copy-done.1
  2.9 18.2 %all_to_all.10 = bf16[16,16,1152]{2,1,0:T(8,128)(2,1)S(1)} all-to-all(bf16[16,16,1152]{2,1,0:T(8,128)(2,1)S(1)} %bitcast.64), channel_id=1, replica_groups=mesh['z'=16,'xl'=2,'core'=2,'tp'=8] {'xl','tp'}, dimensions={0} | all-to-all | bytes 1179648 | tf_op jit(solution)/shard_map/all_to_all | solution.py:270
  21.1 0.1 slice.56
  21.1 1.9 %collective-permute-start = (bf16[256,1024]{1,0:T(8,128)(2,1)S(1)}, bf16[256,1024]{1,0:T(8,128)(2,1)S(1)}, u32[]{:S(2)}, u32[]{:S(2)}) collective-permute-start(bf16[256,1024]{1,0:T(8,128)(2,1)S(1)} %bitcast.58), channel_id=1, source_target_pairs={{0,8},{8,0},{1,9},{9,1},{2,10},{10,2},{3,11},{11,3},{4,12},{12,4},... | collective-permute-start | bytes 1572872 | tf_op jit(solution)/shard_map/ppermute | solution.py:252
  23.1 14.4 %collective-permute-start.2 = (bf16[128,256]{1,0:T(8,128)(2,1)S(1)}, bf16[128,256]{1,0:T(8,128)(2,1)S(1)}, u32[]{:S(2)}, u32[]{:S(2)}) collective-permute-start(bf16[128,256]{1,0:T(8,128)(2,1)S(1)} %get-tuple-element.33), channel_id=1, source_target_pairs={{0,352},{8,168},{32,384},{40,200},{64,416},{72,232},{96,448},{104,... | collective-permute-start | bytes 196616 | tf_op jit(solution)/shard_map/ppermute | solution.py:248
  37.5 1.9 %collective-permute-start.1 = (bf16[128,256]{1,0:T(8,128)(2,1)S(1)}, bf16[128,256]{1,0:T(8,128)(2,1)S(1)}, u32[]{:S(2)}, u32[]{:S(2)}) collective-permute-start(bf16[128,256]{1,0:T(8,128)(2,1)S(1)} %get-tuple-element.33), channel_id=1, source_target_pairs={{0,160},{8,360},{32,192},{40,392},{64,224},{72,424},{96,256},{104,... | collective-permute-start | bytes 196616 | tf_op jit(solution)/shard_map/ppermute | solution.py:248
  39.5 5.2 %collective-permute-done.2 = bf16[128,256]{1,0:T(8,128)(2,1)S(1)} collective-permute-done((bf16[128,256]{1,0:T(8,128)(2,1)S(1)}, bf16[128,256]{1,0:T(8,128)(2,1)S(1)}, u32[]{:S(2)}, u32[]{:S(2)}) %collective-permute-start.2) | collective-permute-done | bytes 65568 | tf_op jit(solution)/shard_map/ppermute | solution.py:248
  44.6 2.7 %collective-permute-start.7 = (bf16[1,128,256]{2,1,0:T(8,128)(2,1)S(1)}, bf16[1,128,256]{2,1,0:T(8,128)(2,1)S(1)}, u32[]{:S(2)}, u32[]{:S(2)}) collective-permute-start(bf16[1,128,256]{2,1,0:T(8,128)(2,1)S(1)} %bitcast.72), channel_id=1, source_target_pairs={{0,416},{8,104},{32,448},{40,136},{64,480},{72,168},{96,0},{104,20... | collective-permute-start | bytes 196616 | tf_op jit(solution)/shard_map/ppermute | solution.py:248
  47.3 3.2 %collective-permute-done.1 = bf16[128,256]{1,0:T(8,128)(2,1)S(1)} collective-permute-done((bf16[128,256]{1,0:T(8,128)(2,1)S(1)}, bf16[128,256]{1,0:T(8,128)(2,1)S(1)}, u32[]{:S(2)}, u32[]{:S(2)}) %collective-permute-start.1) | collective-permute-done | bytes 65568 | tf_op jit(solution)/shard_map/ppermute | solution.py:248
  50.5 7.1 %collective-permute-start.6 = (bf16[3,128,256]{2,1,0:T(8,128)(2,1)S(1)}, bf16[3,128,256]{2,1,0:T(8,128)(2,1)S(1)}, u32[]{:S(2)}, u32[]{:S(2)}) collective-permute-start(bf16[3,128,256]{2,1,0:T(8,128)(2,1)S(1)} %pad_maximum_fusion.p0), channel_id=1, source_target_pairs={{0,448},{8,72},{32,480},{40,104},{64,0},{72,136},{96,32},{104,168}... | collective-permute-start | bytes 589832 | tf_op jit(solution)/shard_map/ppermute | solution.py:248
  57.7 1.9 %collective-permute-start.5 = (bf16[3,128,256]{2,1,0:T(8,128)(2,1)S(1)}, bf16[3,128,256]{2,1,0:T(8,128)(2,1)S(1)}, u32[]{:S(2)}, u32[]{:S(2)}) collective-permute-start(bf16[3,128,256]{2,1,0:T(8,128)(2,1)S(1)} %pad_maximum_fusion.p0), channel_id=1, source_target_pairs={{0,64},{8,456},{32,96},{40,488},{64,128},{72,8},{96,160},{104,40},... | collective-permute-start | bytes 589832 | tf_op jit(solution)/shard_map/ppermute | solution.py:248
  59.6 2.8 %collective-permute-start.4 = (bf16[3,128,256]{2,1,0:T(8,128)(2,1)S(1)}, bf16[3,128,256]{2,1,0:T(8,128)(2,1)S(1)}, u32[]{:S(2)}, u32[]{:S(2)}) collective-permute-start(bf16[3,128,256]{2,1,0:T(8,128)(2,1)S(1)} %pad_maximum_fusion.p0), channel_id=1, source_target_pairs={{0,480},{8,40},{32,0},{40,72},{64,32},{72,104},{96,64},{104,136},{... | collective-permute-start | bytes 589832 | tf_op jit(solution)/shard_map/ppermute | solution.py:248
  62.4 0.0 collective-permute-done.7.p5
  62.4 3.1 %collective-permute-start.3 = (bf16[3,128,256]{2,1,0:T(8,128)(2,1)S(1)}, bf16[3,128,256]{2,1,0:T(8,128)(2,1)S(1)}, u32[]{:S(2)}, u32[]{:S(2)}) collective-permute-start(bf16[3,128,256]{2,1,0:T(8,128)(2,1)S(1)} %pad_maximum_fusion.p0), channel_id=1, source_target_pairs={{0,32},{8,488},{32,64},{40,8},{64,96},{72,40},{96,128},{104,72},{1... | collective-permute-start | bytes 589832 | tf_op jit(solution)/shard_map/ppermute | solution.py:248
  65.5 0.1 pad_add_fusion.idx
  65.6 0.0 collective-permute-done.6.p4
  65.6 2.4 %collective-permute-done.5.p3 = bf16[3,128,256]{2,1,0:T(8,128)(2,1)S(1)} collective-permute-done((bf16[3,128,256]{2,1,0:T(8,128)(2,1)S(1)}, bf16[3,128,256]{2,1,0:T(8,128)(2,1)S(1)}, u32[]{:S(2)}, u32[]{:S(2)}) %collective-permute-start.5) | collective-permute-done | bytes 196640 | tf_op jit(solution)/shard_map/ppermute | solution.py:248
  68.0 2.0 %collective-permute-done.4.p2 = bf16[3,128,256]{2,1,0:T(8,128)(2,1)S(1)} collective-permute-done((bf16[3,128,256]{2,1,0:T(8,128)(2,1)S(1)}, bf16[3,128,256]{2,1,0:T(8,128)(2,1)S(1)}, u32[]{:S(2)}, u32[]{:S(2)}) %collective-permute-start.4) | collective-permute-done | bytes 196640 | tf_op jit(solution)/shard_map/ppermute | solution.py:248
  69.9 1.8 %collective-permute-done.3.p1 = bf16[3,128,256]{2,1,0:T(8,128)(2,1)S(1)} collective-permute-done((bf16[3,128,256]{2,1,0:T(8,128)(2,1)S(1)}, bf16[3,128,256]{2,1,0:T(8,128)(2,1)S(1)}, u32[]{:S(2)}, u32[]{:S(2)}) %collective-permute-start.3) | collective-permute-done | bytes 196640 | tf_op jit(solution)/shard_map/ppermute | solution.py:248
  71.8 0.0 collective-permute-done.qb
  71.8 3.8 %attn_fwd.1 = (f32[4,128,512]{2,1,0:T(8,128)S(1)}, f32[16,512]{1,0:T(8,128)S(1)}) custom-call(s32[3]{0:T(128)S(1)} %pad_add_fusion.idx, bf16[256,1024]{1,0:T(8,128)(2,1)S(1)} %bitcast.59, bf16[256,1024]{1,0:T(8,128)(2,1)S(1)} %collective-permute-done.qb, bf16[3,128,256]{2,1,0:T(8,128)(2,1)S(1)} %pad_maximum_fusion.p0, ...), custom_call_target="tpu_custom_call" | custom-call | tf_op jit(solution)/shard_map/attn_fwd/pallas_call | solution.py:200
  75.6 5.4 %all-gather = f32[64,512]{1,0:T(8,128)S(1)} all-gather(f32[16,512]{1,0:T(8,128)S(1)} %get-tuple-element.15.st_own), channel_id=2, replica_groups=mesh['z'=16,'xl'=2,'core'=2,'tp'=8] {'xl','core'}, dimensions={0}, use_global_device_ids=true | all-gather | bytes 163840 | tf_op jit(solution)/shard_map/all_gather | solution.py:280
  81.0 5.3 %attn_bwd.1 = (bf16[256,1024]{1,0:T(8,128)(2,1)S(1)}, bf16[256,1024]{1,0:T(8,128)(2,1)S(1)}, f32[3,128,256]{2,1,0:T(8,128)S(1)}, bf16[3,128,256]{2,1,0:T(8,128)(...) custom-call(s32[3]{0:T(128)S(1)} %pad_add_fusion.idx, ...), custom_call_target="tpu_custom_call" | custom-call | tf_op jit(solution)/shard_map/attn_bwd/pallas_call | solution.py:223
  86.3 21.9 %collective-permute-start.9 = (bf16[3,128,256]{2,1,0:T(8,128)(2,1)S(1)}, bf16[3,128,256]{2,1,0:T(8,128)(2,1)S(1)}, u32[]{:S(2)}, u32[]{:S(2)}) collective-permute-start(bf16[3,128,256]{2,1,0:T(8,128)(2,1)S(1)} %get-tuple-element.19), channel_id=1, source_target_pairs={{0,480},{8,40},{32,0},{40,72},{64,32},{72,104},{96,64},{104,136},{... | collective-permute-start | bytes 589832 | tf_op jit(solution)/shard_map/ppermute | solution.py:248
  108.2 1.9 %collective-permute-start.10 = (bf16[3,128,256]{2,1,0:T(8,128)(2,1)S(1)}, bf16[3,128,256]{2,1,0:T(8,128)(2,1)S(1)}, u32[]{:S(2)}, u32[]{:S(2)}) collective-permute-start(bf16[3,128,256]{2,1,0:T(8,128)(2,1)S(1)} %get-tuple-element.20), channel_id=1, source_target_pairs={{0,32},{8,488},{32,64},{40,8},{64,96},{72,40},{96,128},{104,72},{1... | collective-permute-start | bytes 589832 | tf_op jit(solution)/shard_map/ppermute | solution.py:248
  110.2 3.4 %collective-permute-start.11 = (bf16[3,128,256]{2,1,0:T(8,128)(2,1)S(1)}, bf16[3,128,256]{2,1,0:T(8,128)(2,1)S(1)}, u32[]{:S(2)}, u32[]{:S(2)}) collective-permute-start(bf16[3,128,256]{2,1,0:T(8,128)(2,1)S(1)} %get-tuple-element.21), channel_id=1, source_target_pairs={{0,448},{8,72},{32,480},{40,104},{64,0},{72,136},{96,32},{104,168}... | collective-permute-start | bytes 589832 | tf_op jit(solution)/shard_map/ppermute | solution.py:248
  113.6 3.4 %collective-permute-start.12 = (bf16[3,128,256]{2,1,0:T(8,128)(2,1)S(1)}, bf16[3,128,256]{2,1,0:T(8,128)(2,1)S(1)}, u32[]{:S(2)}, u32[]{:S(2)}) collective-permute-start(bf16[3,128,256]{2,1,0:T(8,128)(2,1)S(1)} %get-tuple-element.22), channel_id=1, source_target_pairs={{0,64},{8,456},{32,96},{40,488},{64,128},{72,8},{96,160},{104,40},... | collective-permute-start | bytes 589832 | tf_op jit(solution)/shard_map/ppermute | solution.py:248
  116.9 1.9 %collective-permute-start.14 = (bf16[1,128,256]{2,1,0:T(8,128)(2,1)S(1)}, bf16[1,128,256]{2,1,0:T(8,128)(2,1)S(1)}, u32[]{:S(2)}, u32[]{:S(2)}) collective-permute-start(bf16[1,128,256]{2,1,0:T(8,128)(2,1)S(1)} %get-tuple-element.23), channel_id=1, source_target_pairs={{0,96},{8,424},{32,128},{40,456},{64,160},{72,488},{96,192},{104,8... | collective-permute-start | bytes 196616 | tf_op jit(solution)/shard_map/ppermute | solution.py:248
  118.9 0.0 collective-permute-done.9
  118.9 0.9 collective-permute-done.10
  119.8 0.0 collective-permute-done.11
  119.8 4.1 %collective-permute-done.12 = bf16[3,128,256]{2,1,0:T(8,128)(2,1)S(1)} collective-permute-done((bf16[3,128,256]{2,1,0:T(8,128)(2,1)S(1)}, bf16[3,128,256]{2,1,0:T(8,128)(2,1)S(1)}, u32[]{:S(2)}, u32[]{:S(2)}) %collective-permute-start.12) | collective-permute-done | bytes 196640 | tf_op jit(solution)/shard_map/ppermute | solution.py:248
  123.9 0.1 convert_add_fusion
  124.0 7.6 %collective-permute-start.13 = (bf16[128,256]{1,0:T(8,128)(2,1)S(1)}, bf16[128,256]{1,0:T(8,128)(2,1)S(1)}, u32[]{:S(2)}, u32[]{:S(2)}) collective-permute-start(bf16[128,256]{1,0:T(8,128)(2,1)S(1)} %fusion.5), channel_id=1, source_target_pairs={{0,352},{8,168},{32,384},{40,200},{64,416},{72,232},{96,448},{104,... | collective-permute-start | bytes 196616 | tf_op jit(solution)/shard_map/ppermute | solution.py:248
  131.6 0.0 collective-permute-done.14
  131.7 3.1 %collective-permute-start.15 = (bf16[128,256]{1,0:T(8,128)(2,1)S(1)}, bf16[128,256]{1,0:T(8,128)(2,1)S(1)}, u32[]{:S(2)}, u32[]{:S(2)}) collective-permute-start(bf16[128,256]{1,0:T(8,128)(2,1)S(1)} %fusion.6), channel_id=1, source_target_pairs={{0,160},{8,360},{32,192},{40,392},{64,224},{72,424},{96,256},{104,... | collective-permute-start | bytes 196616 | tf_op jit(solution)/shard_map/ppermute | solution.py:248
  134.7 1.9 %collective-permute-start.8 = (bf16[256,1024]{1,0:T(8,128)(2,1)S(1)}, bf16[256,1024]{1,0:T(8,128)(2,1)S(1)}, u32[]{:S(2)}, u32[]{:S(2)}) collective-permute-start(bf16[256,1024]{1,0:T(8,128)(2,1)S(1)} %get-tuple-element.17), channel_id=1, source_target_pairs={{0,8},{8,0},{1,9},{9,1},{2,10},{10,2},{3,11},{11,3},{4,12},{12,4},... | collective-permute-start | bytes 1572872 | tf_op jit(solution)/shard_map/ppermute | solution.py:252
  136.6 0.0 collective-permute-done.13
  136.6 9.0 %collective-permute-done.15 = bf16[128,256]{1,0:T(8,128)(2,1)S(1)} collective-permute-done((bf16[128,256]{1,0:T(8,128)(2,1)S(1)}, bf16[128,256]{1,0:T(8,128)(2,1)S(1)}, u32[]{:S(2)}, u32[]{:S(2)}) %collective-permute-start.15) | collective-permute-done | bytes 65568 | tf_op jit(solution)/shard_map/ppermute | solution.py:248
  145.7 0.0 collective-permute-done.8
  145.7 0.2 add_convert_fusion
  146.0 13.7 %all_to_all.11 = bf16[16,16,1152]{2,1,0:T(8,128)(2,1)S(1)} all-to-all(bf16[16,16,1152]{2,1,0:T(8,128)(2,1)S(1)} %maximum_maximum_fusion.1), channel_id=1, replica_groups=mesh['z'=16,'xl'=2,'core'=2,'tp'=8] {'xl','tp'}, dimensions={0} | all-to-all | bytes 1179648 | tf_op jit(solution)/shard_map/all_to_all | solution.py:298
  159.7 0.6 slice_bitcast_fusion.3
  160.3 0.1 slice_reduce_fusion
  160.4 0.7 copy.14
  161.1 0.7 copy.13
  (11 shorter events, 0.2 us)
Async XLA Ops:
  1.6 1.2 copy-start
  1.6 1.2 copy-start.1
  21.1 50.7 %collective-permute-start = (bf16[256,1024]{1,0:T(8,128)(2,1)S(1)}, bf16[256,1024]{1,0:T(8,128)(2,1)S(1)}, u32[]{:S(2)}, u32[]{:S(2)}) collective-permute-start(bf16[256,1024]{1,0:T(8,128)(2,1)S(1)} %bitcast.58), channel_id=1, source_target_pairs={{0,8},{8,0},{1,9},{9,1},{2,10},{10,2},{3,11},{11,3},{4,12},{12,4},... | collective-permute-start | bytes 1572872 | tf_op jit(solution)/shard_map/ppermute | solution.py:252
  23.1 21.5 %collective-permute-start.2 = (bf16[128,256]{1,0:T(8,128)(2,1)S(1)}, bf16[128,256]{1,0:T(8,128)(2,1)S(1)}, u32[]{:S(2)}, u32[]{:S(2)}) collective-permute-start(bf16[128,256]{1,0:T(8,128)(2,1)S(1)} %get-tuple-element.33), channel_id=1, source_target_pairs={{0,352},{8,168},{32,384},{40,200},{64,416},{72,232},{96,448},{104,... | collective-permute-start | bytes 196616 | tf_op jit(solution)/shard_map/ppermute | solution.py:248
  37.5 13.0 %collective-permute-start.1 = (bf16[128,256]{1,0:T(8,128)(2,1)S(1)}, bf16[128,256]{1,0:T(8,128)(2,1)S(1)}, u32[]{:S(2)}, u32[]{:S(2)}) collective-permute-start(bf16[128,256]{1,0:T(8,128)(2,1)S(1)} %get-tuple-element.33), channel_id=1, source_target_pairs={{0,160},{8,360},{32,192},{40,392},{64,224},{72,424},{96,256},{104,... | collective-permute-start | bytes 196616 | tf_op jit(solution)/shard_map/ppermute | solution.py:248
  44.6 17.8 %collective-permute-start.7 = (bf16[1,128,256]{2,1,0:T(8,128)(2,1)S(1)}, bf16[1,128,256]{2,1,0:T(8,128)(2,1)S(1)}, u32[]{:S(2)}, u32[]{:S(2)}) collective-permute-start(bf16[1,128,256]{2,1,0:T(8,128)(2,1)S(1)} %bitcast.72), channel_id=1, source_target_pairs={{0,416},{8,104},{32,448},{40,136},{64,480},{72,168},{96,0},{104,20... | collective-permute-start | bytes 196616 | tf_op jit(solution)/shard_map/ppermute | solution.py:248
  50.5 15.0 %collective-permute-start.6 = (bf16[3,128,256]{2,1,0:T(8,128)(2,1)S(1)}, bf16[3,128,256]{2,1,0:T(8,128)(2,1)S(1)}, u32[]{:S(2)}, u32[]{:S(2)}) collective-permute-start(bf16[3,128,256]{2,1,0:T(8,128)(2,1)S(1)} %pad_maximum_fusion.p0), channel_id=1, source_target_pairs={{0,448},{8,72},{32,480},{40,104},{64,0},{72,136},{96,32},{104,168}... | collective-permute-start | bytes 589832 | tf_op jit(solution)/shard_map/ppermute | solution.py:248
  57.7 10.3 %collective-permute-start.5 = (bf16[3,128,256]{2,1,0:T(8,128)(2,1)S(1)}, bf16[3,128,256]{2,1,0:T(8,128)(2,1)S(1)}, u32[]{:S(2)}, u32[]{:S(2)}) collective-permute-start(bf16[3,128,256]{2,1,0:T(8,128)(2,1)S(1)} %pad_maximum_fusion.p0), channel_id=1, source_target_pairs={{0,64},{8,456},{32,96},{40,488},{64,128},{72,8},{96,160},{104,40},... | collective-permute-start | bytes 589832 | tf_op jit(solution)/shard_map/ppermute | solution.py:248
  59.6 10.3 %collective-permute-start.4 = (bf16[3,128,256]{2,1,0:T(8,128)(2,1)S(1)}, bf16[3,128,256]{2,1,0:T(8,128)(2,1)S(1)}, u32[]{:S(2)}, u32[]{:S(2)}) collective-permute-start(bf16[3,128,256]{2,1,0:T(8,128)(2,1)S(1)} %pad_maximum_fusion.p0), channel_id=1, source_target_pairs={{0,480},{8,40},{32,0},{40,72},{64,32},{72,104},{96,64},{104,136},{... | collective-permute-start | bytes 589832 | tf_op jit(solution)/shard_map/ppermute | solution.py:248
  62.4 9.4 %collective-permute-start.3 = (bf16[3,128,256]{2,1,0:T(8,128)(2,1)S(1)}, bf16[3,128,256]{2,1,0:T(8,128)(2,1)S(1)}, u32[]{:S(2)}, u32[]{:S(2)}) collective-permute-start(bf16[3,128,256]{2,1,0:T(8,128)(2,1)S(1)} %pad_maximum_fusion.p0), channel_id=1, source_target_pairs={{0,32},{8,488},{32,64},{40,8},{64,96},{72,40},{96,128},{104,72},{1... | collective-permute-start | bytes 589832 | tf_op jit(solution)/shard_map/ppermute | solution.py:248
  86.3 32.5 %collective-permute-start.9 = (bf16[3,128,256]{2,1,0:T(8,128)(2,1)S(1)}, bf16[3,128,256]{2,1,0:T(8,128)(2,1)S(1)}, u32[]{:S(2)}, u32[]{:S(2)}) collective-permute-start(bf16[3,128,256]{2,1,0:T(8,128)(2,1)S(1)} %get-tuple-element.19), channel_id=1, source_target_pairs={{0,480},{8,40},{32,0},{40,72},{64,32},{72,104},{96,64},{104,136},{... | collective-permute-start | bytes 589832 | tf_op jit(solution)/shard_map/ppermute | solution.py:248
  108.2 11.6 %collective-permute-start.10 = (bf16[3,128,256]{2,1,0:T(8,128)(2,1)S(1)}, bf16[3,128,256]{2,1,0:T(8,128)(2,1)S(1)}, u32[]{:S(2)}, u32[]{:S(2)}) collective-permute-start(bf16[3,128,256]{2,1,0:T(8,128)(2,1)S(1)} %get-tuple-element.20), channel_id=1, source_target_pairs={{0,32},{8,488},{32,64},{40,8},{64,96},{72,40},{96,128},{104,72},{1... | collective-permute-start | bytes 589832 | tf_op jit(solution)/shard_map/ppermute | solution.py:248
  110.2 9.6 %collective-permute-start.11 = (bf16[3,128,256]{2,1,0:T(8,128)(2,1)S(1)}, bf16[3,128,256]{2,1,0:T(8,128)(2,1)S(1)}, u32[]{:S(2)}, u32[]{:S(2)}) collective-permute-start(bf16[3,128,256]{2,1,0:T(8,128)(2,1)S(1)} %get-tuple-element.21), channel_id=1, source_target_pairs={{0,448},{8,72},{32,480},{40,104},{64,0},{72,136},{96,32},{104,168}... | collective-permute-start | bytes 589832 | tf_op jit(solution)/shard_map/ppermute | solution.py:248
  113.6 10.3 %collective-permute-start.12 = (bf16[3,128,256]{2,1,0:T(8,128)(2,1)S(1)}, bf16[3,128,256]{2,1,0:T(8,128)(2,1)S(1)}, u32[]{:S(2)}, u32[]{:S(2)}) collective-permute-start(bf16[3,128,256]{2,1,0:T(8,128)(2,1)S(1)} %get-tuple-element.22), channel_id=1, source_target_pairs={{0,64},{8,456},{32,96},{40,488},{64,128},{72,8},{96,160},{104,40},... | collective-permute-start | bytes 589832 | tf_op jit(solution)/shard_map/ppermute | solution.py:248
  116.9 14.7 %collective-permute-start.14 = (bf16[1,128,256]{2,1,0:T(8,128)(2,1)S(1)}, bf16[1,128,256]{2,1,0:T(8,128)(2,1)S(1)}, u32[]{:S(2)}, u32[]{:S(2)}) collective-permute-start(bf16[1,128,256]{2,1,0:T(8,128)(2,1)S(1)} %get-tuple-element.23), channel_id=1, source_target_pairs={{0,96},{8,424},{32,128},{40,456},{64,160},{72,488},{96,192},{104,8... | collective-permute-start | bytes 196616 | tf_op jit(solution)/shard_map/ppermute | solution.py:248
  124.0 12.6 %collective-permute-start.13 = (bf16[128,256]{1,0:T(8,128)(2,1)S(1)}, bf16[128,256]{1,0:T(8,128)(2,1)S(1)}, u32[]{:S(2)}, u32[]{:S(2)}) collective-permute-start(bf16[128,256]{1,0:T(8,128)(2,1)S(1)} %fusion.5), channel_id=1, source_target_pairs={{0,352},{8,168},{32,384},{40,200},{64,416},{72,232},{96,448},{104,... | collective-permute-start | bytes 196616 | tf_op jit(solution)/shard_map/ppermute | solution.py:248
  131.7 14.0 %collective-permute-start.15 = (bf16[128,256]{1,0:T(8,128)(2,1)S(1)}, bf16[128,256]{1,0:T(8,128)(2,1)S(1)}, u32[]{:S(2)}, u32[]{:S(2)}) collective-permute-start(bf16[128,256]{1,0:T(8,128)(2,1)S(1)} %fusion.6), channel_id=1, source_target_pairs={{0,160},{8,360},{32,192},{40,392},{64,224},{72,424},{96,256},{104,... | collective-permute-start | bytes 196616 | tf_op jit(solution)/shard_map/ppermute | solution.py:248
  134.7 11.0 %collective-permute-start.8 = (bf16[256,1024]{1,0:T(8,128)(2,1)S(1)}, bf16[256,1024]{1,0:T(8,128)(2,1)S(1)}, u32[]{:S(2)}, u32[]{:S(2)}) collective-permute-start(bf16[256,1024]{1,0:T(8,128)(2,1)S(1)} %get-tuple-element.17), channel_id=1, source_target_pairs={{0,8},{8,0},{1,9},{9,1},{2,10},{10,2},{3,11},{11,3},{4,12},{12,4},... | collective-permute-start | bytes 1572872 | tf_op jit(solution)/shard_map/ppermute | solution.py:252

commit v4 on v3

v4 whole, which is shorter than its diff:
```python
import functools

import jax
import jax.numpy as jnp
from jax import lax
from jax.experimental import pallas as pl
from jax.experimental.pallas import tpu as pltpu
from jax.sharding import Mesh, PartitionSpec as P

D = 128
G = 4
SCALE = D ** (-0.5)
LOG2E = 1.4426950408889634
C2 = SCALE * LOG2E
NEG = -1e30
SIDE = ("xl", "tp")
COLS = ("xl", "core")
NT = (((1,), (1,)), ((), ()))
NN = (((1,), (0,)), ((), ()))
BF = jnp.bfloat16
F32 = jnp.float32

EVEN = (0, 4, 2, 6)
ODD = (1, 5, 3, 7)


def dot(a, b, dims):
    return lax.dot_general(a, b, dims, preferred_element_type=F32)


def is_live(z, core, k, planes):
    return jnp.where(core == 0, k <= z, k >= planes - z)


def distance(order, j):
    k = jnp.int32(order[0])
    for i in range(1, len(order)):
        k = jnp.where(j == i, order[i], k)
    return k


def own_mask(idx, per, rows, tok):
    xl, core = idx[1], idx[2]
    share = tok // 2
    k = lax.broadcasted_iota(jnp.int32, (per, 1), 0)
    src = k // share
    tp = per // tok
    key_tok = ((src // tp) * 2 + core) * per + (src % tp) * tok + xl * share + k % share
    r = lax.broadcasted_iota(jnp.int32, (1, rows), 1)
    half = rows // 2
    row_core = jnp.where(r < half, core, 1 - core)
    row_tok = (((r % half) // per) * 2 + row_core) * per + r % per
    return key_tok <= row_tok


def both(a, b, lo):
    return jnp.concatenate([a[:, lo : lo + D], b[:, lo : lo + D]], axis=0)


def put_row(ref, row, x, core):
    half = x.shape[1] // 2
    ref[row : row + 1, pl.ds(pl.multiple_of(core * half, half), half)] = x[:, :half]
    ref[row : row + 1, pl.ds(pl.multiple_of((1 - core) * half, half), half)] = x[:, half:]


def get_row(ref, row, core):
    half = ref.shape[-1] // 2
    lo = ref[row : row + 1, pl.ds(pl.multiple_of(core * half, half), half)]
    hi = ref[row : row + 1, pl.ds(pl.multiple_of((1 - core) * half, half), half)]
    return jnp.concatenate([lo, hi], axis=1)


def attend(qa, qb, kv, ml, acc, mask=None):
    k, vt = kv[:, :D], kv[:, D:].T
    for h in range(G):
        s = dot(k, both(qa, qb, h * D), NT)
        if mask is not None:
            s = jnp.where(mask, s, NEG)
        m_old = ml[h : h + 1, :]
        m_new = jnp.maximum(m_old, jnp.max(s, axis=0, keepdims=True))
        p = jnp.exp2((s - m_new) * C2)
        alpha = jnp.exp2((m_old - m_new) * C2)
        ml[h : h + 1, :] = m_new
        ml[G + h : G + h + 1, :] = ml[G + h : G + h + 1, :] * alpha + jnp.sum(
            p, axis=0, keepdims=True
        )
        acc[h] = acc[h] * alpha + dot(vt, p.astype(BF), NN)


def attend_planes(idx, planes, order, first, qa, qb, kvs, ml, acc):
    z, core = idx[0], idx[2]
    per = kvs.shape[1]

    def plane(j, _):
        @pl.when(is_live(z, core, distance(order, j), planes))
        def _():
            kv = kvs[pl.ds(2 * j, 2)].reshape(2 * per, 2 * D)
            attend(qa, qb, kv, ml, acc)

        return 0

    lax.fori_loop(first, len(order), plane, 0)


def fwd_even_kernel(planes, tok, idx, qa, qb, kvs, ml, acc):
    rows = 2 * qa.shape[0]
    ml[0:G, :] = jnp.full((G, rows), NEG, F32)
    ml[G:, :] = jnp.zeros((ml.shape[0] - G, rows), F32)
    acc[...] = jnp.zeros(acc.shape, F32)
    attend(qa, qb, kvs[0], ml, acc, own_mask(idx, kvs.shape[1], rows, tok))
    attend_planes(idx, planes, EVEN, 1, qa, qb, kvs, ml, acc)


def fwd_odd_kernel(planes, idx, qa, qb, kvs, kv8, ml_in, acc_in, o_out, st_out, ml, acc):
    z, core = idx[0], idx[2]
    ml[...] = ml_in[...]
    acc[...] = acc_in[...]
    attend_planes(idx, planes, ODD, 0, qa, qb, kvs, ml, acc)

    @pl.when(is_live(z, core, planes // 2, planes))
    def _():
        attend(qa, qb, kv8[...], ml, acc)

    st_out[...] = jnp.zeros(st_out.shape, F32)
    for h in range(G):
        o_t = acc[h]
        l = ml[G + h : G + h + 1, :]
        do_t = both(qa, qb, (G + h) * D).T.astype(F32)
        put_row(st_out, h, ml[h : h + 1, :], core)
        put_row(st_out, G + h, l, core)
        put_row(st_out, 2 * G + h, jnp.sum(do_t * o_t, axis=0, keepdims=True), core)
        o_out[h] = o_t * (1.0 / l)


def joined_stats(st_all, core, h):
    ms = [get_row(st_all.at[i], h, core) for i in range(4)]
    ls = [get_row(st_all.at[i], G + h, core) for i in range(4)]
    ds = [get_row(st_all.at[i], 2 * G + h, core) for i in range(4)]
    top = functools.reduce(jnp.maximum, ms)
    w = [jnp.exp2((m - top) * C2) for m in ms]
    total = functools.reduce(jnp.add, [a * b for a, b in zip(w, ls)])
    inv = 1.0 / total
    delta = functools.reduce(jnp.add, [a * b for a, b in zip(w, ds)]) * inv
    return top, inv, top * C2 + jnp.log2(total), delta


def store_stats(st_all, core, rows_s):
    for h in range(G):
        _, _, lse2, delta = joined_stats(st_all, core, h)
        rows_s[h : h + 1, :] = lse2
        rows_s[G + h : G + h + 1, :] = delta


def grads(qa, qb, kv, rows_s, dq, mask=None):
    k, v = kv[:, :D], kv[:, D:]
    kt = k.T
    dk = jnp.zeros(k.shape, F32)
    dv = jnp.zeros(k.shape, F32)
    for h in range(G):
        q, do = both(qa, qb, h * D), both(qa, qb, (G + h) * D)
        s = dot(k, q, NT)
        p = jnp.exp2(s * C2 - rows_s[h : h + 1, :])
        if mask is not None:
            p = jnp.where(mask, p, 0.0)
        dv = dv + dot(p.astype(BF), do, NN)
        dp = dot(v, do, NT)
        ds = (p * (dp - rows_s[G + h : G + h + 1, :])).astype(BF)
        dk = dk + dot(ds, q, NN)
        dq[h] += dot(kt, ds, NN)
    return jnp.concatenate([dk * SCALE, dv], axis=1)


def grad_planes(idx, planes, order, first, qa, qb, kvs, rows_s, dq, g_out):
    z, core = idx[0], idx[2]
    per = kvs.shape[1]

    def plane(j, _):
        live = is_live(z, core, distance(order, j), planes)

        @pl.when(live)
        def _():
            kv = kvs[pl.ds(2 * j, 2)].reshape(2 * per, 2 * D)
            g = grads(qa, qb, kv, rows_s, dq)
            g_out[pl.ds(2 * j, 2)] = g.reshape(2, per, 2 * D).astype(g_out.dtype)

        @pl.when(jnp.logical_not(live))
        def _():
            g_out[pl.ds(2 * j, 2)] = jnp.zeros((2, per, 2 * D), g_out.dtype)

        return 0

    lax.fori_loop(first, len(order), plane, 0)


def bwd_odd_kernel(planes, idx, qa, qb, kvs, kv8, st_all, g_out, g8_out, dq, rows_s):
    z, core = idx[0], idx[2]
    store_stats(st_all, core, rows_s)
    dq[...] = jnp.zeros(dq.shape, F32)
    grad_planes(idx, planes, ODD, 0, qa, qb, kvs, rows_s, dq, g_out)
    live = is_live(z, core, planes // 2, planes)

    @pl.when(live)
    def _():
        g8_out[...] = grads(qa, qb, kv8[...], rows_s, dq).astype(g8_out.dtype)

    @pl.when(jnp.logical_not(live))
    def _():
        g8_out[...] = jnp.zeros(g8_out.shape, g8_out.dtype)


def bwd_even_kernel(
    planes, tok, idx, qa, qb, kvs, st_own, st_all, o_in, dq_in, g_out, od_a, od_b, dq, rows_s
):
    core = idx[2]
    half = qa.shape[0]
    store_stats(st_all, core, rows_s)
    dq[...] = dq_in[...]
    mask = own_mask(idx, kvs.shape[1], 2 * half, tok)
    g_out[0] = grads(qa, qb, kvs[0], rows_s, dq, mask)
    g_out[1] = jnp.zeros(kvs.shape[1:], F32)
    grad_planes(idx, planes, EVEN, 1, qa, qb, kvs, rows_s, dq, g_out)
    for h in range(G):
        top, inv, _, _ = joined_stats(st_all, core, h)
        m_own = get_row(st_own, h, core)
        l_own = get_row(st_own, G + h, core)
        share = jnp.exp2((m_own - top) * C2) * l_own * inv
        o = (o_in[h] * share).T.astype(BF)
        g = (dq[h] * SCALE).T.astype(BF)
        for ref, lo in ((od_a, 0), (od_b, half)):
            ref[:, h * D : (h + 1) * D] = o[lo : lo + half]
            ref[:, (G + h) * D : (G + h + 1) * D] = g[lo : lo + half]


def call(kernel, name, out_shape, args, scratch=()):
    vm = pl.BlockSpec(memory_space=pltpu.VMEM)
    return pl.pallas_call(
        kernel,
        out_shape=tuple(jax.ShapeDtypeStruct(s, d) for s, d in out_shape),
        in_specs=[pl.BlockSpec(memory_space=pltpu.SMEM)] + [vm] * (len(args) - 1),
        out_specs=(vm,) * len(out_shape),
        scratch_shapes=[pltpu.VMEM(s, F32) for s in scratch],
        compiler_params=pltpu.CompilerParams(vmem_limit_bytes=40 << 20),
        name=name,
    )(*args)


def shift(x, by):
    n = lax.axis_size("z")
    route = [(2 * i + c, 2 * ((i + by * (1 - 2 * c)) % n) + c) for i in range(n) for c in range(2)]
    return lax.ppermute(x, ("z", "core"), route)


def other_core(x):
    return lax.ppermute(x, "core", [(0, 1), (1, 0)])


def shards(query, keys, values, grad):
    tok = query.shape[0]
    tp = lax.axis_size("tp")
    nx = lax.axis_size("xl")
    planes = lax.axis_size("z")
    share = tok // nx
    rows = 2 * nx * tp * tok
    idx = jnp.stack([lax.axis_index(a) for a in ("z", "xl", "core")]).astype(jnp.int32)
    hw = G * D

    def kv_rows(x):
        return x.reshape(nx, share, tp, D).transpose(0, 2, 1, 3)

    kv = jnp.concatenate([kv_rows(keys), kv_rows(values)], axis=2)
    qd = jnp.concatenate([query.reshape(tok, tp, hw), grad.reshape(tok, tp, hw)], axis=2)
    qd = jnp.broadcast_to(qd.transpose(1, 0, 2)[None], (nx, tp, tok, 2 * hw))
    sent = jnp.concatenate([qd, kv], axis=3).reshape(nx * tp, tok, 2 * hw + D)
    got = lax.all_to_all(sent, SIDE, split_axis=0, concat_axis=0, tiled=True)
    qa = got[:, :, : 2 * hw].reshape(nx * tp * tok, 2 * hw)
    kv = got[:, :, 2 * hw :]
    kv = jnp.concatenate([kv[:, :share], kv[:, share:]], axis=2).reshape(nx * tp * share, 2 * D)

    at0 = jnp.stack([kv, other_core(kv)])
    at4 = shift(at0, 4)
    qb = other_core(qa)
    at04 = jnp.concatenate([at0, at4])
    even = jnp.concatenate([at04, shift(at04, 2)])
    odd = shift(even, 1)
    at8 = shift(even[6], 2)

    heads = ((G, D, rows), F32)
    ml, acc = call(
        functools.partial(fwd_even_kernel, planes, tok),
        "fwd_even",
        (((2 * G, rows), F32), heads),
        (idx, qa, qb, even),
    )
    o, st = call(
        functools.partial(fwd_odd_kernel, planes),
        "fwd_odd",
        (heads, ((16, rows), F32)),
        (idx, qa, qb, odd, at8, ml, acc),
        ((2 * G, rows), (G, D, rows)),
    )
    st_all = lax.all_gather(st, COLS, axis=0, tiled=False)
    g_odd, g8, dq = call(
        functools.partial(bwd_odd_kernel, planes),
        "bwd_odd",
        ((odd.shape, BF), (at8.shape, BF), heads),
        (idx, qa, qb, odd, at8, st_all),
        ((2 * G, rows),),
    )
    near, near8 = shift(g_odd, -1), shift(g8, -2)
    g_even, od_a, od_b = call(
        functools.partial(bwd_even_kernel, planes, tok),
        "bwd_even",
        ((even.shape, F32), (qa.shape, BF), (qa.shape, BF)),
        (idx, qa, qb, even, st, st_all, o, dq),
        ((G, D, rows), (2 * G, rows)),
    )
    od = od_a.astype(F32) + other_core(od_b).astype(F32)
    od = od.astype(BF).reshape(nx * tp, tok, 2 * hw)

    g_even = g_even + near.astype(F32)
    g26 = jnp.concatenate([g_even[4:6], g_even[6:7] + near8[None].astype(F32), g_even[7:]])
    g04 = g_even[:4] + shift(g26.astype(BF), -2).astype(F32)
    g0 = g04[:2] + shift(g04[2:].astype(BF), -4).astype(F32)
    gkv = g0[0] + other_core(g0[1].astype(BF)).astype(F32)
    gkv = gkv.astype(BF).reshape(nx * tp, share, 2 * D)
    gkv = jnp.concatenate([gkv[:, :, :D], gkv[:, :, D:]], axis=1)

    back = jnp.concatenate([od, gkv], axis=2)
    back = lax.all_to_all(back, SIDE, split_axis=0, concat_axis=0, tiled=True)
    back = back.reshape(nx, tp, tok, 2 * hw + D)
    od = jnp.sum(back[:, :, :, : 2 * hw].astype(F32), axis=0).astype(BF)

    def to_tokens(x):
        return x.transpose(1, 0, 2).reshape(tok, -1)

    def kv_tokens(x):
        return x.transpose(0, 2, 1, 3).reshape(tok, tp * D)

    return (
        to_tokens(od[:, :, :hw]),
        to_tokens(od[:, :, hw:]),
        kv_tokens(back[:, :, :share, 2 * hw :]),
        kv_tokens(back[:, :, share:, 2 * hw :]),
    )


def solution(mesh):
    tp = mesh.shape["tp"]
    inner = Mesh(mesh.devices.reshape(16, 2, 2, tp), ("z", "xl", "core", "tp"))
    spec = P(("z", "xl", "core", "tp"), None)
    return jax.shard_map(
        shards, mesh=inner, in_specs=(spec,) * 4, out_specs=(spec,) * 4, check_vma=False
    )
```

time: 162 us -> 156 us (0.963)
  the two profiles are of different devices: /device:TPU:2 before, /device:TPU:1 now
where the time goes in v4:
time: 156 us
  starting transfers between devices  57.7 us (37%)
  blocking collectives  42.9 us (28%)
  waiting for transfers between devices  42.5 us (27%)
  Pallas kernels  6.35 us (4%)
  local copies, waits for them, and re-layouts  4.22 us (3%)
    ppermute x8, waiting for transfers between devices, shift(): return lax.ppermute(x, ('z', 'core'), route)  40.9 us
    ppermute x8, starting transfers between devices, shift(): return lax.ppermute(x, ('z', 'core'), route)  37.3 us
    ppermute x4, starting transfers between devices, other_core(): return lax.ppermute(x, 'core', [(0, 1), (1, 0)])  20.4 us
    all_to_all x1, blocking collectives, shards(): got = lax.all_to_all(sent, SIDE, split_axis=0, concat_axis=0, tiled=True)  17.5 us
    all_to_all x1, blocking collectives, shards(): back = lax.all_to_all(back, SIDE, split_axis=0, concat_axis=0, tiled=True)  14.4 us
    all_gather x1, blocking collectives, shards(): st_all = lax.all_gather(st, COLS, axis=0, tiled=False)  11 us
    pallas_call x4, Pallas kernels, call(): pl.pallas_call(kernel, out_shape=tuple((jax.ShapeDtypeStruct(s, d) for s,...  6.35 us
  transfers between devices with their start and end apart: 12, of which 8 were waited for; matrix products, arithmetic and copies ran while one was open for 0% of the time, Pallas kernels for 3%

profile of v4, /device:TPU:1, one launch (start us, length us, event | category | flops | bytes accessed | tf_op | source)
XLA Modules:
  0.0 155.5 jit_solution(2230295954213210593)
XLA Ops:
  0.6 0.9 copy.15
  1.6 0.0 copy-start
  1.6 0.0 copy-start.1
  1.6 1.0 copy.16
  2.6 0.2 copy.10
  2.7 0.1 broadcast_in_dim.2
  2.8 0.0 copy-done
  2.8 0.0 copy-done.1
  2.9 17.5 %all_to_all.10 = bf16[16,16,1152]{2,1,0:T(8,128)(2,1)S(1)} all-to-all(bf16[16,16,1152]{2,1,0:T(8,128)(2,1)S(1)} %bitcast.67), channel_id=1, replica_groups=mesh['z'=16,'xl'=2,'core'=2,'tp'=8] {'xl','tp'}, dimensions={0} | all-to-all | bytes 1179648 | tf_op jit(solution)/shard_map/all_to_all | solution.py:274
  20.4 5.0 %collective-permute-start.1 = (bf16[128,256]{1,0:T(8,128)(2,1)S(1)}, bf16[128,256]{1,0:T(8,128)(2,1)S(1)}, u32[]{:S(2)}, u32[]{:S(2)}) collective-permute-start(bf16[128,256]{1,0:T(8,128)(2,1)S(1)} %get-tuple-element.35), channel_id=1, source_target_pairs={{0,8},{8,0},{1,9},{9,1},{2,10},{10,2},{3,11},{11,3},{4,12},{12,4},... | collective-permute-start | bytes 196616 | tf_op jit(solution)/shard_map/ppermute | solution.py:254
  25.4 0.9 collective-permute-done.1
  26.3 12.5 %collective-permute-start.2 = (bf16[2,128,256]{2,1,0:T(8,128)(2,1)S(1)}, bf16[2,128,256]{2,1,0:T(8,128)(2,1)S(1)}, u32[]{:S(2)}, u32[]{:S(2)}) collective-permute-start(bf16[2,128,256]{2,1,0:T(8,128)(2,1)S(1)} %pad_maximum_fusion.3), channel_id=1, source_target_pairs={{0,128},{8,392},{32,160},{40,424},{64,192},{72,456},{96,224},{104,... | collective-permute-start | bytes 393224 | tf_op jit(solution)/shard_map/ppermute | solution.py:250
  38.8 6.1 %collective-permute-done.2 = bf16[2,128,256]{2,1,0:T(8,128)(2,1)S(1)} collective-permute-done((bf16[2,128,256]{2,1,0:T(8,128)(2,1)S(1)}, bf16[2,128,256]{2,1,0:T(8,128)(2,1)S(1)}, u32[]{:S(2)}, u32[]{:S(2)}) %collective-permute-start.2) | collective-permute-done | bytes 131104 | tf_op jit(solution)/shard_map/ppermute | solution.py:250
  44.9 4.4 %collective-permute-start.3 = (bf16[4,128,256]{2,1,0:T(8,128)(2,1)S(1)}, bf16[4,128,256]{2,1,0:T(8,128)(2,1)S(1)}, u32[]{:S(2)}, u32[]{:S(2)}) collective-permute-start(bf16[4,128,256]{2,1,0:T(8,128)(2,1)S(1)} %pad_maximum_fusion.1), channel_id=1, source_target_pairs={{0,64},{8,456},{32,96},{40,488},{64,128},{72,8},{96,160},{104,40},... | collective-permute-start | bytes 786440 | tf_op jit(solution)/shard_map/ppermute | solution.py:250
  49.4 0.1 slice.83
  49.4 1.9 %collective-permute-start = (bf16[256,1024]{1,0:T(8,128)(2,1)S(1)}, bf16[256,1024]{1,0:T(8,128)(2,1)S(1)}, u32[]{:S(2)}, u32[]{:S(2)}) collective-permute-start(bf16[256,1024]{1,0:T(8,128)(2,1)S(1)} %bitcast.58), channel_id=1, source_target_pairs={{0,8},{8,0},{1,9},{9,1},{2,10},{10,2},{3,11},{11,3},{4,12},{12,4},... | collective-permute-start | bytes 1572872 | tf_op jit(solution)/shard_map/ppermute | solution.py:254
  51.4 3.8 %collective-permute-done.3 = bf16[4,128,256]{2,1,0:T(8,128)(2,1)S(1)} collective-permute-done((bf16[4,128,256]{2,1,0:T(8,128)(2,1)S(1)}, bf16[4,128,256]{2,1,0:T(8,128)(2,1)S(1)}, u32[]{:S(2)}, u32[]{:S(2)}) %collective-permute-start.3) | collective-permute-done | bytes 262176 | tf_op jit(solution)/shard_map/ppermute | solution.py:250
  55.2 0.1 pad_maximum_fusion.kvs
  55.3 4.4 %collective-permute-start.4 = (bf16[8,128,256]{2,1,0:T(8,128)(2,1)S(1)}, bf16[8,128,256]{2,1,0:T(8,128)(2,1)S(1)}, u32[]{:S(2)}, u32[]{:S(2)}) collective-permute-start(bf16[8,128,256]{2,1,0:T(8,128)(2,1)S(1)} %pad_maximum_fusion.kvs), channel_id=1, source_target_pairs={{0,32},{8,488},{32,64},{40,8},{64,96},{72,40},{96,128},{104,72},{1... | collective-permute-start | bytes 1572872 | tf_op jit(solution)/shard_map/ppermute | solution.py:250
  59.7 4.8 %collective-permute-start.5 = (bf16[128,256]{1,0:T(8,128)(2,1)S(1)}, bf16[128,256]{1,0:T(8,128)(2,1)S(1)}, u32[]{:S(2)}, u32[]{:S(2)}) collective-permute-start(bf16[128,256]{1,0:T(8,128)(2,1)S(1)} %slice_bitcast_fusion.3), channel_id=1, source_target_pairs={{0,64},{8,456},{32,96},{40,488},{64,128},{72,8},{96,160},{104,40},... | collective-permute-start | bytes 196616 | tf_op jit(solution)/shard_map/ppermute | solution.py:250
  64.6 0.1 pad_add_fusion.idx
  64.6 0.0 collective-permute-done.qb
  64.6 1.8 %fwd_even.1 = (f32[8,512]{1,0:T(8,128)S(1)}, f32[4,128,512]{2,1,0:T(8,128)S(1)}) custom-call(s32[3]{0:T(128)S(1)} %pad_add_fusion.idx, bf16[256,1024]{1,0:T(8,128)(2,1)S(1)} %bitcast.59, bf16[256,1024]{1,0:T(8,128)(2,1)S(1)} %collective-permute-done.qb, bf16[8,128,256]{2,1,0:T(8,128)(2,1)S(1)} %pad_maximum_fusion.kvs), custom_call_target="tpu_custom_call" | custom-call | tf_op jit(solution)/shard_map/fwd_even/pallas_call | solution.py:236
  66.5 0.7 collective-permute-done.5.kv8
  67.2 0.0 collective-permute-done.4.kvs
  67.2 0.9 fwd_odd.1
  68.1 11.0 %all-gather = f32[64,512]{1,0:T(8,128)S(1)} all-gather(f32[16,512]{1,0:T(8,128)S(1)} %get-tuple-element.16.st_own), channel_id=2, replica_groups=mesh['z'=16,'xl'=2,'core'=2,'tp'=8] {'xl','core'}, dimensions={0}, use_global_device_ids=true | all-gather | bytes 163840 | tf_op jit(solution)/shard_map/all_gather | solution.py:301
  79.1 0.8 bwd_odd.1
  79.9 3.2 %collective-permute-start.7 = (bf16[8,128,256]{2,1,0:T(8,128)(2,1)S(1)}, bf16[8,128,256]{2,1,0:T(8,128)(2,1)S(1)}, u32[]{:S(2)}, u32[]{:S(2)}) collective-permute-start(bf16[8,128,256]{2,1,0:T(8,128)(2,1)S(1)} %get-tuple-element.22), channel_id=1, source_target_pairs={{0,480},{8,40},{32,0},{40,72},{64,32},{72,104},{96,64},{104,136},{... | collective-permute-start | bytes 1572872 | tf_op jit(solution)/shard_map/ppermute | solution.py:250
  83.2 4.1 %collective-permute-start.8 = (bf16[128,256]{1,0:T(8,128)(2,1)S(1)}, bf16[128,256]{1,0:T(8,128)(2,1)S(1)}, u32[]{:S(2)}, u32[]{:S(2)}) collective-permute-start(bf16[128,256]{1,0:T(8,128)(2,1)S(1)} %get-tuple-element.23), channel_id=1, source_target_pairs={{0,448},{8,72},{32,480},{40,104},{64,0},{72,136},{96,32},{104,168}... | collective-permute-start | bytes 196616 | tf_op jit(solution)/shard_map/ppermute | solution.py:250
  87.3 2.8 %bwd_even.1 = (f32[8,128,256]{2,1,0:T(8,128)S(1)}, bf16[256,1024]{1,0:T(8,128)(2,1)S(1)}, bf16[256,1024]{1,0:T(8,128)(2,1)S(1)}) custom-call(s32[3]{0:T(128)S(1)} %pad_add_fusion.idx, bf16[256,1024]{1,0:T(8,128)(2,1)S(1)} %bitcast.62, bf16[256,1024]{1,0:T(8,128)(2,1)S(1)} %collective-permute-done.qb, bf16[8,128,256]{2,1,0:T(8,128)(2,1)S(1)} %pad_maximum_fusion.kvs, ...), custom_call_target="tpu_custom_call" | custom-call | tf_op jit(solution)/shard_map/bwd_even/pallas_call | solution.py:236
  90.1 17.9 %collective-permute-done.7 = bf16[8,128,256]{2,1,0:T(8,128)(2,1)S(1)} collective-permute-done((bf16[8,128,256]{2,1,0:T(8,128)(2,1)S(1)}, bf16[8,128,256]{2,1,0:T(8,128)(2,1)S(1)}, u32[]{:S(2)}, u32[]{:S(2)}) %collective-permute-start.7) | collective-permute-done | bytes 524320 | tf_op jit(solution)/shard_map/ppermute | solution.py:250
  108.0 0.2 fusion.7
  108.2 2.2 %collective-permute-done.8 = bf16[128,256]{1,0:T(8,128)(2,1)S(1)} collective-permute-done((bf16[128,256]{1,0:T(8,128)(2,1)S(1)}, bf16[128,256]{1,0:T(8,128)(2,1)S(1)}, u32[]{:S(2)}, u32[]{:S(2)}) %collective-permute-start.8) | collective-permute-done | bytes 65568 | tf_op jit(solution)/shard_map/ppermute | solution.py:250
  110.5 1.9 %collective-permute-start.9 = (bf16[4,128,256]{2,1,0:T(8,128)(2,1)S(1)}, bf16[4,128,256]{2,1,0:T(8,128)(2,1)S(1)}, u32[]{:S(2)}, u32[]{:S(2)}) collective-permute-start(bf16[4,128,256]{2,1,0:T(8,128)(2,1)S(1)} %pad_maximum_fusion.2), channel_id=1, source_target_pairs={{0,448},{8,72},{32,480},{40,104},{64,0},{72,136},{96,32},{104,168}... | collective-permute-start | bytes 786440 | tf_op jit(solution)/shard_map/ppermute | solution.py:250
  112.4 10.1 %collective-permute-done.9 = bf16[4,128,256]{2,1,0:T(8,128)(2,1)S(1)} collective-permute-done((bf16[4,128,256]{2,1,0:T(8,128)(2,1)S(1)}, bf16[4,128,256]{2,1,0:T(8,128)(2,1)S(1)}, u32[]{:S(2)}, u32[]{:S(2)}) %collective-permute-start.9) | collective-permute-done | bytes 262176 | tf_op jit(solution)/shard_map/ppermute | solution.py:250
  122.5 0.1 slice_add_fusion
  122.6 1.9 %collective-permute-start.10 = (bf16[2,128,256]{2,1,0:T(8,128)(2,1)S(1)}, bf16[2,128,256]{2,1,0:T(8,128)(2,1)S(1)}, u32[]{:S(2)}, u32[]{:S(2)}) collective-permute-start(bf16[2,128,256]{2,1,0:T(8,128)(2,1)S(1)} %slice.124), channel_id=1, source_target_pairs={{0,384},{8,136},{32,416},{40,168},{64,448},{72,200},{96,480},{104,... | collective-permute-start | bytes 393224 | tf_op jit(solution)/shard_map/ppermute | solution.py:250
  124.5 8.8 %collective-permute-start.6 = (bf16[256,1024]{1,0:T(8,128)(2,1)S(1)}, bf16[256,1024]{1,0:T(8,128)(2,1)S(1)}, u32[]{:S(2)}, u32[]{:S(2)}) collective-permute-start(bf16[256,1024]{1,0:T(8,128)(2,1)S(1)} %get-tuple-element.20), channel_id=1, source_target_pairs={{0,8},{8,0},{1,9},{9,1},{2,10},{10,2},{3,11},{11,3},{4,12},{12,4},... | collective-permute-start | bytes 1572872 | tf_op jit(solution)/shard_map/ppermute | solution.py:254
  133.4 0.0 collective-permute-done.10
  133.4 4.6 %collective-permute-start.11 = (bf16[128,256]{1,0:T(8,128)(2,1)S(1)}, bf16[128,256]{1,0:T(8,128)(2,1)S(1)}, u32[]{:S(2)}, u32[]{:S(2)}) collective-permute-start(bf16[128,256]{1,0:T(8,128)(2,1)S(1)} %fusion.4), channel_id=1, source_target_pairs={{0,8},{8,0},{1,9},{9,1},{2,10},{10,2},{3,11},{11,3},{4,12},{12,4},... | collective-permute-start | bytes 196616 | tf_op jit(solution)/shard_map/ppermute | solution.py:254
  138.1 0.0 collective-permute-done.6
  138.1 0.2 add_convert_fusion
  138.3 0.7 collective-permute-done.11
  139.1 14.4 %all_to_all.11 = bf16[16,16,1152]{2,1,0:T(8,128)(2,1)S(1)} all-to-all(bf16[16,16,1152]{2,1,0:T(8,128)(2,1)S(1)} %maximum_maximum_fusion.1), channel_id=1, replica_groups=mesh['z'=16,'xl'=2,'core'=2,'tp'=8] {'xl','tp'}, dimensions={0} | all-to-all | bytes 1179648 | tf_op jit(solution)/shard_map/all_to_all | solution.py:329
  153.4 0.6 slice_bitcast_fusion.4
  154.1 0.1 slice_reduce_fusion
  154.2 0.7 copy.14
  154.8 0.7 copy.13
  (18 shorter events, 0.3 us)
Async XLA Ops:
  1.6 1.2 copy-start
  1.6 1.2 copy-start.1
  20.4 5.9 %collective-permute-start.1 = (bf16[128,256]{1,0:T(8,128)(2,1)S(1)}, bf16[128,256]{1,0:T(8,128)(2,1)S(1)}, u32[]{:S(2)}, u32[]{:S(2)}) collective-permute-start(bf16[128,256]{1,0:T(8,128)(2,1)S(1)} %get-tuple-element.35), channel_id=1, source_target_pairs={{0,8},{8,0},{1,9},{9,1},{2,10},{10,2},{3,11},{11,3},{4,12},{12,4},... | collective-permute-start | bytes 196616 | tf_op jit(solution)/shard_map/ppermute | solution.py:254
  26.3 18.6 %collective-permute-start.2 = (bf16[2,128,256]{2,1,0:T(8,128)(2,1)S(1)}, bf16[2,128,256]{2,1,0:T(8,128)(2,1)S(1)}, u32[]{:S(2)}, u32[]{:S(2)}) collective-permute-start(bf16[2,128,256]{2,1,0:T(8,128)(2,1)S(1)} %pad_maximum_fusion.3), channel_id=1, source_target_pairs={{0,128},{8,392},{32,160},{40,424},{64,192},{72,456},{96,224},{104,... | collective-permute-start | bytes 393224 | tf_op jit(solution)/shard_map/ppermute | solution.py:250
  44.9 10.3 %collective-permute-start.3 = (bf16[4,128,256]{2,1,0:T(8,128)(2,1)S(1)}, bf16[4,128,256]{2,1,0:T(8,128)(2,1)S(1)}, u32[]{:S(2)}, u32[]{:S(2)}) collective-permute-start(bf16[4,128,256]{2,1,0:T(8,128)(2,1)S(1)} %pad_maximum_fusion.1), channel_id=1, source_target_pairs={{0,64},{8,456},{32,96},{40,488},{64,128},{72,8},{96,160},{104,40},... | collective-permute-start | bytes 786440 | tf_op jit(solution)/shard_map/ppermute | solution.py:250
  49.4 15.2 %collective-permute-start = (bf16[256,1024]{1,0:T(8,128)(2,1)S(1)}, bf16[256,1024]{1,0:T(8,128)(2,1)S(1)}, u32[]{:S(2)}, u32[]{:S(2)}) collective-permute-start(bf16[256,1024]{1,0:T(8,128)(2,1)S(1)} %bitcast.58), channel_id=1, source_target_pairs={{0,8},{8,0},{1,9},{9,1},{2,10},{10,2},{3,11},{11,3},{4,12},{12,4},... | collective-permute-start | bytes 1572872 | tf_op jit(solution)/shard_map/ppermute | solution.py:254
  55.3 11.9 %collective-permute-start.4 = (bf16[8,128,256]{2,1,0:T(8,128)(2,1)S(1)}, bf16[8,128,256]{2,1,0:T(8,128)(2,1)S(1)}, u32[]{:S(2)}, u32[]{:S(2)}) collective-permute-start(bf16[8,128,256]{2,1,0:T(8,128)(2,1)S(1)} %pad_maximum_fusion.kvs), channel_id=1, source_target_pairs={{0,32},{8,488},{32,64},{40,8},{64,96},{72,40},{96,128},{104,72},{1... | collective-permute-start | bytes 1572872 | tf_op jit(solution)/shard_map/ppermute | solution.py:250
  59.7 7.5 %collective-permute-start.5 = (bf16[128,256]{1,0:T(8,128)(2,1)S(1)}, bf16[128,256]{1,0:T(8,128)(2,1)S(1)}, u32[]{:S(2)}, u32[]{:S(2)}) collective-permute-start(bf16[128,256]{1,0:T(8,128)(2,1)S(1)} %slice_bitcast_fusion.3), channel_id=1, source_target_pairs={{0,64},{8,456},{32,96},{40,488},{64,128},{72,8},{96,160},{104,40},... | collective-permute-start | bytes 196616 | tf_op jit(solution)/shard_map/ppermute | solution.py:250
  79.9 28.1 %collective-permute-start.7 = (bf16[8,128,256]{2,1,0:T(8,128)(2,1)S(1)}, bf16[8,128,256]{2,1,0:T(8,128)(2,1)S(1)}, u32[]{:S(2)}, u32[]{:S(2)}) collective-permute-start(bf16[8,128,256]{2,1,0:T(8,128)(2,1)S(1)} %get-tuple-element.22), channel_id=1, source_target_pairs={{0,480},{8,40},{32,0},{40,72},{64,32},{72,104},{96,64},{104,136},{... | collective-permute-start | bytes 1572872 | tf_op jit(solution)/shard_map/ppermute | solution.py:250
  83.2 27.2 %collective-permute-start.8 = (bf16[128,256]{1,0:T(8,128)(2,1)S(1)}, bf16[128,256]{1,0:T(8,128)(2,1)S(1)}, u32[]{:S(2)}, u32[]{:S(2)}) collective-permute-start(bf16[128,256]{1,0:T(8,128)(2,1)S(1)} %get-tuple-element.23), channel_id=1, source_target_pairs={{0,448},{8,72},{32,480},{40,104},{64,0},{72,136},{96,32},{104,168}... | collective-permute-start | bytes 196616 | tf_op jit(solution)/shard_map/ppermute | solution.py:250
  110.5 12.0 %collective-permute-start.9 = (bf16[4,128,256]{2,1,0:T(8,128)(2,1)S(1)}, bf16[4,128,256]{2,1,0:T(8,128)(2,1)S(1)}, u32[]{:S(2)}, u32[]{:S(2)}) collective-permute-start(bf16[4,128,256]{2,1,0:T(8,128)(2,1)S(1)} %pad_maximum_fusion.2), channel_id=1, source_target_pairs={{0,448},{8,72},{32,480},{40,104},{64,0},{72,136},{96,32},{104,168}... | collective-permute-start | bytes 786440 | tf_op jit(solution)/shard_map/ppermute | solution.py:250
  122.6 10.8 %collective-permute-start.10 = (bf16[2,128,256]{2,1,0:T(8,128)(2,1)S(1)}, bf16[2,128,256]{2,1,0:T(8,128)(2,1)S(1)}, u32[]{:S(2)}, u32[]{:S(2)}) collective-permute-start(bf16[2,128,256]{2,1,0:T(8,128)(2,1)S(1)} %slice.124), channel_id=1, source_target_pairs={{0,384},{8,136},{32,416},{40,168},{64,448},{72,200},{96,480},{104,... | collective-permute-start | bytes 393224 | tf_op jit(solution)/shard_map/ppermute | solution.py:250
  124.5 13.5 %collective-permute-start.6 = (bf16[256,1024]{1,0:T(8,128)(2,1)S(1)}, bf16[256,1024]{1,0:T(8,128)(2,1)S(1)}, u32[]{:S(2)}, u32[]{:S(2)}) collective-permute-start(bf16[256,1024]{1,0:T(8,128)(2,1)S(1)} %get-tuple-element.20), channel_id=1, source_target_pairs={{0,8},{8,0},{1,9},{9,1},{2,10},{10,2},{3,11},{11,3},{4,12},{12,4},... | collective-permute-start | bytes 1572872 | tf_op jit(solution)/shard_map/ppermute | solution.py:254
  133.4 5.5 %collective-permute-start.11 = (bf16[128,256]{1,0:T(8,128)(2,1)S(1)}, bf16[128,256]{1,0:T(8,128)(2,1)S(1)}, u32[]{:S(2)}, u32[]{:S(2)}) collective-permute-start(bf16[128,256]{1,0:T(8,128)(2,1)S(1)} %fusion.4), channel_id=1, source_target_pairs={{0,8},{8,0},{1,9},{9,1},{2,10},{10,2},{3,11},{11,3},{4,12},{12,4},... | collective-permute-start | bytes 196616 | tf_op jit(solution)/shard_map/ppermute | solution.py:254

commit v5 on v4

--- a/solution.py
+++ b/solution.py
@@ -13,6 +13,7 @@
 LOG2E = 1.4426950408889634
 C2 = SCALE * LOG2E
 NEG = -1e30
+DEAD = 2e30
 SIDE = ("xl", "tp")
 COLS = ("xl", "core")
 NT = (((1,), (1,)), ((), ()))
@@ -70,56 +71,77 @@
     return jnp.concatenate([lo, hi], axis=1)
 
 
-def attend(qa, qb, kv, ml, acc, mask=None):
+def gate(z, core, k, planes):
+    return jnp.where(is_live(z, core, k, planes), 0.0, DEAD).astype(F32)
+
+
+def attend(qa, qb, kv, spans, ml, acc):
     k, vt = kv[:, :D], kv[:, D:].T
+    ahead = dot(k, both(qa, qb, 0), NT)
     for h in range(G):
-        s = dot(k, both(qa, qb, h * D), NT)
-        if mask is not None:
-            s = jnp.where(mask, s, NEG)
+        s = ahead
+        if h + 1 < G:
+            ahead = dot(k, both(qa, qb, (h + 1) * D), NT)
         m_old = ml[h : h + 1, :]
-        m_new = jnp.maximum(m_old, jnp.max(s, axis=0, keepdims=True))
-        p = jnp.exp2((s - m_new) * C2)
+        m_new, at, cuts = m_old, 0, []
+        for size, shut, mask in spans:
+            cut = s[at : at + size]
+            if mask is not None:
+                cut = jnp.where(mask, cut, NEG)
+            top = jnp.max(cut, axis=0, keepdims=True)
+            m_new = jnp.maximum(m_new, top if shut is None else top - shut)
+            cuts.append(cut)
+            at += size
+        total, ps = jnp.zeros_like(m_old), []
+        for cut, (_, shut, _) in zip(cuts, spans):
+            p = jnp.exp2((cut - (m_new if shut is None else m_new + shut)) * C2)
+            total = total + jnp.sum(p, axis=0, keepdims=True)
+            ps.append(p.astype(BF))
         alpha = jnp.exp2((m_old - m_new) * C2)
         ml[h : h + 1, :] = m_new
-        ml[G + h : G + h + 1, :] = ml[G + h : G + h + 1, :] * alpha + jnp.sum(
-            p, axis=0, keepdims=True
-        )
-        acc[h] = acc[h] * alpha + dot(vt, p.astype(BF), NN)
-
-
-def attend_planes(idx, planes, order, first, qa, qb, kvs, ml, acc):
+        ml[G + h : G + h + 1, :] = ml[G + h : G + h + 1, :] * alpha + total
+        acc[h] = acc[h] * alpha + dot(vt, jnp.concatenate(ps, axis=0), NN)
+
+
+def fwd_even_kernel(planes, tok, idx, qa, qb, kvs, ml, acc):
     z, core = idx[0], idx[2]
+    rows = 2 * qa.shape[0]
     per = kvs.shape[1]
-
-    def plane(j, _):
-        @pl.when(is_live(z, core, distance(order, j), planes))
-        def _():
-            kv = kvs[pl.ds(2 * j, 2)].reshape(2 * per, 2 * D)
-            attend(qa, qb, kv, ml, acc)
-
-        return 0
-
-    lax.fori_loop(first, len(order), plane, 0)
-
-
-def fwd_even_kernel(planes, tok, idx, qa, qb, kvs, ml, acc):
-    rows = 2 * qa.shape[0]
+    shut = [gate(z, core, k, planes) for k in EVEN]
     ml[0:G, :] = jnp.full((G, rows), NEG, F32)
     ml[G:, :] = jnp.zeros((ml.shape[0] - G, rows), F32)
     acc[...] = jnp.zeros(acc.shape, F32)
-    attend(qa, qb, kvs[0], ml, acc, own_mask(idx, kvs.shape[1], rows, tok))
-    attend_planes(idx, planes, EVEN, 1, qa, qb, kvs, ml, acc)
+    kv = jnp.concatenate([kvs[0], kvs[2], kvs[3]], axis=0)
+    spans = ((per, None, own_mask(idx, per, rows, tok)), (2 * per, shut[1], None))
+    attend(qa, qb, kv, spans, ml, acc)
+
+    @pl.when(shut[2] + shut[3] < 2 * DEAD)
+    def _():
+        kv = kvs[4:].reshape(4 * per, 2 * D)
+        attend(qa, qb, kv, [(2 * per, s, None) for s in shut[2:]], ml, acc)
 
 
 def fwd_odd_kernel(planes, idx, qa, qb, kvs, kv8, ml_in, acc_in, o_out, st_out, ml, acc):
     z, core = idx[0], idx[2]
+    per = kvs.shape[1]
     ml[...] = ml_in[...]
     acc[...] = acc_in[...]
-    attend_planes(idx, planes, ODD, 0, qa, qb, kvs, ml, acc)
+
+    def pair(j, _):
+        shut = [gate(z, core, distance(ODD[i::2], j), planes) for i in range(2)]
+
+        @pl.when(shut[0] + shut[1] < 2 * DEAD)
+        def _():
+            kv = kvs[pl.ds(4 * j, 4)].reshape(4 * per, 2 * D)
+            attend(qa, qb, kv, [(2 * per, s, None) for s in shut], ml, acc)
+
+        return 0
+
+    lax.fori_loop(0, 2, pair, 0)
 
     @pl.when(is_live(z, core, planes // 2, planes))
     def _():
-        attend(qa, qb, kv8[...], ml, acc)
+        attend(qa, qb, kv8[...], [(per, None, None)], ml, acc)
 
     st_out[...] = jnp.zeros(st_out.shape, F32)
     for h in range(G):
@@ -151,74 +173,98 @@
         rows_s[G + h : G + h + 1, :] = delta
 
 
-def grads(qa, qb, kv, rows_s, dq, mask=None):
+def grads(qa, qb, kv, spans, rows_s, dq):
     k, v = kv[:, :D], kv[:, D:]
     kt = k.T
     dk = jnp.zeros(k.shape, F32)
     dv = jnp.zeros(k.shape, F32)
+
+    def products(h):
+        return dot(k, both(qa, qb, h * D), NT), dot(v, both(qa, qb, (G + h) * D), NT)
+
+    ahead = products(0)
     for h in range(G):
-        q, do = both(qa, qb, h * D), both(qa, qb, (G + h) * D)
-        s = dot(k, q, NT)
-        p = jnp.exp2(s * C2 - rows_s[h : h + 1, :])
-        if mask is not None:
-            p = jnp.where(mask, p, 0.0)
-        dv = dv + dot(p.astype(BF), do, NN)
-        dp = dot(v, do, NT)
-        ds = (p * (dp - rows_s[G + h : G + h + 1, :])).astype(BF)
-        dk = dk + dot(ds, q, NN)
+        s, dp = ahead
+        if h + 1 < G:
+            ahead = products(h + 1)
+        lse2, delta = rows_s[h : h + 1, :], rows_s[G + h : G + h + 1, :]
+        ps, dss, at = [], [], 0
+        for size, shut, mask in spans:
+            p = jnp.exp2(s[at : at + size] * C2 - (lse2 if shut is None else lse2 + shut))
+            if mask is not None:
+                p = jnp.where(mask, p, 0.0)
+            ps.append(p.astype(BF))
+            dss.append((p * (dp[at : at + size] - delta)).astype(BF))
+            at += size
+        ds = jnp.concatenate(dss, axis=0)
+        dv = dv + dot(jnp.concatenate(ps, axis=0), both(qa, qb, (G + h) * D), NN)
+        dk = dk + dot(ds, both(qa, qb, h * D), NN)
         dq[h] += dot(kt, ds, NN)
     return jnp.concatenate([dk * SCALE, dv], axis=1)
 
 
-def grad_planes(idx, planes, order, first, qa, qb, kvs, rows_s, dq, g_out):
-    z, core = idx[0], idx[2]
+def grad_pair(qa, qb, kvs, at, shut, rows_s, dq, g_out):
     per = kvs.shape[1]
-
-    def plane(j, _):
-        live = is_live(z, core, distance(order, j), planes)
-
-        @pl.when(live)
-        def _():
-            kv = kvs[pl.ds(2 * j, 2)].reshape(2 * per, 2 * D)
-            g = grads(qa, qb, kv, rows_s, dq)
-            g_out[pl.ds(2 * j, 2)] = g.reshape(2, per, 2 * D).astype(g_out.dtype)
-
-        @pl.when(jnp.logical_not(live))
-        def _():
-            g_out[pl.ds(2 * j, 2)] = jnp.zeros((2, per, 2 * D), g_out.dtype)
-
-        return 0
-
-    lax.fori_loop(first, len(order), plane, 0)
+    live = shut[0] + shut[1] < 2 * DEAD
+
+    @pl.when(live)
+    def _():
+        kv = kvs[pl.ds(at, 4)].reshape(4 * per, 2 * D)
+        g = grads(qa, qb, kv, [(2 * per, s, None) for s in shut], rows_s, dq)
+        g_out[pl.ds(at, 4)] = g.reshape(4, per, 2 * D).astype(g_out.dtype)
+
+    @pl.when(jnp.logical_not(live))
+    def _():
+        g_out[pl.ds(at, 4)] = jnp.zeros((4, per, 2 * D), g_out.dtype)
 
 
 def bwd_odd_kernel(planes, idx, qa, qb, kvs, kv8, st_all, g_out, g8_out, dq, rows_s):
     z, core = idx[0], idx[2]
     store_stats(st_all, core, rows_s)
     dq[...] = jnp.zeros(dq.shape, F32)
-    grad_planes(idx, planes, ODD, 0, qa, qb, kvs, rows_s, dq, g_out)
+
+    def pair(j, _):
+        shut = [gate(z, core, distance(ODD[i::2], j), planes) for i in range(2)]
+        grad_pair(qa, qb, kvs, 4 * j, shut, rows_s, dq, g_out)
+        return 0
+
+    lax.fori_loop(0, 2, pair, 0)
     live = is_live(z, core, planes // 2, planes)
 
     @pl.when(live)
     def _():
-        g8_out[...] = grads(qa, qb, kv8[...], rows_s, dq).astype(g8_out.dtype)
+        spans = [(kv8.shape[0], None, None)]
+        g8_out[...] = grads(qa, qb, kv8[...], spans, rows_s, dq).astype(g8_out.dtype)
 
     @pl.when(jnp.logical_not(live))
     def _():
         g8_out[...] = jnp.zeros(g8_out.shape, g8_out.dtype)
 
 
-def bwd_even_kernel(
-    planes, tok, idx, qa, qb, kvs, st_own, st_all, o_in, dq_in, g_out, od_a, od_b, dq, rows_s
-):
-    core = idx[2]
-    half = qa.shape[0]
+def bwd_26_kernel(planes, idx, qa, qb, kvs, st_all, dq_in, g_out, dq, rows_s):
+    z, core = idx[0], idx[2]
     store_stats(st_all, core, rows_s)
     dq[...] = dq_in[...]
-    mask = own_mask(idx, kvs.shape[1], 2 * half, tok)
-    g_out[0] = grads(qa, qb, kvs[0], rows_s, dq, mask)
-    g_out[1] = jnp.zeros(kvs.shape[1:], F32)
-    grad_planes(idx, planes, EVEN, 1, qa, qb, kvs, rows_s, dq, g_out)
+    shut = [gate(z, core, k, planes) for k in EVEN[2:]]
+    grad_pair(qa, qb, kvs, 0, shut, rows_s, dq, g_out)
+
+
+def bwd_04_kernel(
+    planes, tok, idx, qa, qb, kvs, st_own, st_all, o_in, dq_in, near, g_out, od_a, od_b, dq, rows_s
+):
+    z, core = idx[0], idx[2]
+    half = qa.shape[0]
+    per = kvs.shape[1]
+    store_stats(st_all, core, rows_s)
+    dq[...] = dq_in[...]
+    mask = own_mask(idx, per, 2 * half, tok)
+    spans = ((per, None, mask), (2 * per, gate(z, core, EVEN[1], planes), None))
+    kv = jnp.concatenate([kvs[0], kvs[2], kvs[3]], axis=0)
+    g = grads(qa, qb, kv, spans, rows_s, dq)
+    g_out[0] = g[:per] + near[0].astype(F32)
+    g_out[1] = near[1].astype(F32)
+    g_out[2] = g[per : 2 * per] + near[2].astype(F32)
+    g_out[3] = g[2 * per :] + near[3].astype(F32)
     for h in range(G):
         top, inv, _, _ = joined_stats(st_all, core, h)
         m_own = get_row(st_own, h, core)
@@ -239,7 +285,7 @@
         in_specs=[pl.BlockSpec(memory_space=pltpu.SMEM)] + [vm] * (len(args) - 1),
         out_specs=(vm,) * len(out_shape),
         scratch_shapes=[pltpu.VMEM(s, F32) for s in scratch],
-        compiler_params=pltpu.CompilerParams(vmem_limit_bytes=40 << 20),
+        compiler_params=pltpu.CompilerParams(vmem_limit_bytes=44 << 20),
         name=name,
     )(*args)
 
@@ -307,19 +353,26 @@
         ((2 * G, rows),),
     )
     near, near8 = shift(g_odd, -1), shift(g8, -2)
-    g_even, od_a, od_b = call(
-        functools.partial(bwd_even_kernel, planes, tok),
-        "bwd_even",
-        ((even.shape, F32), (qa.shape, BF), (qa.shape, BF)),
-        (idx, qa, qb, even, st, st_all, o, dq),
+    g_26, dq = call(
+        functools.partial(bwd_26_kernel, planes),
+        "bwd_26",
+        ((even[4:].shape, F32), heads),
+        (idx, qa, qb, even[4:], st_all, dq),
+        ((2 * G, rows),),
+    )
+    g_04, od_a, od_b = call(
+        functools.partial(bwd_04_kernel, planes, tok),
+        "bwd_04",
+        ((at04.shape, F32), (qa.shape, BF), (qa.shape, BF)),
+        (idx, qa, qb, at04, st, st_all, o, dq, near[:4]),
         ((G, D, rows), (2 * G, rows)),
     )
     od = od_a.astype(F32) + other_core(od_b).astype(F32)
     od = od.astype(BF).reshape(nx * tp, tok, 2 * hw)
 
-    g_even = g_even + near.astype(F32)
-    g26 = jnp.concatenate([g_even[4:6], g_even[6:7] + near8[None].astype(F32), g_even[7:]])
-    g04 = g_even[:4] + shift(g26.astype(BF), -2).astype(F32)
+    g_26 = g_26 + near[4:].astype(F32)
+    g_26 = jnp.concatenate([g_26[:2], g_26[2:3] + near8[None].astype(F32), g_26[3:]])
+    g04 = g_04 + shift(g_26.astype(BF), -2).astype(F32)
     g0 = g04[:2] + shift(g04[2:].astype(BF), -4).astype(F32)
     gkv = g0[0] + other_core(g0[1].astype(BF)).astype(F32)
     gkv = gkv.astype(BF).reshape(nx * tp, share, 2 * D)

time: 156 us -> 150 us (0.962)
  starting transfers between devices: 57.7 us -> 52.1 us
  waiting for transfers between devices: 42.5 us -> 40.5 us
    ppermute x4, starting transfers between devices: 20.4 us -> 14.3 us  [other_core(): return lax.ppermute(x, 'core', [(0, 1), (1, 0)])]
    ppermute x8, waiting for transfers between devices: 40.9 us -> 38.8 us  [shift(): return lax.ppermute(x, ('z', 'core'), route)]
    pallas_call x4 -> x5, Pallas kernels: 6.35 us -> 7.73 us  [call(): pl.pallas_call(kernel, out_shape=tuple((jax.ShapeDtypeStruct(s, d) for s,...]
  transfers between devices with their start and end apart: 12 -> 12, of which waited for: 8 -> 9; matrix products, arithmetic and copies ran while one was open for 0% -> 0% of each run, Pallas kernels for 3% -> 4%
where the time goes in v5:
time: 150 us; the launch traced here: 149 us
  starting transfers between devices  52.1 us (35%)
  blocking collectives  42.9 us (29%)
  waiting for transfers between devices  40.5 us (27%)
  Pallas kernels  7.73 us (5%)
  local copies, waits for them, and re-layouts  4.23 us (3%)
    ppermute x8, waiting for transfers between devices, shift(): return lax.ppermute(x, ('z', 'core'), route)  38.8 us
    ppermute x8, starting transfers between devices, shift(): return lax.ppermute(x, ('z', 'core'), route)  37.9 us
    all_to_all x1, blocking collectives, shards(): got = lax.all_to_all(sent, SIDE, split_axis=0, concat_axis=0, tiled=True)  17.5 us
    all_to_all x1, blocking collectives, shards(): back = lax.all_to_all(back, SIDE, split_axis=0, concat_axis=0, tiled=True)  14.4 us
    ppermute x4, starting transfers between devices, other_core(): return lax.ppermute(x, 'core', [(0, 1), (1, 0)])  14.3 us
    all_gather x1, blocking collectives, shards(): st_all = lax.all_gather(st, COLS, axis=0, tiled=False)  11 us
    pallas_call x5, Pallas kernels, call(): pl.pallas_call(kernel, out_shape=tuple((jax.ShapeDtypeStruct(s, d) for s,...  7.73 us
  transfers between devices with their start and end apart: 12, of which 9 were waited for; matrix products, arithmetic and copies ran while one was open for 0% of the time, Pallas kernels for 4%

profile of v5, /device:TPU:1, one launch (start us, length us, event | category | flops | bytes accessed | tf_op | source)
XLA Modules:
  0.0 149.3 jit_solution(16383973629242109897)
XLA Ops:
  0.6 0.9 copy.15
  1.6 0.0 copy-start
  1.6 0.0 copy-start.1
  1.6 1.0 copy.16
  2.6 0.2 copy.10
  2.7 0.1 broadcast_in_dim.2
  2.8 0.0 copy-done
  2.8 0.0 copy-done.1
  2.9 17.5 %all_to_all.10 = bf16[16,16,1152]{2,1,0:T(8,128)(2,1)S(1)} all-to-all(bf16[16,16,1152]{2,1,0:T(8,128)(2,1)S(1)} %bitcast.69), channel_id=1, replica_groups=mesh['z'=16,'xl'=2,'core'=2,'tp'=8] {'xl','tp'}, dimensions={0} | all-to-all | bytes 1179648 | tf_op jit(solution)/shard_map/all_to_all | solution.py:320
  20.4 5.0 %collective-permute-start.1 = (bf16[128,256]{1,0:T(8,128)(2,1)S(1)}, bf16[128,256]{1,0:T(8,128)(2,1)S(1)}, u32[]{:S(2)}, u32[]{:S(2)}) collective-permute-start(bf16[128,256]{1,0:T(8,128)(2,1)S(1)} %get-tuple-element.39), channel_id=1, source_target_pairs={{0,8},{8,0},{1,9},{9,1},{2,10},{10,2},{3,11},{11,3},{4,12},{12,4},... | collective-permute-start | bytes 196616 | tf_op jit(solution)/shard_map/ppermute | solution.py:300
  25.4 0.9 collective-permute-done.1
  26.3 12.5 %collective-permute-start.2 = (bf16[2,128,256]{2,1,0:T(8,128)(2,1)S(1)}, bf16[2,128,256]{2,1,0:T(8,128)(2,1)S(1)}, u32[]{:S(2)}, u32[]{:S(2)}) collective-permute-start(bf16[2,128,256]{2,1,0:T(8,128)(2,1)S(1)} %pad_maximum_fusion.3), channel_id=1, source_target_pairs={{0,128},{8,392},{32,160},{40,424},{64,192},{72,456},{96,224},{104,... | collective-permute-start | bytes 393224 | tf_op jit(solution)/shard_map/ppermute | solution.py:296
  38.8 6.1 %collective-permute-done.2 = bf16[2,128,256]{2,1,0:T(8,128)(2,1)S(1)} collective-permute-done((bf16[2,128,256]{2,1,0:T(8,128)(2,1)S(1)}, bf16[2,128,256]{2,1,0:T(8,128)(2,1)S(1)}, u32[]{:S(2)}, u32[]{:S(2)}) %collective-permute-start.2) | collective-permute-done | bytes 131104 | tf_op jit(solution)/shard_map/ppermute | solution.py:296
  44.9 4.4 %collective-permute-start.3 = (bf16[4,128,256]{2,1,0:T(8,128)(2,1)S(1)}, bf16[4,128,256]{2,1,0:T(8,128)(2,1)S(1)}, u32[]{:S(2)}, u32[]{:S(2)}) collective-permute-start(bf16[4,128,256]{2,1,0:T(8,128)(2,1)S(1)} %pad_maximum_fusion.1.kvs), channel_id=1, source_target_pairs={{0,64},{8,456},{32,96},{40,488},{64,128},{72,8},{96,160},{104,40},... | collective-permute-start | bytes 786440 | tf_op jit(solution)/shard_map/ppermute | solution.py:296
  49.4 0.1 slice.87
  49.4 1.9 %collective-permute-start = (bf16[256,1024]{1,0:T(8,128)(2,1)S(1)}, bf16[256,1024]{1,0:T(8,128)(2,1)S(1)}, u32[]{:S(2)}, u32[]{:S(2)}) collective-permute-start(bf16[256,1024]{1,0:T(8,128)(2,1)S(1)} %bitcast.58), channel_id=1, source_target_pairs={{0,8},{8,0},{1,9},{9,1},{2,10},{10,2},{3,11},{11,3},{4,12},{12,4},... | collective-permute-start | bytes 1572872 | tf_op jit(solution)/shard_map/ppermute | solution.py:300
  51.4 3.9 %collective-permute-done.3.kvs = bf16[4,128,256]{2,1,0:T(8,128)(2,1)S(1)} collective-permute-done((bf16[4,128,256]{2,1,0:T(8,128)(2,1)S(1)}, bf16[4,128,256]{2,1,0:T(8,128)(2,1)S(1)}, u32[]{:S(2)}, u32[]{:S(2)}) %collective-permute-start.3) | collective-permute-done | bytes 262176 | tf_op jit(solution)/shard_map/ppermute | solution.py:296
  55.2 0.1 pad_maximum_fusion.kvs
  55.3 4.4 %collective-permute-start.4 = (bf16[8,128,256]{2,1,0:T(8,128)(2,1)S(1)}, bf16[8,128,256]{2,1,0:T(8,128)(2,1)S(1)}, u32[]{:S(2)}, u32[]{:S(2)}) collective-permute-start(bf16[8,128,256]{2,1,0:T(8,128)(2,1)S(1)} %pad_maximum_fusion.kvs), channel_id=1, source_target_pairs={{0,32},{8,488},{32,64},{40,8},{64,96},{72,40},{96,128},{104,72},{1... | collective-permute-start | bytes 1572872 | tf_op jit(solution)/shard_map/ppermute | solution.py:296
  59.7 4.8 %collective-permute-start.5 = (bf16[128,256]{1,0:T(8,128)(2,1)S(1)}, bf16[128,256]{1,0:T(8,128)(2,1)S(1)}, u32[]{:S(2)}, u32[]{:S(2)}) collective-permute-start(bf16[128,256]{1,0:T(8,128)(2,1)S(1)} %slice_bitcast_fusion.3), channel_id=1, source_target_pairs={{0,64},{8,456},{32,96},{40,488},{64,128},{72,8},{96,160},{104,40},... | collective-permute-start | bytes 196616 | tf_op jit(solution)/shard_map/ppermute | solution.py:296
  64.6 0.1 pad_add_fusion.idx
  64.6 0.0 collective-permute-done.qb
  64.6 2.1 %fwd_even.1 = (f32[8,512]{1,0:T(8,128)S(1)}, f32[4,128,512]{2,1,0:T(8,128)S(1)}) custom-call(s32[3]{0:T(128)S(1)} %pad_add_fusion.idx, bf16[256,1024]{1,0:T(8,128)(2,1)S(1)} %bitcast.59, bf16[256,1024]{1,0:T(8,128)(2,1)S(1)} %collective-permute-done.qb, bf16[8,128,256]{2,1,0:T(8,128)(2,1)S(1)} %pad_maximum_fusion.kvs), custom_call_target="tpu_custom_call" | custom-call | tf_op jit(solution)/shard_map/fwd_even/pallas_call | solution.py:282
  66.7 0.5 collective-permute-done.5.kv8
  67.2 0.0 collective-permute-done.4.kvs
  67.2 0.9 fwd_odd.1
  68.1 11.0 %all-gather = f32[64,512]{1,0:T(8,128)S(1)} all-gather(f32[16,512]{1,0:T(8,128)S(1)} %get-tuple-element.18.st_own), channel_id=2, replica_groups=mesh['z'=16,'xl'=2,'core'=2,'tp'=8] {'xl','core'}, dimensions={0}, use_global_device_ids=true | all-gather | bytes 163840 | tf_op jit(solution)/shard_map/all_gather | solution.py:347
  79.1 0.8 bwd_odd.1
  79.9 3.6 %collective-permute-start.6 = (bf16[8,128,256]{2,1,0:T(8,128)(2,1)S(1)}, bf16[8,128,256]{2,1,0:T(8,128)(2,1)S(1)}, u32[]{:S(2)}, u32[]{:S(2)}) collective-permute-start(bf16[8,128,256]{2,1,0:T(8,128)(2,1)S(1)} %get-tuple-element.22), channel_id=1, source_target_pairs={{0,480},{8,40},{32,0},{40,72},{64,32},{72,104},{96,64},{104,136},{... | collective-permute-start | bytes 1572872 | tf_op jit(solution)/shard_map/ppermute | solution.py:296
  83.5 4.2 %collective-permute-start.8 = (bf16[128,256]{1,0:T(8,128)(2,1)S(1)}, bf16[128,256]{1,0:T(8,128)(2,1)S(1)}, u32[]{:S(2)}, u32[]{:S(2)}) collective-permute-start(bf16[128,256]{1,0:T(8,128)(2,1)S(1)} %get-tuple-element.27), channel_id=1, source_target_pairs={{0,448},{8,72},{32,480},{40,104},{64,0},{72,136},{96,32},{104,168}... | collective-permute-start | bytes 196616 | tf_op jit(solution)/shard_map/ppermute | solution.py:296
  87.7 0.9 bwd_26.1
  88.7 13.2 %collective-permute-done.6 = bf16[8,128,256]{2,1,0:T(8,128)(2,1)S(1)} collective-permute-done((bf16[8,128,256]{2,1,0:T(8,128)(2,1)S(1)}, bf16[8,128,256]{2,1,0:T(8,128)(2,1)S(1)}, u32[]{:S(2)}, u32[]{:S(2)}) %collective-permute-start.6) | collective-permute-done | bytes 524320 | tf_op jit(solution)/shard_map/ppermute | solution.py:296
  101.8 0.1 fusion.7
  101.9 2.3 %collective-permute-done.8 = bf16[128,256]{1,0:T(8,128)(2,1)S(1)} collective-permute-done((bf16[128,256]{1,0:T(8,128)(2,1)S(1)}, bf16[128,256]{1,0:T(8,128)(2,1)S(1)}, u32[]{:S(2)}, u32[]{:S(2)}) %collective-permute-start.8) | collective-permute-done | bytes 65568 | tf_op jit(solution)/shard_map/ppermute | solution.py:296
  104.3 1.9 %collective-permute-start.9 = (bf16[4,128,256]{2,1,0:T(8,128)(2,1)S(1)}, bf16[4,128,256]{2,1,0:T(8,128)(2,1)S(1)}, u32[]{:S(2)}, u32[]{:S(2)}) collective-permute-start(bf16[4,128,256]{2,1,0:T(8,128)(2,1)S(1)} %pad_maximum_fusion.2), channel_id=1, source_target_pairs={{0,448},{8,72},{32,480},{40,104},{64,0},{72,136},{96,32},{104,168}... | collective-permute-start | bytes 786440 | tf_op jit(solution)/shard_map/ppermute | solution.py:296
  106.3 3.1 %bwd_04.1 = (f32[4,128,256]{2,1,0:T(8,128)S(1)}, bf16[256,1024]{1,0:T(8,128)(2,1)S(1)}, bf16[256,1024]{1,0:T(8,128)(2,1)S(1)}) custom-call(s32[3]{0:T(128)S(1)} %pad_add_fusion.idx, bf16[256,1024]{1,0:T(8,128)(2,1)S(1)} %bitcast.63, bf16[256,1024]{1,0:T(8,128)(2,1)S(1)} %collective-permute-done.qb, bf16[4,128,256]{2,1,0:T(8,128)(2,1)S(1)} %pad_maximum_fusion.1.kvs, ...), custom_call_target="tpu_custom_call" | custom-call | tf_op jit(solution)/shard_map/bwd_04/pallas_call | solution.py:282
  109.4 6.9 %collective-permute-done.9 = bf16[4,128,256]{2,1,0:T(8,128)(2,1)S(1)} collective-permute-done((bf16[4,128,256]{2,1,0:T(8,128)(2,1)S(1)}, bf16[4,128,256]{2,1,0:T(8,128)(2,1)S(1)}, u32[]{:S(2)}, u32[]{:S(2)}) %collective-permute-start.9) | collective-permute-done | bytes 262176 | tf_op jit(solution)/shard_map/ppermute | solution.py:296
  116.2 0.1 convert_add_fusion
  116.3 1.9 %collective-permute-start.10 = (bf16[2,128,256]{2,1,0:T(8,128)(2,1)S(1)}, bf16[2,128,256]{2,1,0:T(8,128)(2,1)S(1)}, u32[]{:S(2)}, u32[]{:S(2)}) collective-permute-start(bf16[2,128,256]{2,1,0:T(8,128)(2,1)S(1)} %slice.129), channel_id=1, source_target_pairs={{0,384},{8,136},{32,416},{40,168},{64,448},{72,200},{96,480},{104,... | collective-permute-start | bytes 393224 | tf_op jit(solution)/shard_map/ppermute | solution.py:296
  118.3 4.9 %collective-permute-start.7 = (bf16[256,1024]{1,0:T(8,128)(2,1)S(1)}, bf16[256,1024]{1,0:T(8,128)(2,1)S(1)}, u32[]{:S(2)}, u32[]{:S(2)}) collective-permute-start(bf16[256,1024]{1,0:T(8,128)(2,1)S(1)} %get-tuple-element.24), channel_id=1, source_target_pairs={{0,8},{8,0},{1,9},{9,1},{2,10},{10,2},{3,11},{11,3},{4,12},{12,4},... | collective-permute-start | bytes 1572872 | tf_op jit(solution)/shard_map/ppermute | solution.py:300
  123.2 6.0 %collective-permute-done.10 = bf16[2,128,256]{2,1,0:T(8,128)(2,1)S(1)} collective-permute-done((bf16[2,128,256]{2,1,0:T(8,128)(2,1)S(1)}, bf16[2,128,256]{2,1,0:T(8,128)(2,1)S(1)}, u32[]{:S(2)}, u32[]{:S(2)}) %collective-permute-start.10) | collective-permute-done | bytes 131104 | tf_op jit(solution)/shard_map/ppermute | solution.py:296
  129.2 2.4 %collective-permute-start.11 = (bf16[128,256]{1,0:T(8,128)(2,1)S(1)}, bf16[128,256]{1,0:T(8,128)(2,1)S(1)}, u32[]{:S(2)}, u32[]{:S(2)}) collective-permute-start(bf16[128,256]{1,0:T(8,128)(2,1)S(1)} %fusion.4), channel_id=1, source_target_pairs={{0,8},{8,0},{1,9},{9,1},{2,10},{10,2},{3,11},{11,3},{4,12},{12,4},... | collective-permute-start | bytes 196616 | tf_op jit(solution)/shard_map/ppermute | solution.py:300
  131.6 0.9 collective-permute-done.11
  132.6 0.0 collective-permute-done.7
  132.6 0.2 add_convert_fusion
  132.8 14.4 %all_to_all.11 = bf16[16,16,1152]{2,1,0:T(8,128)(2,1)S(1)} all-to-all(bf16[16,16,1152]{2,1,0:T(8,128)(2,1)S(1)} %maximum_maximum_fusion.1), channel_id=1, replica_groups=mesh['z'=16,'xl'=2,'core'=2,'tp'=8] {'xl','tp'}, dimensions={0} | all-to-all | bytes 1179648 | tf_op jit(solution)/shard_map/all_to_all | solution.py:382
  147.2 0.6 slice_bitcast_fusion.4
  147.8 0.1 slice_reduce_fusion
  147.9 0.7 copy.14
  148.6 0.7 copy.13
  (19 shorter events, 0.4 us)
Async XLA Ops:
  1.6 1.2 copy-start
  1.6 1.2 copy-start.1
  20.4 5.9 %collective-permute-start.1 = (bf16[128,256]{1,0:T(8,128)(2,1)S(1)}, bf16[128,256]{1,0:T(8,128)(2,1)S(1)}, u32[]{:S(2)}, u32[]{:S(2)}) collective-permute-start(bf16[128,256]{1,0:T(8,128)(2,1)S(1)} %get-tuple-element.39), channel_id=1, source_target_pairs={{0,8},{8,0},{1,9},{9,1},{2,10},{10,2},{3,11},{11,3},{4,12},{12,4},... | collective-permute-start | bytes 196616 | tf_op jit(solution)/shard_map/ppermute | solution.py:300
  26.3 18.6 %collective-permute-start.2 = (bf16[2,128,256]{2,1,0:T(8,128)(2,1)S(1)}, bf16[2,128,256]{2,1,0:T(8,128)(2,1)S(1)}, u32[]{:S(2)}, u32[]{:S(2)}) collective-permute-start(bf16[2,128,256]{2,1,0:T(8,128)(2,1)S(1)} %pad_maximum_fusion.3), channel_id=1, source_target_pairs={{0,128},{8,392},{32,160},{40,424},{64,192},{72,456},{96,224},{104,... | collective-permute-start | bytes 393224 | tf_op jit(solution)/shard_map/ppermute | solution.py:296
  44.9 10.3 %collective-permute-start.3 = (bf16[4,128,256]{2,1,0:T(8,128)(2,1)S(1)}, bf16[4,128,256]{2,1,0:T(8,128)(2,1)S(1)}, u32[]{:S(2)}, u32[]{:S(2)}) collective-permute-start(bf16[4,128,256]{2,1,0:T(8,128)(2,1)S(1)} %pad_maximum_fusion.1.kvs), channel_id=1, source_target_pairs={{0,64},{8,456},{32,96},{40,488},{64,128},{72,8},{96,160},{104,40},... | collective-permute-start | bytes 786440 | tf_op jit(solution)/shard_map/ppermute | solution.py:296
  49.4 15.2 %collective-permute-start = (bf16[256,1024]{1,0:T(8,128)(2,1)S(1)}, bf16[256,1024]{1,0:T(8,128)(2,1)S(1)}, u32[]{:S(2)}, u32[]{:S(2)}) collective-permute-start(bf16[256,1024]{1,0:T(8,128)(2,1)S(1)} %bitcast.58), channel_id=1, source_target_pairs={{0,8},{8,0},{1,9},{9,1},{2,10},{10,2},{3,11},{11,3},{4,12},{12,4},... | collective-permute-start | bytes 1572872 | tf_op jit(solution)/shard_map/ppermute | solution.py:300
  55.3 11.9 %collective-permute-start.4 = (bf16[8,128,256]{2,1,0:T(8,128)(2,1)S(1)}, bf16[8,128,256]{2,1,0:T(8,128)(2,1)S(1)}, u32[]{:S(2)}, u32[]{:S(2)}) collective-permute-start(bf16[8,128,256]{2,1,0:T(8,128)(2,1)S(1)} %pad_maximum_fusion.kvs), channel_id=1, source_target_pairs={{0,32},{8,488},{32,64},{40,8},{64,96},{72,40},{96,128},{104,72},{1... | collective-permute-start | bytes 1572872 | tf_op jit(solution)/shard_map/ppermute | solution.py:296
  59.7 7.5 %collective-permute-start.5 = (bf16[128,256]{1,0:T(8,128)(2,1)S(1)}, bf16[128,256]{1,0:T(8,128)(2,1)S(1)}, u32[]{:S(2)}, u32[]{:S(2)}) collective-permute-start(bf16[128,256]{1,0:T(8,128)(2,1)S(1)} %slice_bitcast_fusion.3), channel_id=1, source_target_pairs={{0,64},{8,456},{32,96},{40,488},{64,128},{72,8},{96,160},{104,40},... | collective-permute-start | bytes 196616 | tf_op jit(solution)/shard_map/ppermute | solution.py:296
  79.9 21.9 %collective-permute-start.6 = (bf16[8,128,256]{2,1,0:T(8,128)(2,1)S(1)}, bf16[8,128,256]{2,1,0:T(8,128)(2,1)S(1)}, u32[]{:S(2)}, u32[]{:S(2)}) collective-permute-start(bf16[8,128,256]{2,1,0:T(8,128)(2,1)S(1)} %get-tuple-element.22), channel_id=1, source_target_pairs={{0,480},{8,40},{32,0},{40,72},{64,32},{72,104},{96,64},{104,136},{... | collective-permute-start | bytes 1572872 | tf_op jit(solution)/shard_map/ppermute | solution.py:296
  83.5 20.8 %collective-permute-start.8 = (bf16[128,256]{1,0:T(8,128)(2,1)S(1)}, bf16[128,256]{1,0:T(8,128)(2,1)S(1)}, u32[]{:S(2)}, u32[]{:S(2)}) collective-permute-start(bf16[128,256]{1,0:T(8,128)(2,1)S(1)} %get-tuple-element.27), channel_id=1, source_target_pairs={{0,448},{8,72},{32,480},{40,104},{64,0},{72,136},{96,32},{104,168}... | collective-permute-start | bytes 196616 | tf_op jit(solution)/shard_map/ppermute | solution.py:296
  104.3 11.9 %collective-permute-start.9 = (bf16[4,128,256]{2,1,0:T(8,128)(2,1)S(1)}, bf16[4,128,256]{2,1,0:T(8,128)(2,1)S(1)}, u32[]{:S(2)}, u32[]{:S(2)}) collective-permute-start(bf16[4,128,256]{2,1,0:T(8,128)(2,1)S(1)} %pad_maximum_fusion.2), channel_id=1, source_target_pairs={{0,448},{8,72},{32,480},{40,104},{64,0},{72,136},{96,32},{104,168}... | collective-permute-start | bytes 786440 | tf_op jit(solution)/shard_map/ppermute | solution.py:296
  116.3 12.8 %collective-permute-start.10 = (bf16[2,128,256]{2,1,0:T(8,128)(2,1)S(1)}, bf16[2,128,256]{2,1,0:T(8,128)(2,1)S(1)}, u32[]{:S(2)}, u32[]{:S(2)}) collective-permute-start(bf16[2,128,256]{2,1,0:T(8,128)(2,1)S(1)} %slice.129), channel_id=1, source_target_pairs={{0,384},{8,136},{32,416},{40,168},{64,448},{72,200},{96,480},{104,... | collective-permute-start | bytes 393224 | tf_op jit(solution)/shard_map/ppermute | solution.py:296
  118.3 14.3 %collective-permute-start.7 = (bf16[256,1024]{1,0:T(8,128)(2,1)S(1)}, bf16[256,1024]{1,0:T(8,128)(2,1)S(1)}, u32[]{:S(2)}, u32[]{:S(2)}) collective-permute-start(bf16[256,1024]{1,0:T(8,128)(2,1)S(1)} %get-tuple-element.24), channel_id=1, source_target_pairs={{0,8},{8,0},{1,9},{9,1},{2,10},{10,2},{3,11},{11,3},{4,12},{12,4},... | collective-permute-start | bytes 1572872 | tf_op jit(solution)/shard_map/ppermute | solution.py:300
  129.2 3.3 %collective-permute-start.11 = (bf16[128,256]{1,0:T(8,128)(2,1)S(1)}, bf16[128,256]{1,0:T(8,128)(2,1)S(1)}, u32[]{:S(2)}, u32[]{:S(2)}) collective-permute-start(bf16[128,256]{1,0:T(8,128)(2,1)S(1)} %fusion.4), channel_id=1, source_target_pairs={{0,8},{8,0},{1,9},{9,1},{2,10},{10,2},{3,11},{11,3},{4,12},{12,4},... | collective-permute-start | bytes 196616 | tf_op jit(solution)/shard_map/ppermute | solution.py:300

commit v6 on v5

--- a/solution.py
+++ b/solution.py
@@ -33,13 +33,6 @@
     return jnp.where(core == 0, k <= z, k >= planes - z)
 
 
-def distance(order, j):
-    k = jnp.int32(order[0])
-    for i in range(1, len(order)):
-        k = jnp.where(j == i, order[i], k)
-    return k
-
-
 def own_mask(idx, per, rows, tok):
     xl, core = idx[1], idx[2]
     share = tok // 2
@@ -71,8 +64,9 @@
     return jnp.concatenate([lo, hi], axis=1)
 
 
-def gate(z, core, k, planes):
-    return jnp.where(is_live(z, core, k, planes), 0.0, DEAD).astype(F32)
+def gates(idx, planes, order):
+    live = [is_live(idx[0], idx[2], k, planes) for k in order]
+    return [jnp.where(x, 0.0, DEAD).astype(F32) for x in live], functools.reduce(jnp.logical_or, live)
 
 
 def attend(qa, qb, kv, spans, ml, acc):
@@ -103,45 +97,39 @@
         acc[h] = acc[h] * alpha + dot(vt, jnp.concatenate(ps, axis=0), NN)
 
 
-def fwd_even_kernel(planes, tok, idx, qa, qb, kvs, ml, acc):
-    z, core = idx[0], idx[2]
+def fwd_even_kernel(planes, tok, idx, qa, qb, mine, other, ml, acc):
     rows = 2 * qa.shape[0]
-    per = kvs.shape[1]
-    shut = [gate(z, core, k, planes) for k in EVEN]
+    per = mine.shape[1]
+    shut, live = gates(idx, planes, EVEN[1:])
+    spans = [(per, s, None) for s in shut]
     ml[0:G, :] = jnp.full((G, rows), NEG, F32)
     ml[G:, :] = jnp.zeros((ml.shape[0] - G, rows), F32)
     acc[...] = jnp.zeros(acc.shape, F32)
-    kv = jnp.concatenate([kvs[0], kvs[2], kvs[3]], axis=0)
-    spans = ((per, None, own_mask(idx, per, rows, tok)), (2 * per, shut[1], None))
-    attend(qa, qb, kv, spans, ml, acc)
-
-    @pl.when(shut[2] + shut[3] < 2 * DEAD)
-    def _():
-        kv = kvs[4:].reshape(4 * per, 2 * D)
-        attend(qa, qb, kv, [(2 * per, s, None) for s in shut[2:]], ml, acc)
-
-
-def fwd_odd_kernel(planes, idx, qa, qb, kvs, kv8, ml_in, acc_in, o_out, st_out, ml, acc):
-    z, core = idx[0], idx[2]
-    per = kvs.shape[1]
+    own = (per, None, own_mask(idx, per, rows, tok))
+    attend(qa, qb, mine[...].reshape(-1, 2 * D), [own] + spans, ml, acc)
+
+    @pl.when(live)
+    def _():
+        attend(qa, qb, other[1:].reshape(-1, 2 * D), spans, ml, acc)
+
+
+def fwd_odd_kernel(planes, idx, qa, qb, mine, other, kv8, ml_in, acc_in, o_out, st_out, ml, acc):
+    core = idx[2]
+    per = mine.shape[1]
     ml[...] = ml_in[...]
     acc[...] = acc_in[...]
-
-    def pair(j, _):
-        shut = [gate(z, core, distance(ODD[i::2], j), planes) for i in range(2)]
-
-        @pl.when(shut[0] + shut[1] < 2 * DEAD)
-        def _():
-            kv = kvs[pl.ds(4 * j, 4)].reshape(4 * per, 2 * D)
-            attend(qa, qb, kv, [(2 * per, s, None) for s in shut], ml, acc)
-
-        return 0
-
-    lax.fori_loop(0, 2, pair, 0)
-
-    @pl.when(is_live(z, core, planes // 2, planes))
-    def _():
-        attend(qa, qb, kv8[...], [(per, None, None)], ml, acc)
+    shut, live = gates(idx, planes, ODD)
+    shut8, live8 = gates(idx, planes, (planes // 2,))
+    spans = [(per, s, None) for s in shut]
+
+    @pl.when(live)
+    def _():
+        attend(qa, qb, other[...].reshape(-1, 2 * D), spans, ml, acc)
+
+    @pl.when(jnp.logical_or(live, live8))
+    def _():
+        kv = jnp.concatenate([mine[...].reshape(-1, 2 * D), kv8[...]], axis=0)
+        attend(qa, qb, kv, spans + [(per, shut8[0], None)], ml, acc)
 
     st_out[...] = jnp.zeros(st_out.shape, F32)
     for h in range(G):
@@ -203,68 +191,76 @@
     return jnp.concatenate([dk * SCALE, dv], axis=1)
 
 
-def grad_pair(qa, qb, kvs, at, shut, rows_s, dq, g_out):
-    per = kvs.shape[1]
-    live = shut[0] + shut[1] < 2 * DEAD
+def zero_all(refs):
+    for ref in refs:
+        ref[...] = jnp.zeros(ref.shape, ref.dtype)
+
+
+def bwd_odd_other_kernel(planes, idx, qa, qb, other, st_all, g_out, dq, rows_s):
+    per = other.shape[1]
+    store_stats(st_all, idx[2], rows_s)
+    dq[...] = jnp.zeros(dq.shape, F32)
+    shut, live = gates(idx, planes, ODD)
 
     @pl.when(live)
     def _():
-        kv = kvs[pl.ds(at, 4)].reshape(4 * per, 2 * D)
-        g = grads(qa, qb, kv, [(2 * per, s, None) for s in shut], rows_s, dq)
-        g_out[pl.ds(at, 4)] = g.reshape(4, per, 2 * D).astype(g_out.dtype)
+        spans = [(per, s, None) for s in shut]
+        g = grads(qa, qb, other[...].reshape(-1, 2 * D), spans, rows_s, dq)
+        g_out[...] = g.reshape(g_out.shape).astype(g_out.dtype)
 
     @pl.when(jnp.logical_not(live))
     def _():
-        g_out[pl.ds(at, 4)] = jnp.zeros((4, per, 2 * D), g_out.dtype)
-
-
-def bwd_odd_kernel(planes, idx, qa, qb, kvs, kv8, st_all, g_out, g8_out, dq, rows_s):
-    z, core = idx[0], idx[2]
-    store_stats(st_all, core, rows_s)
-    dq[...] = jnp.zeros(dq.shape, F32)
-
-    def pair(j, _):
-        shut = [gate(z, core, distance(ODD[i::2], j), planes) for i in range(2)]
-        grad_pair(qa, qb, kvs, 4 * j, shut, rows_s, dq, g_out)
-        return 0
-
-    lax.fori_loop(0, 2, pair, 0)
-    live = is_live(z, core, planes // 2, planes)
+        zero_all((g_out,))
+
+
+def bwd_odd_mine_kernel(planes, idx, qa, qb, mine, kv8, st_all, dq_in, g_out, g8_out, dq, rows_s):
+    per = mine.shape[1]
+    store_stats(st_all, idx[2], rows_s)
+    dq[...] = dq_in[...]
+    shut, live = gates(idx, planes, ODD + (planes // 2,))
 
     @pl.when(live)
     def _():
-        spans = [(kv8.shape[0], None, None)]
-        g8_out[...] = grads(qa, qb, kv8[...], spans, rows_s, dq).astype(g8_out.dtype)
+        spans = [(per, s, None) for s in shut]
+        kv = jnp.concatenate([mine[...].reshape(-1, 2 * D), kv8[...]], axis=0)
+        g = grads(qa, qb, kv, spans, rows_s, dq)
+        g_out[...] = g[: 4 * per].reshape(g_out.shape).astype(g_out.dtype)
+        g8_out[...] = g[4 * per :].astype(g8_out.dtype)
 
     @pl.when(jnp.logical_not(live))
     def _():
-        g8_out[...] = jnp.zeros(g8_out.shape, g8_out.dtype)
-
-
-def bwd_26_kernel(planes, idx, qa, qb, kvs, st_all, dq_in, g_out, dq, rows_s):
-    z, core = idx[0], idx[2]
+        zero_all((g_out, g8_out))
+
+
+def bwd_even_other_kernel(planes, idx, qa, qb, other, st_all, dq_in, g_out, dq, rows_s):
+    per = other.shape[1]
+    store_stats(st_all, idx[2], rows_s)
+    dq[...] = dq_in[...]
+    shut, live = gates(idx, planes, EVEN[1:])
+
+    @pl.when(live)
+    def _():
+        spans = [(per, s, None) for s in shut]
+        g = grads(qa, qb, other[1:].reshape(-1, 2 * D), spans, rows_s, dq)
+        g_out[...] = g.reshape(g_out.shape)
+
+    @pl.when(jnp.logical_not(live))
+    def _():
+        zero_all((g_out,))
+
+
+def bwd_even_mine_kernel(
+    planes, tok, idx, qa, qb, mine, st_own, st_all, o_in, dq_in, g_out, od_a, od_b, dq, rows_s
+):
+    core = idx[2]
+    half = qa.shape[0]
+    per = mine.shape[1]
     store_stats(st_all, core, rows_s)
     dq[...] = dq_in[...]
-    shut = [gate(z, core, k, planes) for k in EVEN[2:]]
-    grad_pair(qa, qb, kvs, 0, shut, rows_s, dq, g_out)
-
-
-def bwd_04_kernel(
-    planes, tok, idx, qa, qb, kvs, st_own, st_all, o_in, dq_in, near, g_out, od_a, od_b, dq, rows_s
-):
-    z, core = idx[0], idx[2]
-    half = qa.shape[0]
-    per = kvs.shape[1]
-    store_stats(st_all, core, rows_s)
-    dq[...] = dq_in[...]
-    mask = own_mask(idx, per, 2 * half, tok)
-    spans = ((per, None, mask), (2 * per, gate(z, core, EVEN[1], planes), None))
-    kv = jnp.concatenate([kvs[0], kvs[2], kvs[3]], axis=0)
-    g = grads(qa, qb, kv, spans, rows_s, dq)
-    g_out[0] = g[:per] + near[0].astype(F32)
-    g_out[1] = near[1].astype(F32)
-    g_out[2] = g[per : 2 * per] + near[2].astype(F32)
-    g_out[3] = g[2 * per :] + near[3].astype(F32)
+    shut, _ = gates(idx, planes, EVEN[1:])
+    spans = [(per, None, own_mask(idx, per, 2 * half, tok))] + [(per, s, None) for s in shut]
+    g = grads(qa, qb, mine[...].reshape(-1, 2 * D), spans, rows_s, dq)
+    g_out[...] = g.reshape(g_out.shape)
     for h in range(G):
         top, inv, _, _ = joined_stats(st_all, core, h)
         m_own = get_row(st_own, h, core)
@@ -322,59 +318,73 @@
     kv = got[:, :, 2 * hw :]
     kv = jnp.concatenate([kv[:, :share], kv[:, share:]], axis=2).reshape(nx * tp * share, 2 * D)
 
-    at0 = jnp.stack([kv, other_core(kv)])
-    at4 = shift(at0, 4)
+    def gathered(x):
+        at04 = jnp.stack([x, shift(x, 4)])
+        even = jnp.concatenate([at04, shift(at04, 2)])
+        return even, shift(even, 1)
+
+    even_m, odd_m = gathered(kv)
+    even_o, odd_o = gathered(other_core(kv))
+    at8 = shift(even_m[3], 2)
     qb = other_core(qa)
-    at04 = jnp.concatenate([at0, at4])
-    even = jnp.concatenate([at04, shift(at04, 2)])
-    odd = shift(even, 1)
-    at8 = shift(even[6], 2)
 
     heads = ((G, D, rows), F32)
+    blocks = even_m.shape
     ml, acc = call(
         functools.partial(fwd_even_kernel, planes, tok),
         "fwd_even",
         (((2 * G, rows), F32), heads),
-        (idx, qa, qb, even),
+        (idx, qa, qb, even_m, even_o),
     )
     o, st = call(
         functools.partial(fwd_odd_kernel, planes),
         "fwd_odd",
         (heads, ((16, rows), F32)),
-        (idx, qa, qb, odd, at8, ml, acc),
+        (idx, qa, qb, odd_m, odd_o, at8, ml, acc),
         ((2 * G, rows), (G, D, rows)),
     )
     st_all = lax.all_gather(st, COLS, axis=0, tiled=False)
-    g_odd, g8, dq = call(
-        functools.partial(bwd_odd_kernel, planes),
-        "bwd_odd",
-        ((odd.shape, BF), (at8.shape, BF), heads),
-        (idx, qa, qb, odd, at8, st_all),
+    g_odd_o, dq = call(
+        functools.partial(bwd_odd_other_kernel, planes),
+        "bwd_odd_o",
+        ((blocks, BF), heads),
+        (idx, qa, qb, odd_o, st_all),
         ((2 * G, rows),),
     )
-    near, near8 = shift(g_odd, -1), shift(g8, -2)
-    g_26, dq = call(
-        functools.partial(bwd_26_kernel, planes),
-        "bwd_26",
-        ((even[4:].shape, F32), heads),
-        (idx, qa, qb, even[4:], st_all, dq),
+    near_o = shift(g_odd_o, -1).astype(F32)
+    g_odd_m, g8, dq = call(
+        functools.partial(bwd_odd_mine_kernel, planes),
+        "bwd_odd_m",
+        ((blocks, BF), (at8.shape, BF), heads),
+        (idx, qa, qb, odd_m, at8, st_all, dq),
         ((2 * G, rows),),
     )
-    g_04, od_a, od_b = call(
-        functools.partial(bwd_04_kernel, planes, tok),
-        "bwd_04",
-        ((at04.shape, F32), (qa.shape, BF), (qa.shape, BF)),
-        (idx, qa, qb, at04, st, st_all, o, dq, near[:4]),
+    near_m, near8 = shift(g_odd_m, -1).astype(F32), shift(g8, -2).astype(F32)
+    g_o, dq = call(
+        functools.partial(bwd_even_other_kernel, planes),
+        "bwd_even_o",
+        (((3, *blocks[1:]), F32), heads),
+        (idx, qa, qb, even_o, st_all, dq),
+        ((2 * G, rows),),
+    )
+    far_o = shift((g_o[1:] + near_o[2:]).astype(BF), -2).astype(F32)
+    g_m, od_a, od_b = call(
+        functools.partial(bwd_even_mine_kernel, planes, tok),
+        "bwd_even_m",
+        ((blocks, F32), (qa.shape, BF), (qa.shape, BF)),
+        (idx, qa, qb, even_m, st, st_all, o, dq),
         ((G, D, rows), (2 * G, rows)),
     )
     od = od_a.astype(F32) + other_core(od_b).astype(F32)
     od = od.astype(BF).reshape(nx * tp, tok, 2 * hw)
 
-    g_26 = g_26 + near[4:].astype(F32)
-    g_26 = jnp.concatenate([g_26[:2], g_26[2:3] + near8[None].astype(F32), g_26[3:]])
-    g04 = g_04 + shift(g_26.astype(BF), -2).astype(F32)
-    g0 = g04[:2] + shift(g04[2:].astype(BF), -4).astype(F32)
-    gkv = g0[0] + other_core(g0[1].astype(BF)).astype(F32)
+    g_m = g_m + near_m
+    far_m = jnp.stack([g_m[2], g_m[3] + near8]).astype(BF)
+    far_m = shift(far_m, -2).astype(F32)
+    last_o = shift((g_o[0] + near_o[1] + far_o[1]).astype(BF), -4).astype(F32)
+    last_m = shift((g_m[1] + far_m[1]).astype(BF), -4).astype(F32)
+    gkv_o = other_core((near_o[0] + far_o[0] + last_o).astype(BF)).astype(F32)
+    gkv = g_m[0] + far_m[0] + last_m + gkv_o
     gkv = gkv.astype(BF).reshape(nx * tp, share, 2 * D)
     gkv = jnp.concatenate([gkv[:, :, :D], gkv[:, :, D:]], axis=1)
 

time: 150 us -> 149 us (level)
  waiting for transfers between devices: 40.5 us -> 7.87 us
  starting transfers between devices: 52.1 us -> 83.7 us
  blocking collectives: 42.9 us -> 41 us
    ppermute x8 -> x14, waiting for transfers between devices: 38.8 us -> 6.06 us  [shift(): return lax.ppermute(x, ('z', 'core'), route)]
    ppermute x8 -> x14, starting transfers between devices: 37.9 us -> 66.6 us  [shift(): return lax.ppermute(x, ('z', 'core'), route)]
    ppermute x4, starting transfers between devices: 14.3 us -> 17.1 us  [other_core(): return lax.ppermute(x, 'core', [(0, 1), (1, 0)])]
    all_gather x1, blocking collectives: 11 us -> 8.87 us  [shards(): st_all = lax.all_gather(st, COLS, axis=0, tiled=False)]
    pallas_call x5 -> x6, Pallas kernels: 7.73 us -> 9.16 us  [call(): pl.pallas_call(kernel, out_shape=tuple((jax.ShapeDtypeStruct(s, d) for s,...]
  transfers between devices with their start and end apart: 12 -> 18, of which waited for: 9 -> 4; matrix products, arithmetic and copies ran while one was open for 0% -> 0% of each run, Pallas kernels for 4% -> 5%
where the time goes in v6:
time: 149 us; the launch traced here: 148 us
  starting transfers between devices  83.7 us (56%)
  blocking collectives  41 us (28%)
  Pallas kernels  9.16 us (6%)
  waiting for transfers between devices  7.87 us (5%)
  local copies, waits for them, and re-layouts  4.18 us (3%)
    ppermute x14, starting transfers between devices, shift(): return lax.ppermute(x, ('z', 'core'), route)  66.6 us
    all_to_all x1, blocking collectives, shards(): got = lax.all_to_all(sent, SIDE, split_axis=0, concat_axis=0, tiled=True)  17.5 us
    ppermute x4, starting transfers between devices, other_core(): return lax.ppermute(x, 'core', [(0, 1), (1, 0)])  17.1 us
    all_to_all x1, blocking collectives, shards(): back = lax.all_to_all(back, SIDE, split_axis=0, concat_axis=0, tiled=True)  14.6 us
    pallas_call x6, Pallas kernels, call(): pl.pallas_call(kernel, out_shape=tuple((jax.ShapeDtypeStruct(s, d) for s,...  9.16 us
    all_gather x1, blocking collectives, shards(): st_all = lax.all_gather(st, COLS, axis=0, tiled=False)  8.87 us
    ppermute x14, waiting for transfers between devices, shift(): return lax.ppermute(x, ('z', 'core'), route)  6.06 us
  transfers between devices with their start and end apart: 18, of which 4 were waited for; matrix products, arithmetic and copies ran while one was open for 0% of the time, Pallas kernels for 5%

profile of v6, /device:TPU:1, one launch (start us, length us, event | category | flops | bytes accessed | tf_op | source)
XLA Modules:
  0.0 147.9 jit_solution(6979264028978957109)
XLA Ops:
  0.6 0.9 copy.15
  1.6 0.0 copy-start
  1.6 0.0 copy-start.1
  1.6 1.0 copy.16
  2.6 0.2 copy.10
  2.7 0.1 broadcast_in_dim.2
  2.8 0.0 copy-done
  2.8 0.0 copy-done.1
  2.9 17.5 %all_to_all.10 = bf16[16,16,1152]{2,1,0:T(8,128)(2,1)S(1)} all-to-all(bf16[16,16,1152]{2,1,0:T(8,128)(2,1)S(1)} %bitcast.90), channel_id=1, replica_groups=mesh['z'=16,'xl'=2,'core'=2,'tp'=8] {'xl','tp'}, dimensions={0} | all-to-all | bytes 1179648 | tf_op jit(solution)/shard_map/all_to_all | solution.py:316
  20.4 5.0 %collective-permute-start.4 = (bf16[128,256]{1,0:T(8,128)(2,1)S(1)}, bf16[128,256]{1,0:T(8,128)(2,1)S(1)}, u32[]{:S(2)}, u32[]{:S(2)}) collective-permute-start(bf16[128,256]{1,0:T(8,128)(2,1)S(1)} %get-tuple-element.41), channel_id=1, source_target_pairs={{0,8},{8,0},{1,9},{9,1},{2,10},{10,2},{3,11},{11,3},{4,12},{12,4},... | collective-permute-start | bytes 196616 | tf_op jit(solution)/shard_map/ppermute | solution.py:296
  25.4 12.5 %collective-permute-start.1 = (bf16[128,256]{1,0:T(8,128)(2,1)S(1)}, bf16[128,256]{1,0:T(8,128)(2,1)S(1)}, u32[]{:S(2)}, u32[]{:S(2)}) collective-permute-start(bf16[128,256]{1,0:T(8,128)(2,1)S(1)} %get-tuple-element.41), channel_id=1, source_target_pairs={{0,128},{8,392},{32,160},{40,424},{64,192},{72,456},{96,224},{104,... | collective-permute-start | bytes 196616 | tf_op jit(solution)/shard_map/ppermute | solution.py:292
  37.9 0.0 collective-permute-done.4
  37.9 5.2 %collective-permute-start.5 = (bf16[128,256]{1,0:T(8,128)(2,1)S(1)}, bf16[128,256]{1,0:T(8,128)(2,1)S(1)}, u32[]{:S(2)}, u32[]{:S(2)}) collective-permute-start(bf16[128,256]{1,0:T(8,128)(2,1)S(1)} %collective-permute-done.4), channel_id=1, source_target_pairs={{0,128},{8,392},{32,160},{40,424},{64,192},{72,456},{96,224},{104,... | collective-permute-start | bytes 196616 | tf_op jit(solution)/shard_map/ppermute | solution.py:292
  43.1 0.0 collective-permute-done.1
  43.1 3.9 %collective-permute-start.2 = (bf16[2,128,256]{2,1,0:T(8,128)(2,1)S(1)}, bf16[2,128,256]{2,1,0:T(8,128)(2,1)S(1)}, u32[]{:S(2)}, u32[]{:S(2)}) collective-permute-start(bf16[2,128,256]{2,1,0:T(8,128)(2,1)S(1)} %pad_maximum_fusion.2), channel_id=1, source_target_pairs={{0,64},{8,456},{32,96},{40,488},{64,128},{72,8},{96,160},{104,40},... | collective-permute-start | bytes 393224 | tf_op jit(solution)/shard_map/ppermute | solution.py:292
  47.0 0.5 collective-permute-done.5
  47.6 5.6 %collective-permute-start.6 = (bf16[2,128,256]{2,1,0:T(8,128)(2,1)S(1)}, bf16[2,128,256]{2,1,0:T(8,128)(2,1)S(1)}, u32[]{:S(2)}, u32[]{:S(2)}) collective-permute-start(bf16[2,128,256]{2,1,0:T(8,128)(2,1)S(1)} %pad_maximum_fusion.3), channel_id=1, source_target_pairs={{0,64},{8,456},{32,96},{40,488},{64,128},{72,8},{96,160},{104,40},... | collective-permute-start | bytes 393224 | tf_op jit(solution)/shard_map/ppermute | solution.py:292
  53.2 0.1 slice.100
  53.3 1.9 %collective-permute-start = (bf16[256,1024]{1,0:T(8,128)(2,1)S(1)}, bf16[256,1024]{1,0:T(8,128)(2,1)S(1)}, u32[]{:S(2)}, u32[]{:S(2)}) collective-permute-start(bf16[256,1024]{1,0:T(8,128)(2,1)S(1)} %bitcast.77), channel_id=1, source_target_pairs={{0,8},{8,0},{1,9},{9,1},{2,10},{10,2},{3,11},{11,3},{4,12},{12,4},... | collective-permute-start | bytes 1572872 | tf_op jit(solution)/shard_map/ppermute | solution.py:296
  55.2 0.0 collective-permute-done.2
  55.3 2.3 %collective-permute-start.3 = (bf16[4,128,256]{2,1,0:T(8,128)(2,1)S(1)}, bf16[4,128,256]{2,1,0:T(8,128)(2,1)S(1)}, u32[]{:S(2)}, u32[]{:S(2)}) collective-permute-start(bf16[4,128,256]{2,1,0:T(8,128)(2,1)S(1)} %pad_maximum_fusion.mine), channel_id=1, source_target_pairs={{0,32},{8,488},{32,64},{40,8},{64,96},{72,40},{96,128},{104,72},{1... | collective-permute-start | bytes 786440 | tf_op jit(solution)/shard_map/ppermute | solution.py:292
  57.6 0.0 collective-permute-done.6
  57.6 2.6 %collective-permute-start.7 = (bf16[4,128,256]{2,1,0:T(8,128)(2,1)S(1)}, bf16[4,128,256]{2,1,0:T(8,128)(2,1)S(1)}, u32[]{:S(2)}, u32[]{:S(2)}) collective-permute-start(bf16[4,128,256]{2,1,0:T(8,128)(2,1)S(1)} %pad_maximum_fusion.1.other), channel_id=1, source_target_pairs={{0,32},{8,488},{32,64},{40,8},{64,96},{72,40},{96,128},{104,72},{1... | collective-permute-start | bytes 786440 | tf_op jit(solution)/shard_map/ppermute | solution.py:292
  60.2 4.0 %collective-permute-start.8 = (bf16[128,256]{1,0:T(8,128)(2,1)S(1)}, bf16[128,256]{1,0:T(8,128)(2,1)S(1)}, u32[]{:S(2)}, u32[]{:S(2)}) collective-permute-start(bf16[128,256]{1,0:T(8,128)(2,1)S(1)} %slice_bitcast_fusion.3), channel_id=1, source_target_pairs={{0,64},{8,456},{32,96},{40,488},{64,128},{72,8},{96,160},{104,40},... | collective-permute-start | bytes 196616 | tf_op jit(solution)/shard_map/ppermute | solution.py:292
  64.2 0.1 pad_add_fusion.idx
  64.3 0.0 collective-permute-done.qb
  64.3 2.2 %fwd_even.1 = (f32[8,512]{1,0:T(8,128)S(1)}, f32[4,128,512]{2,1,0:T(8,128)S(1)}) custom-call(s32[3]{0:T(128)S(1)} %pad_add_fusion.idx, bf16[256,1024]{1,0:T(8,128)(2,1)S(1)} %bitcast.78, bf16[256,1024]{1,0:T(8,128)(2,1)S(1)} %collective-permute-done.qb, bf16[4,128,256]{2,1,0:T(8,128)(2,1)S(1)} %pad_maximum_fusion.mine, ...), custom_call_target="tpu_custom_call" | custom-call | tf_op jit(solution)/shard_map/fwd_even/pallas_call | solution.py:278
  66.4 0.4 collective-permute-done.8.kv8
  66.8 0.0 collective-permute-done.3.mine
  66.8 0.0 collective-permute-done.7.other
  66.8 0.9 fwd_odd.1
  67.7 8.9 %all-gather = f32[64,512]{1,0:T(8,128)S(1)} all-gather(f32[16,512]{1,0:T(8,128)S(1)} %get-tuple-element.20.st_own), channel_id=2, replica_groups=mesh['z'=16,'xl'=2,'core'=2,'tp'=8] {'xl','core'}, dimensions={0}, use_global_device_ids=true | all-gather | bytes 163840 | tf_op jit(solution)/shard_map/all_gather | solution.py:346
  76.6 0.7 bwd_odd_o.1
  77.3 7.2 %collective-permute-start.14 = (bf16[4,128,256]{2,1,0:T(8,128)(2,1)S(1)}, bf16[4,128,256]{2,1,0:T(8,128)(2,1)S(1)}, u32[]{:S(2)}, u32[]{:S(2)}) collective-permute-start(bf16[4,128,256]{2,1,0:T(8,128)(2,1)S(1)} %get-tuple-element.30), channel_id=1, source_target_pairs={{0,480},{8,40},{32,0},{40,72},{64,32},{72,104},{96,64},{104,136},{... | collective-permute-start | bytes 786440 | tf_op jit(solution)/shard_map/ppermute | solution.py:292
  84.6 0.9 bwd_odd_m.1
  85.5 2.9 %collective-permute-start.10 = (bf16[4,128,256]{2,1,0:T(8,128)(2,1)S(1)}, bf16[4,128,256]{2,1,0:T(8,128)(2,1)S(1)}, u32[]{:S(2)}, u32[]{:S(2)}) collective-permute-start(bf16[4,128,256]{2,1,0:T(8,128)(2,1)S(1)} %get-tuple-element.28), channel_id=1, source_target_pairs={{0,480},{8,40},{32,0},{40,72},{64,32},{72,104},{96,64},{104,136},{... | collective-permute-start | bytes 786440 | tf_op jit(solution)/shard_map/ppermute | solution.py:292
  88.4 4.4 %collective-permute-start.11 = (bf16[128,256]{1,0:T(8,128)(2,1)S(1)}, bf16[128,256]{1,0:T(8,128)(2,1)S(1)}, u32[]{:S(2)}, u32[]{:S(2)}) collective-permute-start(bf16[128,256]{1,0:T(8,128)(2,1)S(1)} %get-tuple-element.29), channel_id=1, source_target_pairs={{0,448},{8,72},{32,480},{40,104},{64,0},{72,136},{96,32},{104,168}... | collective-permute-start | bytes 196616 | tf_op jit(solution)/shard_map/ppermute | solution.py:292
  92.8 0.7 bwd_even_o.1
  93.5 3.8 %bwd_even_m.1 = (f32[4,128,256]{2,1,0:T(8,128)S(1)}, bf16[256,1024]{1,0:T(8,128)(2,1)S(1)}, bf16[256,1024]{1,0:T(8,128)(2,1)S(1)}) custom-call(s32[3]{0:T(128)S(1)} %pad_add_fusion.idx, bf16[256,1024]{1,0:T(8,128)(2,1)S(1)} %bitcast.83, bf16[256,1024]{1,0:T(8,128)(2,1)S(1)} %collective-permute-done.qb, bf16[4,128,256]{2,1,0:T(8,128)(2,1)S(1)} %pad_maximum_fusion.mine, ...), custom_call_target="tpu_custom_call" | custom-call | tf_op jit(solution)/shard_map/bwd_even_m/pallas_call | solution.py:278
  97.3 0.0 collective-permute-done.14
  97.4 1.9 %collective-permute-start.15 = (bf16[2,128,256]{2,1,0:T(8,128)(2,1)S(1)}, bf16[2,128,256]{2,1,0:T(8,128)(2,1)S(1)}, u32[]{:S(2)}, u32[]{:S(2)}) collective-permute-start(bf16[2,128,256]{2,1,0:T(8,128)(2,1)S(1)} %fusion), channel_id=1, source_target_pairs={{0,448},{8,72},{32,480},{40,104},{64,0},{72,136},{96,32},{104,168}... | collective-permute-start | bytes 393224 | tf_op jit(solution)/shard_map/ppermute | solution.py:292
  99.3 0.0 collective-permute-done.10
  99.3 0.1 convert_add_fusion
  99.4 0.0 collective-permute-done.11
  99.5 3.7 %collective-permute-start.12 = (bf16[2,128,256]{2,1,0:T(8,128)(2,1)S(1)}, bf16[2,128,256]{2,1,0:T(8,128)(2,1)S(1)}, u32[]{:S(2)}, u32[]{:S(2)}) collective-permute-start(bf16[2,128,256]{2,1,0:T(8,128)(2,1)S(1)} %pad_maximum_fusion.4), channel_id=1, source_target_pairs={{0,448},{8,72},{32,480},{40,104},{64,0},{72,136},{96,32},{104,168}... | collective-permute-start | bytes 393224 | tf_op jit(solution)/shard_map/ppermute | solution.py:292
  103.2 5.1 %collective-permute-done.15 = bf16[2,128,256]{2,1,0:T(8,128)(2,1)S(1)} collective-permute-done((bf16[2,128,256]{2,1,0:T(8,128)(2,1)S(1)}, bf16[2,128,256]{2,1,0:T(8,128)(2,1)S(1)}, u32[]{:S(2)}, u32[]{:S(2)}) %collective-permute-start.15) | collective-permute-done | bytes 131104 | tf_op jit(solution)/shard_map/ppermute | solution.py:292
  108.3 4.8 %collective-permute-start.16 = (bf16[128,256]{1,0:T(8,128)(2,1)S(1)}, bf16[128,256]{1,0:T(8,128)(2,1)S(1)}, u32[]{:S(2)}, u32[]{:S(2)}) collective-permute-start(bf16[128,256]{1,0:T(8,128)(2,1)S(1)} %fusion.15), channel_id=1, source_target_pairs={{0,384},{8,136},{32,416},{40,168},{64,448},{72,200},{96,480},{104,... | collective-permute-start | bytes 196616 | tf_op jit(solution)/shard_map/ppermute | solution.py:292
  113.1 0.0 collective-permute-done.12
  113.2 5.6 %collective-permute-start.13 = (bf16[128,256]{1,0:T(8,128)(2,1)S(1)}, bf16[128,256]{1,0:T(8,128)(2,1)S(1)}, u32[]{:S(2)}, u32[]{:S(2)}) collective-permute-start(bf16[128,256]{1,0:T(8,128)(2,1)S(1)} %fusion.14), channel_id=1, source_target_pairs={{0,384},{8,136},{32,416},{40,168},{64,448},{72,200},{96,480},{104,... | collective-permute-start | bytes 196616 | tf_op jit(solution)/shard_map/ppermute | solution.py:292
  118.9 0.0 collective-permute-done.16
  118.9 8.3 %collective-permute-start.17 = (bf16[128,256]{1,0:T(8,128)(2,1)S(1)}, bf16[128,256]{1,0:T(8,128)(2,1)S(1)}, u32[]{:S(2)}, u32[]{:S(2)}) collective-permute-start(bf16[128,256]{1,0:T(8,128)(2,1)S(1)} %fusion.4), channel_id=1, source_target_pairs={{0,8},{8,0},{1,9},{9,1},{2,10},{10,2},{3,11},{11,3},{4,12},{12,4},... | collective-permute-start | bytes 196616 | tf_op jit(solution)/shard_map/ppermute | solution.py:296
  127.2 1.9 %collective-permute-start.9 = (bf16[256,1024]{1,0:T(8,128)(2,1)S(1)}, bf16[256,1024]{1,0:T(8,128)(2,1)S(1)}, u32[]{:S(2)}, u32[]{:S(2)}) collective-permute-start(bf16[256,1024]{1,0:T(8,128)(2,1)S(1)} %get-tuple-element.26), channel_id=1, source_target_pairs={{0,8},{8,0},{1,9},{9,1},{2,10},{10,2},{3,11},{11,3},{4,12},{12,4},... | collective-permute-start | bytes 1572872 | tf_op jit(solution)/shard_map/ppermute | solution.py:296
  129.1 0.0 collective-permute-done.13
  129.1 0.0 collective-permute-done.17
  129.2 1.8 %collective-permute-done.9 = bf16[256,1024]{1,0:T(8,128)(2,1)S(1)} collective-permute-done((bf16[256,1024]{1,0:T(8,128)(2,1)S(1)}, bf16[256,1024]{1,0:T(8,128)(2,1)S(1)}, u32[]{:S(2)}, u32[]{:S(2)}) %collective-permute-start.9) | collective-permute-done | bytes 524320 | tf_op jit(solution)/shard_map/ppermute | solution.py:296
  131.0 0.2 add_convert_fusion
  131.2 14.6 %all_to_all.11 = bf16[16,16,1152]{2,1,0:T(8,128)(2,1)S(1)} all-to-all(bf16[16,16,1152]{2,1,0:T(8,128)(2,1)S(1)} %maximum_maximum_fusion.1), channel_id=1, replica_groups=mesh['z'=16,'xl'=2,'core'=2,'tp'=8] {'xl','tp'}, dimensions={0} | all-to-all | bytes 1179648 | tf_op jit(solution)/shard_map/all_to_all | solution.py:392
  145.8 0.6 slice_bitcast_fusion.4
  146.5 0.1 slice_reduce_fusion
  146.6 0.7 copy.14
  147.2 0.7 copy.13
  (23 shorter events, 0.5 us)
Async XLA Ops:
  1.6 1.2 copy-start
  1.6 1.2 copy-start.1
  20.4 17.5 %collective-permute-start.4 = (bf16[128,256]{1,0:T(8,128)(2,1)S(1)}, bf16[128,256]{1,0:T(8,128)(2,1)S(1)}, u32[]{:S(2)}, u32[]{:S(2)}) collective-permute-start(bf16[128,256]{1,0:T(8,128)(2,1)S(1)} %get-tuple-element.41), channel_id=1, source_target_pairs={{0,8},{8,0},{1,9},{9,1},{2,10},{10,2},{3,11},{11,3},{4,12},{12,4},... | collective-permute-start | bytes 196616 | tf_op jit(solution)/shard_map/ppermute | solution.py:296
  25.4 17.7 %collective-permute-start.1 = (bf16[128,256]{1,0:T(8,128)(2,1)S(1)}, bf16[128,256]{1,0:T(8,128)(2,1)S(1)}, u32[]{:S(2)}, u32[]{:S(2)}) collective-permute-start(bf16[128,256]{1,0:T(8,128)(2,1)S(1)} %get-tuple-element.41), channel_id=1, source_target_pairs={{0,128},{8,392},{32,160},{40,424},{64,192},{72,456},{96,224},{104,... | collective-permute-start | bytes 196616 | tf_op jit(solution)/shard_map/ppermute | solution.py:292
  37.9 9.6 %collective-permute-start.5 = (bf16[128,256]{1,0:T(8,128)(2,1)S(1)}, bf16[128,256]{1,0:T(8,128)(2,1)S(1)}, u32[]{:S(2)}, u32[]{:S(2)}) collective-permute-start(bf16[128,256]{1,0:T(8,128)(2,1)S(1)} %collective-permute-done.4), channel_id=1, source_target_pairs={{0,128},{8,392},{32,160},{40,424},{64,192},{72,456},{96,224},{104,... | collective-permute-start | bytes 196616 | tf_op jit(solution)/shard_map/ppermute | solution.py:292
  43.1 12.1 %collective-permute-start.2 = (bf16[2,128,256]{2,1,0:T(8,128)(2,1)S(1)}, bf16[2,128,256]{2,1,0:T(8,128)(2,1)S(1)}, u32[]{:S(2)}, u32[]{:S(2)}) collective-permute-start(bf16[2,128,256]{2,1,0:T(8,128)(2,1)S(1)} %pad_maximum_fusion.2), channel_id=1, source_target_pairs={{0,64},{8,456},{32,96},{40,488},{64,128},{72,8},{96,160},{104,40},... | collective-permute-start | bytes 393224 | tf_op jit(solution)/shard_map/ppermute | solution.py:292
  47.6 10.0 %collective-permute-start.6 = (bf16[2,128,256]{2,1,0:T(8,128)(2,1)S(1)}, bf16[2,128,256]{2,1,0:T(8,128)(2,1)S(1)}, u32[]{:S(2)}, u32[]{:S(2)}) collective-permute-start(bf16[2,128,256]{2,1,0:T(8,128)(2,1)S(1)} %pad_maximum_fusion.3), channel_id=1, source_target_pairs={{0,64},{8,456},{32,96},{40,488},{64,128},{72,8},{96,160},{104,40},... | collective-permute-start | bytes 393224 | tf_op jit(solution)/shard_map/ppermute | solution.py:292
  53.3 11.0 %collective-permute-start = (bf16[256,1024]{1,0:T(8,128)(2,1)S(1)}, bf16[256,1024]{1,0:T(8,128)(2,1)S(1)}, u32[]{:S(2)}, u32[]{:S(2)}) collective-permute-start(bf16[256,1024]{1,0:T(8,128)(2,1)S(1)} %bitcast.77), channel_id=1, source_target_pairs={{0,8},{8,0},{1,9},{9,1},{2,10},{10,2},{3,11},{11,3},{4,12},{12,4},... | collective-permute-start | bytes 1572872 | tf_op jit(solution)/shard_map/ppermute | solution.py:296
  55.3 11.6 %collective-permute-start.3 = (bf16[4,128,256]{2,1,0:T(8,128)(2,1)S(1)}, bf16[4,128,256]{2,1,0:T(8,128)(2,1)S(1)}, u32[]{:S(2)}, u32[]{:S(2)}) collective-permute-start(bf16[4,128,256]{2,1,0:T(8,128)(2,1)S(1)} %pad_maximum_fusion.mine), channel_id=1, source_target_pairs={{0,32},{8,488},{32,64},{40,8},{64,96},{72,40},{96,128},{104,72},{1... | collective-permute-start | bytes 786440 | tf_op jit(solution)/shard_map/ppermute | solution.py:292
  57.6 9.2 %collective-permute-start.7 = (bf16[4,128,256]{2,1,0:T(8,128)(2,1)S(1)}, bf16[4,128,256]{2,1,0:T(8,128)(2,1)S(1)}, u32[]{:S(2)}, u32[]{:S(2)}) collective-permute-start(bf16[4,128,256]{2,1,0:T(8,128)(2,1)S(1)} %pad_maximum_fusion.1.other), channel_id=1, source_target_pairs={{0,32},{8,488},{32,64},{40,8},{64,96},{72,40},{96,128},{104,72},{1... | collective-permute-start | bytes 786440 | tf_op jit(solution)/shard_map/ppermute | solution.py:292
  60.2 6.6 %collective-permute-start.8 = (bf16[128,256]{1,0:T(8,128)(2,1)S(1)}, bf16[128,256]{1,0:T(8,128)(2,1)S(1)}, u32[]{:S(2)}, u32[]{:S(2)}) collective-permute-start(bf16[128,256]{1,0:T(8,128)(2,1)S(1)} %slice_bitcast_fusion.3), channel_id=1, source_target_pairs={{0,64},{8,456},{32,96},{40,488},{64,128},{72,8},{96,160},{104,40},... | collective-permute-start | bytes 196616 | tf_op jit(solution)/shard_map/ppermute | solution.py:292
  77.3 20.0 %collective-permute-start.14 = (bf16[4,128,256]{2,1,0:T(8,128)(2,1)S(1)}, bf16[4,128,256]{2,1,0:T(8,128)(2,1)S(1)}, u32[]{:S(2)}, u32[]{:S(2)}) collective-permute-start(bf16[4,128,256]{2,1,0:T(8,128)(2,1)S(1)} %get-tuple-element.30), channel_id=1, source_target_pairs={{0,480},{8,40},{32,0},{40,72},{64,32},{72,104},{96,64},{104,136},{... | collective-permute-start | bytes 786440 | tf_op jit(solution)/shard_map/ppermute | solution.py:292
  85.5 13.9 %collective-permute-start.10 = (bf16[4,128,256]{2,1,0:T(8,128)(2,1)S(1)}, bf16[4,128,256]{2,1,0:T(8,128)(2,1)S(1)}, u32[]{:S(2)}, u32[]{:S(2)}) collective-permute-start(bf16[4,128,256]{2,1,0:T(8,128)(2,1)S(1)} %get-tuple-element.28), channel_id=1, source_target_pairs={{0,480},{8,40},{32,0},{40,72},{64,32},{72,104},{96,64},{104,136},{... | collective-permute-start | bytes 786440 | tf_op jit(solution)/shard_map/ppermute | solution.py:292
  88.4 11.0 %collective-permute-start.11 = (bf16[128,256]{1,0:T(8,128)(2,1)S(1)}, bf16[128,256]{1,0:T(8,128)(2,1)S(1)}, u32[]{:S(2)}, u32[]{:S(2)}) collective-permute-start(bf16[128,256]{1,0:T(8,128)(2,1)S(1)} %get-tuple-element.29), channel_id=1, source_target_pairs={{0,448},{8,72},{32,480},{40,104},{64,0},{72,136},{96,32},{104,168}... | collective-permute-start | bytes 196616 | tf_op jit(solution)/shard_map/ppermute | solution.py:292
  97.4 10.9 %collective-permute-start.15 = (bf16[2,128,256]{2,1,0:T(8,128)(2,1)S(1)}, bf16[2,128,256]{2,1,0:T(8,128)(2,1)S(1)}, u32[]{:S(2)}, u32[]{:S(2)}) collective-permute-start(bf16[2,128,256]{2,1,0:T(8,128)(2,1)S(1)} %fusion), channel_id=1, source_target_pairs={{0,448},{8,72},{32,480},{40,104},{64,0},{72,136},{96,32},{104,168}... | collective-permute-start | bytes 393224 | tf_op jit(solution)/shard_map/ppermute | solution.py:292
  99.5 13.7 %collective-permute-start.12 = (bf16[2,128,256]{2,1,0:T(8,128)(2,1)S(1)}, bf16[2,128,256]{2,1,0:T(8,128)(2,1)S(1)}, u32[]{:S(2)}, u32[]{:S(2)}) collective-permute-start(bf16[2,128,256]{2,1,0:T(8,128)(2,1)S(1)} %pad_maximum_fusion.4), channel_id=1, source_target_pairs={{0,448},{8,72},{32,480},{40,104},{64,0},{72,136},{96,32},{104,168}... | collective-permute-start | bytes 393224 | tf_op jit(solution)/shard_map/ppermute | solution.py:292
  108.3 10.5 %collective-permute-start.16 = (bf16[128,256]{1,0:T(8,128)(2,1)S(1)}, bf16[128,256]{1,0:T(8,128)(2,1)S(1)}, u32[]{:S(2)}, u32[]{:S(2)}) collective-permute-start(bf16[128,256]{1,0:T(8,128)(2,1)S(1)} %fusion.15), channel_id=1, source_target_pairs={{0,384},{8,136},{32,416},{40,168},{64,448},{72,200},{96,480},{104,... | collective-permute-start | bytes 196616 | tf_op jit(solution)/shard_map/ppermute | solution.py:292
  113.2 15.9 %collective-permute-start.13 = (bf16[128,256]{1,0:T(8,128)(2,1)S(1)}, bf16[128,256]{1,0:T(8,128)(2,1)S(1)}, u32[]{:S(2)}, u32[]{:S(2)}) collective-permute-start(bf16[128,256]{1,0:T(8,128)(2,1)S(1)} %fusion.14), channel_id=1, source_target_pairs={{0,384},{8,136},{32,416},{40,168},{64,448},{72,200},{96,480},{104,... | collective-permute-start | bytes 196616 | tf_op jit(solution)/shard_map/ppermute | solution.py:292
  118.9 10.2 %collective-permute-start.17 = (bf16[128,256]{1,0:T(8,128)(2,1)S(1)}, bf16[128,256]{1,0:T(8,128)(2,1)S(1)}, u32[]{:S(2)}, u32[]{:S(2)}) collective-permute-start(bf16[128,256]{1,0:T(8,128)(2,1)S(1)} %fusion.4), channel_id=1, source_target_pairs={{0,8},{8,0},{1,9},{9,1},{2,10},{10,2},{3,11},{11,3},{4,12},{12,4},... | collective-permute-start | bytes 196616 | tf_op jit(solution)/shard_map/ppermute | solution.py:296
  127.2 3.8 %collective-permute-start.9 = (bf16[256,1024]{1,0:T(8,128)(2,1)S(1)}, bf16[256,1024]{1,0:T(8,128)(2,1)S(1)}, u32[]{:S(2)}, u32[]{:S(2)}) collective-permute-start(bf16[256,1024]{1,0:T(8,128)(2,1)S(1)} %get-tuple-element.26), channel_id=1, source_target_pairs={{0,8},{8,0},{1,9},{9,1},{2,10},{10,2},{3,11},{11,3},{4,12},{12,4},... | collective-permute-start | bytes 1572872 | tf_op jit(solution)/shard_map/ppermute | solution.py:296
